TPU v7x, 32 devices: a whole 2x2x4 slice. The times are simulated.
32 devices in a mesh: slab: 16 (over z, y, core), chan: 2 (over x).
Axes of the slice: x: 2, y: 2, z: 4, core: 2. Of those that a mesh axis runs over, the one named last changes fastest.
Arguments:
- activations: float32 [64, 64, 32, 128], P('chan', 'slab'), may hold values from -6 to 6
- kernel: float32 [64, 27, 64], P(None, None, 'chan'), may hold values from -0.15625 to 0.15625
- cotangent: float32 [64, 64, 32, 128], P('chan', 'slab'), may hold values from -6 to 6
Outputs:
- features: float32 [64, 64, 32, 128], P('chan', 'slab')
- input_grad: float32 [64, 64, 32, 128], P('chan', 'slab')
- weight_grad: float32 [64, 27, 64], P(None, None, 'chan')
All inputs are finite; a program needn't handle non-finite values.
Results may differ from a plain program's by a relative error of at most 0.0003.
Values sent between devices are 32-bit elements; how exact they have to be, the bound alone decides.
No kernel may reach another device: no remote copies, remote signals or barrier semaphores. Data moves between devices by JAX's collectives and lax.ppermute only.
A program may use at most 192 MiB of HBM per device.

v0:
```python
from functools import reduce
import math

import jax
import jax.numpy as jnp
from jax import lax
from jax.sharding import PartitionSpec as P

HIGHEST_PREC = lax.Precision.HIGHEST


def padded_2(cells, sides, width):
    for axis, dim in sides:
        count = lax.axis_size(axis)
        ends = count - 1
        head = lax.slice_in_dim(cells, 0, width, axis=dim)
        tail = lax.slice_in_dim(cells, cells.shape[dim] - width, cells.shape[dim], axis=dim)
        cells = jnp.concatenate(
            [
                lax.ppermute(tail, axis, [(i, (i + 1) % count) for i in range(ends)]),
                cells,
                lax.ppermute(head, axis, [((i + 1) % count, i) for i in range(ends)]),
            ],
            axis=dim,
        )
    return cells


def tap_stack(padded, first_plane, plane_count):
    height = padded.shape[2]
    columns = padded.shape[3]
    slab_part = lax.dynamic_slice_in_dim(padded, first_plane, plane_count + 2, 1)
    framed = jnp.pad(slab_part, ((0, 0), (0, 0), (1, 1), (1, 1)))
    shifted = [
        framed[
            :,
            depth_off : depth_off + plane_count,
            row_off : row_off + height,
            col_off : col_off + columns,
        ]
        for depth_off in range(3)
        for row_off in range(3)
        for col_off in range(3)
    ]
    return jnp.stack(shifted).reshape(27 * padded.shape[0], plane_count * height * columns)


def forward_planes(matrix, padded):
    planes = padded.shape[1] - 2
    blocks = planes // 2
    height = padded.shape[2]
    columns = padded.shape[3]

    def one_block(block_index):
        return jnp.dot(
            matrix,
            tap_stack(padded, 2 * block_index, 2),
            precision=HIGHEST_PREC,
            preferred_element_type=jnp.float32,
        )

    stacked = lax.map(one_block, jnp.arange(blocks))
    rows_out = matrix.shape[0]
    shaped = stacked.reshape(blocks, rows_out, 2, height, columns)
    return jnp.moveaxis(shaped, 0, 1).reshape(rows_out, planes, height, columns)


def per_device(activations, kernel, cotangent):
    channels = kernel.shape[0]
    cin = kernel.shape[2]
    planes = activations.shape[1]
    height = activations.shape[2]
    columns = activations.shape[3]
    padded_in = padded_2(activations, (("slab", 1),), 1)
    kernel_mat = kernel.reshape(channels, 27 * cin)
    features = lax.psum_scatter(
        forward_planes(kernel_mat, padded_in), "chan", scatter_dimension=0, tiled=True
    )
    all_cot = lax.all_gather(cotangent, "chan", axis=0, tiled=True)
    padded_cot = padded_2(all_cot, (("slab", 1),), 1)
    transposed = kernel.reshape(channels, 27 * cin).T

    def back_block(block_index):
        first_plane = 2 * block_index
        cot_slab = lax.dynamic_slice_in_dim(padded_cot, first_plane, 4, 1)
        inner = cot_slab[:, 1:3].reshape(channels, 2 * height * columns)
        patches = tap_stack(padded_in, first_plane, 2)
        grad_part = lax.dot_general(
            inner,
            patches,
            (((1,), (1,)), ((), ())),
            precision=HIGHEST_PREC,
            preferred_element_type=jnp.float32,
        )
        pieces = []
        for depth_off in range(3):
            tap_rows = transposed[9 * depth_off * cin : 9 * (depth_off + 1) * cin]
            source = cot_slab[:, 2 - depth_off : 4 - depth_off].reshape(
                channels, 2 * height * columns
            )
            spread = jnp.dot(
                tap_rows, source, precision=HIGHEST_PREC, preferred_element_type=jnp.float32
            )
            spread = spread.reshape(9, cin, 2, height, columns)
            spread = jnp.pad(spread, ((0, 0), (0, 0), (0, 0), (1, 1), (1, 1)))
            for row_off in range(3):
                for col_off in range(3):
                    pieces.append(
                        spread[
                            3 * row_off + col_off,
                            :,
                            :,
                            2 - row_off : 2 - row_off + height,
                            2 - col_off : 2 - col_off + columns,
                        ]
                    )
        return (grad_part, reduce(jnp.add, pieces))

    grad_parts, grad_blocks = lax.map(back_block, jnp.arange(planes // 2))
    local_grad = jnp.sum(grad_parts, axis=0).reshape(channels, 27, cin)
    input_grad = jnp.moveaxis(grad_blocks, 0, 1).reshape(cin, planes, height, columns)
    summed = lax.psum(local_grad, "slab")
    cells_all = planes * lax.axis_size("slab") * height * columns
    weight_grad = summed / math.sqrt(cells_all)
    return (features, input_grad, weight_grad)


def solution(mesh):
    return jax.shard_map(
        per_device,
        mesh=mesh,
        in_specs=(
            P("chan", "slab", None, None),
            P(None, None, "chan"),
            P("chan", "slab", None, None),
        ),
        out_specs=(
            P("chan", "slab", None, None),
            P("chan", "slab", None, None),
            P(None, None, "chan"),
        ),
        check_vma=False,
    )
```

profile of v0, /device:TPU:0, one launch (start us, length us, event | category | flops | bytes accessed | tf_op | source)
XLA Modules:
  0.0 722.2 jit_solution(16145300914134653498)
XLA Ops:
  8.0 61.1 %all-gather.2.cloned.1.call-done = f32[64,4,32,128]{3,2,1,0:T(8,128)} async-done(((f32[32,4,32,128]{3,2,1,0:T(8,128)}), f32[64,4,32,128]{3,2,1,0:T(8,128)}) %all-gather.2.cloned.1.call-update) | async-done | bytes 4194320 | tf_op jit(solution)/shard_map/all_gather | solution.py:79
  69.0 3.1 fusion.151
  72.1 2.7 collective-permute-start.2
  76.1 2.3 fusion.152
  78.4 4.1 collective-permute-start
  83.9 1.9 copy.13
  85.8 1.9 constant_dynamic-update-slice_fusion.2
  87.7 1.6 constant_dynamic-update-slice_fusion.1
  90.2 6.3 pad_maximum_fusion
  96.5 342.6 %while.27 = (s32[]{:T(128)}, f32[2,64,864]{2,1,0:T(8,128)}, f32[2,32,2,32,128]{4,3,2,1,0:T(8,128)}, s32[2]{0:T(128)S(1)}, f32[64,6,32,128]{3,2,1,0:T(8,128)}, /*...) while((s32[]{:T(128)}, f32[2,64,864]{2,1,0:T(8,128)}, ...), condition=%wide.region_4.5_spmd, body=%wide.region_3.4_spmd.sunk | while | flops 10878451712 | bytes 326124288 | solution.py:119
  98.0 1.8 constant_dynamic-slice_fusion.9
  105.1 2.3 fusion.268
  111.2 1.4 fusion.272
  117.7 2.3 fusion.277
  120.0 1.4 fusion.278
  130.3 2.3 fusion.286
  137.7 31.6 %reshape.95 = f32[864,8192]{1,0:T(8,128)} reshape(f32[27,32,2,32,128]{4,3,2,1,0:T(8,128)} %fusion.290) | data formatting | bytes 56623104 | tf_op jit(solution)/shard_map/while/body/eval_jaxpr/reshape | solution.py:45
  169.4 5.2 constant_dynamic-slice_fusion.10
  174.5 29.7 %fusion.291 = f32[2,64,864]{2,1,0:T(8,128)S(1)} fusion(f32[2,64,864]{2,1,0:T(8,128)S(1)} %copy-done.4, s32[]{:T(128)} %get-tuple-element.333, f32[864,8192]{1,0:T(8,128)} %reshape.95, f32[8,8,64,128]{3,2,1,0:T(8,128)S(1)} %bitcast.468), kind=kOutput, calls=%fused_computation.142.clone.1 | convolution fusion | flops 5435817984 | bytes 30638084 | tf_op jit(solution)/shard_map/while/body/eval_jaxpr/dot_general | solution.py:88
  205.0 8.5 %fusion.293 = f32[8192,288]{0,1:T(8,128)S(1)} fusion(f32[8,8,64,128]{3,2,1,0:T(8,128)S(1)} %bitcast.469, f32[864,64]{1,0:T(8,128)S(1)} %get-tuple-element.352), kind=kOutput, calls=%fused_computation.135.clone.1 | convolution fusion | flops 1811939328 | bytes 11681792 | tf_op jit(solution)/shard_map/while/body/eval_jaxpr/dot_general | solution.py:101
  213.5 5.5 copy.63
  220.3 8.8 %fusion.292 = f32[8192,288]{0,1:T(8,128)S(1)} fusion(f32[8,8,64,128]{3,2,1,0:T(8,128)S(1)} %bitcast.471, f32[864,64]{1,0:T(8,128)S(1)} %get-tuple-element.352), kind=kOutput, calls=%fused_computation.129.clone.1 | convolution fusion | flops 1811939328 | bytes 11681792 | tf_op jit(solution)/shard_map/while/body/eval_jaxpr/dot_general | solution.py:101
  229.1 5.6 copy.61
  234.7 10.5 %fusion.294 = f32[8192,288]{0,1:T(8,128)S(1)} fusion(f32[8,8,64,128]{3,2,1,0:T(8,128)} %bitcast.470, f32[864,64]{1,0:T(8,128)S(1)} %get-tuple-element.352), kind=kOutput, calls=%fused_computation.132.clone.1 | convolution fusion | flops 1811939328 | bytes 11681792 | tf_op jit(solution)/shard_map/while/body/eval_jaxpr/dot_general | solution.py:101
  245.1 5.6 copy.65
  251.3 12.0 %fusion.295 = f32[2,32,2,32,128]{4,3,2,1,0:T(8,128)} fusion(f32[2,32,2,32,128]{4,3,2,1,0:T(8,128)} %get-tuple-element.335, s32[]{:T(128)} %get-tuple-element.333, f32[9,32,2,32,128]{4,3,2,1,0:T(8,128)} %bitcast.466, f32[1,32,2,32,128]{4,3,2,1,0:T(8,128)S(1)} %bitcast.473, f32[9,32,2,32,128]{4,3,2,1,0:T(8,128)} %bitcast.465, ...), kind=kLoop, calls=%fused_computation.166.clone.1 | loop fusion | flops 6815744 | bytes 32506368 | tf_op jit(solution)/shard_map/while/body/jit(dynamic_update_index_in_dim)/dynamic_update_slice | solution.py:119
  264.7 1.8 constant_dynamic-slice_fusion.9
  271.8 2.3 fusion.268
  277.8 1.4 fusion.272
  284.4 2.3 fusion.277
  286.7 1.4 fusion.278
  297.0 2.3 fusion.286
  304.4 31.3 %reshape.95 = f32[864,8192]{1,0:T(8,128)} reshape(f32[27,32,2,32,128]{4,3,2,1,0:T(8,128)} %fusion.290) | data formatting | bytes 56623104 | tf_op jit(solution)/shard_map/while/body/eval_jaxpr/reshape | solution.py:45
  335.7 5.2 constant_dynamic-slice_fusion.10
  340.9 29.9 %fusion.291 = f32[2,64,864]{2,1,0:T(8,128)S(1)} fusion(f32[2,64,864]{2,1,0:T(8,128)S(1)} %copy-done.4, s32[]{:T(128)} %get-tuple-element.333, f32[864,8192]{1,0:T(8,128)} %reshape.95, f32[8,8,64,128]{3,2,1,0:T(8,128)S(1)} %bitcast.468), kind=kOutput, calls=%fused_computation.142.clone.1 | convolution fusion | flops 5435817984 | bytes 30638084 | tf_op jit(solution)/shard_map/while/body/eval_jaxpr/dot_general | solution.py:88
  371.6 8.6 %fusion.293 = f32[8192,288]{0,1:T(8,128)S(1)} fusion(f32[8,8,64,128]{3,2,1,0:T(8,128)S(1)} %bitcast.469, f32[864,64]{1,0:T(8,128)S(1)} %get-tuple-element.352), kind=kOutput, calls=%fused_computation.135.clone.1 | convolution fusion | flops 1811939328 | bytes 11681792 | tf_op jit(solution)/shard_map/while/body/eval_jaxpr/dot_general | solution.py:101
  380.1 5.5 copy.63
  386.9 8.7 %fusion.292 = f32[8192,288]{0,1:T(8,128)S(1)} fusion(f32[8,8,64,128]{3,2,1,0:T(8,128)S(1)} %bitcast.471, f32[864,64]{1,0:T(8,128)S(1)} %get-tuple-element.352), kind=kOutput, calls=%fused_computation.129.clone.1 | convolution fusion | flops 1811939328 | bytes 11681792 | tf_op jit(solution)/shard_map/while/body/eval_jaxpr/dot_general | solution.py:101
  395.7 5.6 copy.61
  401.2 10.3 %fusion.294 = f32[8192,288]{0,1:T(8,128)S(1)} fusion(f32[8,8,64,128]{3,2,1,0:T(8,128)} %bitcast.470, f32[864,64]{1,0:T(8,128)S(1)} %get-tuple-element.352), kind=kOutput, calls=%fused_computation.132.clone.1 | convolution fusion | flops 1811939328 | bytes 11681792 | tf_op jit(solution)/shard_map/while/body/eval_jaxpr/dot_general | solution.py:101
  411.5 5.6 copy.65
  417.6 12.0 %fusion.295 = f32[2,32,2,32,128]{4,3,2,1,0:T(8,128)} fusion(f32[2,32,2,32,128]{4,3,2,1,0:T(8,128)} %get-tuple-element.335, s32[]{:T(128)} %get-tuple-element.333, f32[9,32,2,32,128]{4,3,2,1,0:T(8,128)} %bitcast.466, f32[1,32,2,32,128]{4,3,2,1,0:T(8,128)S(1)} %bitcast.473, f32[9,32,2,32,128]{4,3,2,1,0:T(8,128)} %bitcast.465, ...), kind=kLoop, calls=%fused_computation.166.clone.1 | loop fusion | flops 6815744 | bytes 32506368 | tf_op jit(solution)/shard_map/while/body/jit(dynamic_update_index_in_dim)/dynamic_update_slice | solution.py:119
  441.3 190.0 %while.26 = (s32[]{:T(128)}, f32[2,64,8192]{2,1,0:T(8,128)}, s32[2]{0:T(128)S(1)}, f32[32,6,32,128]{3,2,1,0:T(8,128)}, f32[64,864]{1,0:T(8,128)}, /*index=5*/s32...) while((s32[]{:T(128)}, f32[2,64,8192]{2,1,0:T(8,128)}, s32[2]{0:T(128)S(1)}, ...), condition=%wide.region_1.2_spmd, body=%wide.region_0.1_spmd.sunk | while | flops 5435817984 | bytes 174121712 | solution.py:62
  442.5 1.8 constant_dynamic-slice_fusion.8
  449.5 2.3 fusion.232
  455.6 1.4 fusion.236
  462.2 2.3 fusion.241
  464.5 1.4 fusion.242
  474.8 2.3 fusion.250
  482.2 31.2 %reshape.94 = f32[864,8192]{1,0:T(8,128)} reshape(f32[27,32,2,32,128]{4,3,2,1,0:T(8,128)} %fusion.254) | data formatting | bytes 56623104 | tf_op jit(solution)/shard_map/while/body/eval_jaxpr/reshape | solution.py:45
  513.4 22.9 %fusion.255 = f32[2,64,8192]{2,1,0:T(8,128)} fusion(f32[2,64,8192]{2,1,0:T(8,128)} %get-tuple-element.299, s32[]{:T(128)} %get-tuple-element.298, f32[864,8192]{1,0:T(8,128)} %reshape.94, f32[64,864]{1,0:T(8,128)S(1)} %copy-done.1), kind=kOutput, calls=%fused_computation.25.clone.1 | convolution fusion | flops 5435817984 | bytes 30630400 | tf_op jit(solution)/shard_map/while/body/eval_jaxpr/dot_general | solution.py:55
  537.5 1.8 constant_dynamic-slice_fusion.8
  544.5 2.3 fusion.232
  550.6 1.4 fusion.236
  557.2 2.3 fusion.241
  559.5 1.4 fusion.242
  569.8 2.3 fusion.250
  577.2 31.2 %reshape.94 = f32[864,8192]{1,0:T(8,128)} reshape(f32[27,32,2,32,128]{4,3,2,1,0:T(8,128)} %fusion.254) | data formatting | bytes 56623104 | tf_op jit(solution)/shard_map/while/body/eval_jaxpr/reshape | solution.py:45
  608.4 22.8 %fusion.255 = f32[2,64,8192]{2,1,0:T(8,128)} fusion(f32[2,64,8192]{2,1,0:T(8,128)} %get-tuple-element.299, s32[]{:T(128)} %get-tuple-element.298, f32[864,8192]{1,0:T(8,128)} %reshape.94, f32[64,864]{1,0:T(8,128)S(1)} %copy-done.1), kind=kOutput, calls=%fused_computation.25.clone.1 | convolution fusion | flops 5435817984 | bytes 30630400 | tf_op jit(solution)/shard_map/while/body/eval_jaxpr/dot_general | solution.py:55
  631.2 3.1 copy.26
  634.3 2.4 copy.14
  636.8 1.5 copy.15
  638.3 1.8 broadcast_multiply_fusion
  640.1 75.4 %reduce-scatter.2.cloned.1.call-done = f32[32,4,32,128]{3,2,1,0:T(8,128)} async-done(((f32[64,4,32,128]{3,2,1,0:T(8,128)}), f32[32,4,32,128]{3,2,1,0:T(8,128)}) %reduce-scatter.2.cloned.1.call-update) | async-done | bytes 2097168 | tf_op jit(solution)/shard_map/reduce_scatter | solution.py:76
  (143 shorter events, 126.3 us)
Async XLA Ops:
  7.2 80.6 %copy-start.2 = (f32[32,4,32,128]{3,2,1,0:T(8,128)S(1)}, f32[32,4,32,128]{3,2,1,0:T(8,128)}, u32[]{:S(2)}) copy-start(f32[32,4,32,128]{3,2,1,0:T(8,128)} %param.7) | copy-start | bytes 6291460
  7.2 61.9 %all-gather.2.cloned.1.call-start = ((), (), s32[]{:S(2)}) async-start(), calls=%async_computation.2 | async-start | bytes 6291456 | tf_op jit(solution)/shard_map/all_gather | solution.py:79
  7.9 630.4 %all-reduce.7.cloned.1.call-start = ((), (), s32[]{:S(2)}) async-start(), calls=%async_computation.3 | async-start | bytes 884736 | tf_op jit(solution)/shard_map/psum | solution.py:122
  72.1 18.1 %collective-permute-start.2 = (f32[64,1,32,128]{3,2,1,0:T(8,128)}, f32[64,1,32,128]{3,2,1,0:T(8,128)}, u32[]{:S(2)}, u32[]{:S(2)}) collective-permute-start(f32[64,1,32,128]{3,2,1,0:T(8,128)} %get-tuple-element.203), channel_id=1, source_target_pairs={{0,2},{2,4},{4,6},{6,8},{8,10},{10,12},{12,14},{14,16},{16,18},{18... | collective-permute-start | bytes 3145736 | tf_op jit(solution)/shard_map/ppermute | solution.py:20
  74.8 15.3 %collective-permute-start.3 = (f32[64,1,32,128]{3,2,1,0:T(8,128)}, f32[64,1,32,128]{3,2,1,0:T(8,128)}, u32[]{:S(2)}, u32[]{:S(2)}) collective-permute-start(f32[64,1,32,128]{3,2,1,0:T(8,128)} %get-tuple-element.204), channel_id=1, source_target_pairs={{2,0},{4,2},{6,4},{8,6},{10,8},{12,10},{14,12},{16,14},{18,16},{20... | collective-permute-start | bytes 3145736 | tf_op jit(solution)/shard_map/ppermute | solution.py:22
  78.4 7.3 %collective-permute-start = (f32[32,1,32,128]{3,2,1,0:T(8,128)}, f32[32,1,32,128]{3,2,1,0:T(8,128)}, u32[]{:S(2)}, u32[]{:S(2)}) collective-permute-start(f32[32,1,32,128]{3,2,1,0:T(8,128)} %get-tuple-element.206), channel_id=1, source_target_pairs={{0,2},{2,4},{4,6},{6,8},{8,10},{10,12},{12,14},{14,16},{16,18},{18... | collective-permute-start | bytes 1572872 | tf_op jit(solution)/shard_map/ppermute | solution.py:20
  82.6 6.7 collective-permute-start.1
  85.8 10.8 %copy-start = (f32[64,27,32]{0,2,1:T(8,128)S(1)}, f32[64,27,32]{0,2,1:T(8,128)}, u32[]{:S(2)}) copy-start(f32[64,27,32]{0,2,1:T(8,128)} %param.8) | copy-start | bytes 663556
  169.4 5.2 copy-start.4
  204.2 0.8 copy-start.5
  335.7 5.2 copy-start.4
  370.8 0.8 copy-start.5
  441.2 274.2 %reduce-scatter.2.cloned.1.call-start = ((), (), s32[]{:S(2)}) async-start(), calls=%async_computation.1 | async-start | bytes 6291456 | tf_op jit(solution)/shard_map/reduce_scatter | solution.py:76
  482.2 31.2 %copy-start.1 = (f32[64,864]{1,0:T(8,128)S(1)}, f32[64,864]{1,0:T(8,128)}, u32[]{:S(2)}) copy-start(f32[64,864]{1,0:T(8,128)} %get-tuple-element.313) | copy-start | bytes 663556 | tf_op jit(solution)/shard_map/while
  577.2 31.2 %copy-start.1 = (f32[64,864]{1,0:T(8,128)S(1)}, f32[64,864]{1,0:T(8,128)}, u32[]{:S(2)}) copy-start(f32[64,864]{1,0:T(8,128)} %get-tuple-element.313) | copy-start | bytes 663556 | tf_op jit(solution)/shard_map/while
  631.2 5.5 copy-start.3
Sparse Core Ops, SparseCore 0:
  9.6 59.4 all-gather.1
  441.3 113.9 all-reduce.6
  636.9 78.5 reduce-scatter.1
where the time goes:
time: 728 us; the launch traced here: 722 us
  local copies, waits for them, and re-layouts  355 us (49%)
  matrix products  161 us (22%)
  waiting for transfers between devices  137 us (19%)
  other arithmetic  33.3 us (5%)
  between operations  14 us (2%)
  loops' own time  12.8 us (2%)
  starting transfers between devices  9.55 us (1%)
    while x134, local copies, waits for them, and re-layouts  185 us
    reshape x4, local copies, waits for them, and re-layouts, tap_stack(): jnp.stack(shifted)  125 us
    reduce_scatter x1, waiting for transfers between devices, per_device(): lax.psum_scatter(forward_planes(kernel_mat, padded_in), 'chan', scatter_d...  75.4 us
    all_gather x1, waiting for transfers between devices, per_device(): all_cot = lax.all_gather(cotangent, 'chan', axis=0, tiled=True)  61.1 us
    dot_general x2, matrix products, back_block(): lax.dot_general(inner, patches, (((1,), (1,)), ((), ())), precision=HIGHE...  59.6 us
    dot_general x6, matrix products, back_block(): jnp.dot(tap_rows, source, precision=HIGHEST_PREC, preferred_element_type=...  55.3 us
    dot_general x2, matrix products, one_block(): jnp.dot(matrix, tap_stack(padded, 2 * block_index, 2), precision=HIGHEST_...  45.7 us
    dynamic_update_slice x2, other arithmetic, per_device(): grad_parts, grad_blocks = lax.map(back_block, jnp.arange(planes // 2))  24.1 us
  transfers between devices with their start and end apart: 7, of which 2 were waited for; matrix products, arithmetic and copies ran while one was open for 29% of the time, Pallas kernels for 0%

commit v1 on v0

v1 whole, which is shorter than its diff:
```python
import functools
import math

import jax
import jax.numpy as jnp
from jax import lax
from jax.experimental import pallas as pl
from jax.experimental.pallas import tpu as pltpu
from jax.sharding import PartitionSpec as P

F32 = jnp.float32
BF16 = jnp.bfloat16


def split(x):
    hi = x.astype(BF16)
    return hi, (x - hi.astype(F32)).astype(BF16)


def fill_rows(dst_hi, dst_lo, plane, src, first, stride, chans, padded, height):
    blank = jnp.zeros((padded, dst_hi.shape[-1]), BF16)
    for dst in (dst_hi, dst_lo):
        dst[plane, pl.ds(0, padded), :] = blank
        dst[plane, pl.ds((height + 1) * padded, padded), :] = blank

    def one_row(row, carry):
        hi, lo = split(src[pl.ds(first + row, chans, stride=stride), :])
        start = pl.multiple_of((row + 1) * padded, padded)
        for dst, part in ((dst_hi, hi), (dst_lo, lo)):
            if padded != chans:
                fill = jnp.zeros((padded - chans, part.shape[1]), BF16)
                part = jnp.concatenate([part, fill], axis=0)
            dst[plane, pl.ds(start, padded), :] = part
        return carry

    lax.fori_loop(0, height, one_row, 0, unroll=4)


def fill_field(dst_hi, dst_lo, field, below, above, chans, padded, planes, height):
    fill_rows(dst_hi, dst_lo, 0, below, 0, height, chans, padded, height)
    fill_rows(dst_hi, dst_lo, planes + 1, above, 0, height, chans, padded, height)

    def one_plane(d, carry):
        fill_rows(
            dst_hi, dst_lo, d + 1, field, d * height, planes * height, chans, padded, height
        )
        return carry

    lax.fori_loop(0, planes, one_plane, 0)


def conv_kernel(dims, groups, has_acc, *refs):
    chans, padded, planes, height, outs = dims
    field, below, above, weight = refs[:4]
    refs = refs[4:]
    acc = None
    if has_acc:
        acc, refs = refs[0], refs[1:]
    results = refs[:groups]
    xh, xl = refs[groups:]
    d = pl.program_id(0)
    width = field.shape[-1]

    @pl.when(d == 0)
    def _():
        fill_field(xh, xl, field, below, above, chans, padded, planes, height)

    lane = lax.broadcasted_iota(jnp.int32, (groups * outs, width), 1)
    first = lane == 0
    last = lane == width - 1
    span = 3 * padded
    rows_out = groups * outs

    def one_pair(pair, carry):
        h = 2 * pair
        parts = []
        for src in (xh, xl):
            for i in range(3):
                block = src[d + i, pl.ds(pl.multiple_of(h * padded, padded), 4 * padded), :]
                parts.append(
                    jnp.concatenate([block[:span], block[padded : padded + span]], axis=1)
                )
        parts = parts + parts[:3]
        extra = weight.shape[1] - 9 * span
        if extra:
            parts.append(jnp.zeros((extra, 2 * width), BF16))
        y = jnp.dot(
            weight[...], jnp.concatenate(parts, axis=0), preferred_element_type=F32
        )
        for r in range(2):
            z = y[:, r * width : (r + 1) * width]
            left = pltpu.roll(z[:rows_out], 1, 1)
            right = pltpu.roll(z[2 * rows_out :], width - 1, 1)
            total = (
                z[rows_out : 2 * rows_out]
                + jnp.where(first, 0.0, left)
                + jnp.where(last, 0.0, right)
            )
            for g in range(groups):
                where = pl.ds(h + r, outs, stride=height)
                piece = total[g * outs : (g + 1) * outs]
                if acc is not None:
                    piece = piece + acc.reshape(outs * height, width)[where, :]
                results[g].reshape(outs * height, width)[where, :] = piece
        return carry

    lax.fori_loop(0, height // 2, one_pair, 0)


def conv(field, below, above, weight, outs, groups, acc=None):
    chans, planes, height, width = field.shape
    padded = -(-chans // 16) * 16
    flat = field.reshape(chans * planes * height, width)
    args = [flat, below.reshape(chans * height, width), above.reshape(chans * height, width), weight]
    whole = pl.BlockSpec(memory_space=pltpu.VMEM)
    plane_spec = pl.BlockSpec((outs, 1, height, width), lambda d: (0, d, 0, 0))
    in_specs = [whole] * 4
    if acc is not None:
        args.append(acc)
        in_specs.append(plane_spec)
    cells = planes * height * width
    shape = jax.ShapeDtypeStruct((outs, planes, height, width), F32)
    return pl.pallas_call(
        functools.partial(
            conv_kernel, (chans, padded, planes, height, outs), groups, acc is not None
        ),
        grid=(planes,),
        in_specs=in_specs,
        out_specs=[plane_spec] * groups,
        out_shape=[shape] * groups,
        scratch_shapes=[
            pltpu.VMEM((planes + 2, (height + 2) * padded, width), BF16) for _ in range(2)
        ],
        compiler_params=pltpu.CompilerParams(
            dimension_semantics=("arbitrary",), vmem_limit_bytes=32 << 20
        ),
        cost_estimate=pl.CostEstimate(
            flops=6 * 27 * chans * outs * groups * cells * 2,
            bytes_accessed=4 * (chans + outs * groups) * cells,
            transcendentals=0,
        ),
        name="conv",
    )(*args)


def grad_kernel(dims, field, below, above, cot, out, xh, xl, total):
    chans, padded, planes, height, rows = dims
    outs = cot.shape[0] // (planes * height)
    width = field.shape[-1]
    step = pl.program_id(0)
    span = 3 * padded

    @pl.when(step == 0)
    def _():
        fill_field(xh, xl, field, below, above, chans, padded, planes, height)
        total[...] = jnp.zeros_like(total)

    lane = lax.broadcasted_iota(jnp.int32, (outs, width), 1)
    first = lane == 0
    last = lane == width - 1
    group = padded_outs(outs)

    def one_block(block, carry):
        h = block * rows
        lhs = []
        for src in (xh, xl):
            for i in range(3):
                window = src[
                    step + i, pl.ds(pl.multiple_of(h * padded, padded), (rows + 2) * padded), :
                ]
                lhs.append(
                    jnp.concatenate(
                        [window[r * padded : r * padded + span] for r in range(rows)], axis=1
                    )
                )
        columns = []
        for r in range(rows):
            c = cot[pl.ds(step * height + h + r, outs, stride=planes * height), :]
            moved = [
                jnp.where(last, 0.0, pltpu.roll(c, width - 1, 1)),
                c,
                jnp.where(first, 0.0, pltpu.roll(c, 1, 1)),
            ]
            pieces = [split(m) for m in moved]
            high = [p[0] for p in pieces]
            low = [p[1] for p in pieces]
            gap = group - 3 * outs
            fill = [jnp.zeros((gap, width), BF16)] if gap else []
            columns.append(jnp.concatenate(high + fill + low + fill, axis=0))
        total[...] += lax.dot_general(
            jnp.concatenate(lhs, axis=0),
            jnp.concatenate(columns, axis=1),
            (((1,), (1,)), ((), ())),
            preferred_element_type=F32,
        )
        return carry

    lax.fori_loop(0, height // rows, one_block, 0)

    @pl.when(step == planes - 1)
    def _():
        half = 3 * span
        out[...] = (
            total[:half, :group] + total[:half, group:] + total[half:, :group]
        )


def padded_outs(outs):
    return -(-3 * outs // 128) * 128


def kernel_grad(field, below, above, cot):
    chans, planes, height, width = field.shape
    outs = cot.shape[0]
    padded = -(-chans // 16) * 16
    rows = 4
    group = padded_outs(outs)
    whole = pl.BlockSpec(memory_space=pltpu.VMEM)
    cells = planes * height * width
    return pl.pallas_call(
        functools.partial(grad_kernel, (chans, padded, planes, height, rows)),
        grid=(planes,),
        in_specs=[whole] * 4,
        out_specs=pl.BlockSpec((9 * padded, group), lambda d: (0, 0)),
        out_shape=jax.ShapeDtypeStruct((9 * padded, group), F32),
        scratch_shapes=[
            pltpu.VMEM((planes + 2, (height + 2) * padded, width), BF16) for _ in range(2)
        ]
        + [pltpu.VMEM((18 * padded, 2 * group), F32)],
        compiler_params=pltpu.CompilerParams(
            dimension_semantics=("arbitrary",), vmem_limit_bytes=32 << 20
        ),
        cost_estimate=pl.CostEstimate(
            flops=6 * 27 * chans * outs * cells * 2,
            bytes_accessed=4 * (chans + outs) * cells,
            transcendentals=0,
        ),
        name="kernel_grad",
    )(
        field.reshape(chans * planes * height, width),
        below.reshape(chans * height, width),
        above.reshape(chans * height, width),
        cot.reshape(outs * planes * height, width),
    )


def three_pass(matrix, padded):
    rows, taps, chans = matrix.shape
    matrix = jnp.pad(matrix, ((0, 0), (0, 0), (0, padded - chans)))
    matrix = matrix.reshape(rows, taps * padded)
    high = lax.reduce_precision(matrix, 8, 7)
    low = matrix - high
    wide = jnp.concatenate([high, high, low], axis=1)
    extra = -wide.shape[1] % 128
    return jnp.pad(wide, ((0, 0), (0, extra))).astype(BF16)


def slab_halo(field):
    count = lax.axis_size("slab")
    planes = field.shape[1]
    up = [(i, i + 1) for i in range(count - 1)]
    down = [(i + 1, i) for i in range(count - 1)]
    below = lax.ppermute(field[:, planes - 1 :], "slab", up)
    above = lax.ppermute(field[:, :1], "slab", down)
    return below, above


def slab_sum(value):
    count = lax.axis_size("slab")
    if count & (count - 1):
        return lax.psum(value, "slab")
    bit = 1
    while bit < count:
        value = value + lax.ppermute(value, "slab", [(i, i ^ bit) for i in range(count)])
        bit *= 2
    return value


def per_device(activations, kernel, cotangent):
    groups = lax.axis_size("chan")
    me = lax.axis_index("chan")
    channels, taps, cin = kernel.shape
    mine = channels // groups
    planes, height, width = activations.shape[1:]
    pad_in = -(-cin // 16) * 16
    pad_out = -(-mine // 16) * 16

    cots = [cotangent]
    for s in range(1, groups):
        cots.append(
            lax.ppermute(cotangent, "chan", [((i + s) % groups, i) for i in range(groups)])
        )
    act_halo = slab_halo(activations)
    cot_halo = slab_halo(cotangent)

    w = jnp.roll(kernel.reshape(groups, mine, 3, 3, 3, cin), -me, axis=0)
    forward = w.transpose(4, 0, 1, 2, 3, 5).reshape(3 * channels, 9, cin)
    forward = three_pass(forward, pad_in)
    flipped = w[:, :, ::-1, ::-1, ::-1].transpose(0, 4, 5, 2, 3, 1)
    backward = [three_pass(flipped[s].reshape(3 * cin, 9, mine), pad_out) for s in range(groups)]

    partial = conv(activations, *act_halo, forward, mine, groups)
    received = [
        lax.ppermute(partial[s], "chan", [(i, (i + s) % groups) for i in range(groups)])
        for s in range(1, groups)
    ]

    grads = [kernel_grad(activations, *act_halo, cotangent)]
    (input_grad,) = conv(cotangent, *cot_halo, backward[0], cin, 1)
    for s in range(1, groups):
        halo = slab_halo(cots[s])
        grads.append(kernel_grad(activations, *act_halo, cots[s]))
        (input_grad,) = conv(cots[s], *halo, backward[s], cin, 1, input_grad)

    summed = slab_sum(jnp.stack(grads))
    summed = summed.reshape(groups, 3, 3, pad_in, -1)[:, :, :, :cin, : 3 * mine]
    summed = summed.reshape(groups, 3, 3, cin, 3, mine)
    weight_grad = jnp.roll(summed.transpose(0, 5, 1, 2, 4, 3), me, axis=0)
    cells_all = planes * lax.axis_size("slab") * height * width
    weight_grad = weight_grad.reshape(channels, taps, cin) / math.sqrt(cells_all)

    features = partial[0]
    for part in received:
        features = features + part
    return features, input_grad, weight_grad


def solution(mesh):
    return jax.shard_map(
        per_device,
        mesh=mesh,
        in_specs=(
            P("chan", "slab", None, None),
            P(None, None, "chan"),
            P("chan", "slab", None, None),
        ),
        out_specs=(
            P("chan", "slab", None, None),
            P("chan", "slab", None, None),
            P(None, None, "chan"),
        ),
        check_vma=False,
    )
```

time: 728 us -> 190 us (0.26)
  local copies, waits for them, and re-layouts: 355 us -> 29.2 us
  matrix products: 161 us -> 0 us
  waiting for transfers between devices: 137 us -> 11.1 us
  Pallas kernels: 0 us -> 114 us
  other arithmetic: 33.3 us -> 9.1 us
  starting transfers between devices: 9.55 us -> 23.3 us
  between operations: 14 us -> 0.9 us
  loops' own time: 12.8 us -> 0 us
    while x135 -> x0, local copies, waits for them, and re-layouts: 187 us -> none
    dot_general x10 -> x0, matrix products: 161 us -> none  [the longest x2 59.6 us: back_block(): lax.dot_general(inner, patches, (((1,), (1,)), ((), ())), precision=HIGHE...]
    reshape x5 -> x7, local copies, waits for them, and re-layouts: 128 us -> 10 us  [the longest x4 6.54 us: three_pass(): matrix = matrix.reshape(rows, taps * padded)]
    pallas_call x0 -> x5, Pallas kernels: none -> 114 us  [the longest x3 77 us: conv(): pl.pallas_call(functools.partial(conv_kernel, (chans, padded, planes, hei...]
    reduce_scatter x1 -> x0, waiting for transfers between devices: 75.4 us -> none  [per_device(): lax.psum_scatter(forward_planes(kernel_mat, padded_in), 'chan', scatter_d...]
    all_gather x1 -> x0, waiting for transfers between devices: 61.1 us -> none  [per_device(): all_cot = lax.all_gather(cotangent, 'chan', axis=0, tiled=True)]
    dynamic_update_slice x2 -> x0, other arithmetic: 24.1 us -> none  [per_device(): grad_parts, grad_blocks = lax.map(back_block, jnp.arange(planes // 2))]
    ppermute x4 -> x12, starting transfers between devices: 9.43 us -> 23.3 us  [the longest x3 8.72 us: slab_halo(): below = lax.ppermute(field[:, planes - 1:], 'slab', up)]
  transfers between devices with their start and end apart: 7 -> 12, of which waited for: 2 -> 2; matrix products, arithmetic and copies ran while one was open for 29% -> 15% of each run, Pallas kernels for 0% -> 61%
where the time goes in v1:
time: 190 us; the launch traced here: 187 us
  Pallas kernels  114 us (60%)
  local copies, waits for them, and re-layouts  29.2 us (15%)
  starting transfers between devices  23.3 us (12%)
  waiting for transfers between devices  11.1 us (6%)
  other arithmetic  9.1 us (5%)
    pallas_call x3, Pallas kernels, conv(): pl.pallas_call(functools.partial(conv_kernel, (chans, padded, planes, hei...  77 us
    pallas_call x2, Pallas kernels, kernel_grad(): pl.pallas_call(functools.partial(grad_kernel, (chans, padded, planes, hei...  36.7 us
    ppermute x4, waiting for transfers between devices, slab_sum(): lax.ppermute(value, 'slab', [(i, i ^ bit) for i in range(count)])  11.1 us
    ppermute x3, starting transfers between devices, slab_halo(): below = lax.ppermute(field[:, planes - 1:], 'slab', up)  8.72 us
    ppermute x4, starting transfers between devices, slab_sum(): lax.ppermute(value, 'slab', [(i, i ^ bit) for i in range(count)])  7.2 us
    reshape x4, local copies, waits for them, and re-layouts, three_pass(): matrix = matrix.reshape(rows, taps * padded)  6.54 us
    slice x3, local copies, waits for them, and re-layouts, slab_halo(): above = lax.ppermute(field[:, :1], 'slab', down)  5.85 us
    rev x1, local copies, waits for them, and re-layouts, per_device(): flipped = w[:, :, ::-1, ::-1, ::-1].transpose(0, 4, 5, 2, 3, 1)  5.09 us
  transfers between devices with their start and end apart: 12, of which 2 were waited for; matrix products, arithmetic and copies ran while one was open for 15% of the time, Pallas kernels for 61%

profile of v1, /device:TPU:0, one launch (start us, length us, event | category | flops | bytes accessed | tf_op | source)
XLA Modules:
  0.0 187.2 jit_solution(16000801431903406949)
XLA Ops:
  0.6 0.0 copy-start.8
  0.6 2.3 %fusion.24 = (f32[32,1,32,128]{3,2,1,0:T(8,128)}, f32[32,1,32,128]{3,2,1,0:T(8,128)}) fusion(f32[32,4,32,128]{3,2,1,0:T(8,128)} %param.5), kind=kLoop, calls=%fused_computation.37 | loop fusion | bytes 2097152 | tf_op jit(solution)/shard_map/slice | solution.py:264
  2.9 1.3 collective-permute-start.1
  4.2 3.1 %collective-permute-start = (f32[32,1,32,128]{3,2,1,0:T(8,128)}, f32[32,1,32,128]{3,2,1,0:T(8,128)S(1)}, u32[]{:S(2)}, u32[]{:S(2)}) collective-permute-start(f32[32,1,32,128]{3,2,1,0:T(8,128)} %get-tuple-element.13), channel_id=1, source_target_pairs={{0,2},{2,4},{4,6},{6,8},{8,10},{10,12},{12,14},{14,16},{16,18},{18... | collective-permute-start | bytes 1572872 | tf_op jit(solution)/shard_map/ppermute | solution.py:263
  7.3 3.0 %collective-permute-start.3 = (f32[32,4,32,128]{3,2,1,0:T(8,128)}, f32[32,4,32,128]{3,2,1,0:T(8,128)}, u32[]{:S(2)}, u32[]{:S(2)}) collective-permute-start(f32[32,4,32,128]{3,2,1,0:T(8,128)} %param.7), channel_id=1, source_target_pairs={{1,0},{0,1},{3,2},{2,3},{5,4},{4,5},{7,6},{6,7},{9,8},{8,9},{11,10... | collective-permute-start | bytes 6291464 | tf_op jit(solution)/shard_map/ppermute | solution.py:291
  10.3 2.3 %fusion.22 = (f32[32,1,32,128]{3,2,1,0:T(8,128)}, f32[32,1,32,128]{3,2,1,0:T(8,128)}) fusion(f32[32,4,32,128]{3,2,1,0:T(8,128)} %param.7), kind=kLoop, calls=%fused_computation.35 | loop fusion | bytes 2097152 | tf_op jit(solution)/shard_map/slice | solution.py:264
  12.6 1.3 collective-permute-start.7
  13.9 4.2 %collective-permute-start.6 = (f32[32,1,32,128]{3,2,1,0:T(8,128)}, f32[32,1,32,128]{3,2,1,0:T(8,128)}, u32[]{:S(2)}, u32[]{:S(2)}) collective-permute-start(f32[32,1,32,128]{3,2,1,0:T(8,128)} %get-tuple-element.9), channel_id=1, source_target_pairs={{0,2},{2,4},{4,6},{6,8},{8,10},{10,12},{12,14},{14,16},{16,18},{18... | collective-permute-start | bytes 1572872 | tf_op jit(solution)/shard_map/ppermute | solution.py:263
  18.0 0.0 copy-done.8
  18.0 1.4 reshape.69
  19.5 1.8 copy.21
  21.3 1.6 fusion.27
  22.8 1.6 fusion
  24.4 5.1 %rev.3 = f32[2,32,3,3,3,32]{1,3,2,5,4,0:T(4,128)} reverse(f32[2,32,3,3,3,32]{1,3,2,5,4,0:T(4,128)} %fusion), dimensions={2,3,4} | reverse | bytes 442368 | tf_op jit(solution)/shard_map/rev | solution.py:299
  29.5 0.0 copy-done.5
  29.5 1.4 copy.28
  30.8 1.9 reshape.81
  32.7 0.0 copy-done.6
  32.7 1.2 fusion.25
  33.9 1.3 reshape.78
  35.2 2.0 %reshape.74 = f32[96,288]{1,0:T(8,128)} reshape(f32[1,3,32,3,3,32]{5,4,3,2,1,0:T(4,128)} %get-tuple-element.15) | data formatting | bytes 221184 | tf_op jit(solution)/shard_map/reshape | solution.py:250
  37.3 0.2 fusion.7.refs_3_
  37.5 0.0 collective-permute-done.1
  37.5 0.0 copy-start.1
  37.5 0.0 collective-permute-done
  37.5 0.0 copy-start.3
  37.5 0.8 copy-done.3
  38.4 1.6 copy-done
  40.0 1.0 copy-done.4
  41.0 27.6 %conv.3 = (f32[32,4,32,128]{3,2,1,0:T(8,128)S(1)}, f32[32,4,32,128]{3,2,1,0:T(8,128)}) custom-call(f32[4096,128]{1,0:T(8,128)S(1)} %bitcast.29, f32[1024,128]{1,0:T(8,128)S(1)} %bitcast.36, f32[1024,128]{1,0:T(8,128)S(1)} %bitcast.33, bf16[192,896]{1,0:T(8,128)(2,1)S(1)} %fusion.7.refs_3_), custom_call_target="tpu_custom_call" | custom-call | flops 10871635968 | bytes 6291456 | tf_op jit(solution)/shard_map/conv/pallas_call | solution.py:123
  68.6 0.5 collective-permute-start.2
  69.1 1.0 copy-done.2
  70.2 18.3 %kernel_grad.2 = f32[288,128]{1,0:T(8,128)S(1)} custom-call(f32[4096,128]{1,0:T(8,128)S(1)} %bitcast.30, f32[1024,128]{1,0:T(8,128)S(1)} %bitcast.37, f32[1024,128]{1,0:T(8,128)S(1)} %bitcast.34, f32[4096,128]{1,0:T(8,128)} %bitcast.8.refs_0_.cot), custom_call_target="tpu_custom_call" | custom-call | flops 5435817984 | bytes 4194304 | tf_op jit(solution)/shard_map/kernel_grad/pallas_call | solution.py:220
  88.5 0.0 collective-permute-done.3
  88.5 0.0 copy-start.7
  88.5 18.4 %kernel_grad.3 = f32[288,128]{1,0:T(8,128)S(1)} custom-call(f32[4096,128]{1,0:T(8,128)S(1)} %bitcast.31, f32[1024,128]{1,0:T(8,128)S(1)} %bitcast.38, f32[1024,128]{1,0:T(8,128)S(1)} %bitcast.35, f32[4096,128]{1,0:T(8,128)} %bitcast.4.refs_0_.cot), custom_call_target="tpu_custom_call" | custom-call | flops 5435817984 | bytes 4194304 | tf_op jit(solution)/shard_map/kernel_grad/pallas_call | solution.py:220
  107.0 0.7 collective-permute-start.8
  107.7 0.1 fusion.18.refs_3_
  107.8 0.0 copy-done.7
  107.9 1.0 collective-permute-done.8
  108.9 0.8 fusion.21
  109.7 3.3 %collective-permute-start.9 = (f32[2,288,128]{2,1,0:T(8,128)}, f32[2,288,128]{2,1,0:T(8,128)}, u32[]{:S(2)}, u32[]{:S(2)}) collective-permute-start(f32[2,288,128]{2,1,0:T(8,128)} %fusion.21), channel_id=1, source_target_pairs={{0,4},{2,6},{4,0},{6,2},{8,12},{10,14},{12,8},{14,10},{16,20},{18,... | collective-permute-start | bytes 884744 | tf_op jit(solution)/shard_map/ppermute | solution.py:274
  112.9 0.1 fusion.16.refs_3_
  113.1 1.3 fusion.23
  114.4 1.3 collective-permute-start.5
  115.7 10.0 %collective-permute-done.9 = f32[2,288,128]{2,1,0:T(8,128)} collective-permute-done((f32[2,288,128]{2,1,0:T(8,128)}, f32[2,288,128]{2,1,0:T(8,128)}, u32[]{:S(2)}, u32[]{:S(2)}) %collective-permute-start.9) | collective-permute-done | bytes 294944 | tf_op jit(solution)/shard_map/ppermute | solution.py:274
  125.7 1.5 collective-permute-start.4
  127.2 1.0 fusion.26
  128.2 0.0 collective-permute-done.7
  128.2 2.1 %collective-permute-start.10 = (f32[2,288,128]{2,1,0:T(8,128)S(1)}, f32[2,288,128]{2,1,0:T(8,128)S(1)}, u32[]{:S(2)}, u32[]{:S(2)}) collective-permute-start(f32[2,288,128]{2,1,0:T(8,128)S(1)} %fusion.26), channel_id=1, source_target_pairs={{0,8},{2,10},{4,12},{6,14},{8,0},{10,2},{12,4},{14,6},{16,24},{18,... | collective-permute-start | bytes 884744 | tf_op jit(solution)/shard_map/ppermute | solution.py:274
  130.3 0.0 collective-permute-done.6
  130.3 24.3 %conv.4.refs_4_ = f32[32,4,32,128]{3,2,1,0:T(8,128)S(1)} custom-call(f32[4096,128]{1,0:T(8,128)} %bitcast.8.refs_0_.cot, f32[1024,128]{1,0:T(8,128)} %bitcast.9.refs_1_, f32[1024,128]{1,0:T(8,128)S(1)} %bitcast.32, bf16[96,896]{1,0:T(8,128)(2,1)S(1)} %fusion.18.refs_3_), custom_call_target="tpu_custom_call" | custom-call | flops 5435817984 | bytes 4194304 | tf_op jit(solution)/shard_map/conv/pallas_call | solution.py:123
  154.6 0.0 collective-permute-done.2
  154.6 3.4 %add.29 = f32[32,4,32,128]{3,2,1,0:T(8,128)} add(f32[32,4,32,128]{3,2,1,0:T(8,128)S(1)} %get-tuple-element.6, f32[32,4,32,128]{3,2,1,0:T(8,128)} %collective-permute-done.2) | non-fusion elementwise | flops 524288 | bytes 6291456 | tf_op jit(solution)/shard_map/add | solution.py:324
  158.0 0.0 collective-permute-done.10
  158.1 1.1 collective-permute-start.11
  159.2 0.0 collective-permute-done.5
  159.2 0.0 collective-permute-done.4
  159.2 25.0 %conv.5 = f32[32,4,32,128]{3,2,1,0:T(8,128)} custom-call(f32[4096,128]{1,0:T(8,128)} %bitcast.4.refs_0_.cot, f32[1024,128]{1,0:T(8,128)S(1)} %bitcast.40, f32[1024,128]{1,0:T(8,128)S(1)} %bitcast.39, bf16[96,896]{1,0:T(8,128)(2,1)S(1)} %fusion.16.refs_3_, f32[32,4,32,128]{3,2,1,0:T(8,128)S(1)} %conv.4.refs_4_), custom_call_target="tpu_custom_call" | custom-call | flops 5435817984 | bytes 4194304 | tf_op jit(solution)/shard_map/conv/pallas_call | solution.py:123
  184.2 0.0 collective-permute-done.11
  184.3 0.3 copy.30
  184.6 0.2 fusion.2
  184.8 1.2 copy.27
  186.0 1.3 div.10
  (12 shorter events, 0.2 us)
Async XLA Ops:
  0.6 17.4 %copy-start.8 = (f32[64,27,32]{0,2,1:T(8,128)S(1)}, f32[64,27,32]{0,2,1:T(8,128)}, u32[]{:S(2)}) copy-start(f32[64,27,32]{0,2,1:T(8,128)} %param.6) | copy-start | bytes 663556
  2.9 34.5 %collective-permute-start.1 = (f32[32,1,32,128]{3,2,1,0:T(8,128)}, f32[32,1,32,128]{3,2,1,0:T(8,128)S(1)}, u32[]{:S(2)}, u32[]{:S(2)}) collective-permute-start(f32[32,1,32,128]{3,2,1,0:T(8,128)} %get-tuple-element.12), channel_id=1, source_target_pairs={{2,0},{4,2},{6,4},{8,6},{10,8},{12,10},{14,12},{16,14},{18,16},{20... | collective-permute-start | bytes 1572872 | tf_op jit(solution)/shard_map/ppermute | solution.py:264
  4.2 33.3 %collective-permute-start = (f32[32,1,32,128]{3,2,1,0:T(8,128)}, f32[32,1,32,128]{3,2,1,0:T(8,128)S(1)}, u32[]{:S(2)}, u32[]{:S(2)}) collective-permute-start(f32[32,1,32,128]{3,2,1,0:T(8,128)} %get-tuple-element.13), channel_id=1, source_target_pairs={{0,2},{2,4},{4,6},{6,8},{8,10},{10,12},{12,14},{14,16},{16,18},{18... | collective-permute-start | bytes 1572872 | tf_op jit(solution)/shard_map/ppermute | solution.py:263
  7.3 81.2 %collective-permute-start.3 = (f32[32,4,32,128]{3,2,1,0:T(8,128)}, f32[32,4,32,128]{3,2,1,0:T(8,128)}, u32[]{:S(2)}, u32[]{:S(2)}) collective-permute-start(f32[32,4,32,128]{3,2,1,0:T(8,128)} %param.7), channel_id=1, source_target_pairs={{1,0},{0,1},{3,2},{2,3},{5,4},{4,5},{7,6},{6,7},{9,8},{8,9},{11,10... | collective-permute-start | bytes 6291464 | tf_op jit(solution)/shard_map/ppermute | solution.py:291
  12.6 115.6 %collective-permute-start.7 = (f32[32,1,32,128]{3,2,1,0:T(8,128)}, f32[32,1,32,128]{3,2,1,0:T(8,128)S(1)}, u32[]{:S(2)}, u32[]{:S(2)}) collective-permute-start(f32[32,1,32,128]{3,2,1,0:T(8,128)} %get-tuple-element.8), channel_id=1, source_target_pairs={{2,0},{4,2},{6,4},{8,6},{10,8},{12,10},{14,12},{16,14},{18,16},{20... | collective-permute-start | bytes 1572872 | tf_op jit(solution)/shard_map/ppermute | solution.py:264
  13.9 116.4 %collective-permute-start.6 = (f32[32,1,32,128]{3,2,1,0:T(8,128)}, f32[32,1,32,128]{3,2,1,0:T(8,128)}, u32[]{:S(2)}, u32[]{:S(2)}) collective-permute-start(f32[32,1,32,128]{3,2,1,0:T(8,128)} %get-tuple-element.9), channel_id=1, source_target_pairs={{0,2},{2,4},{4,6},{6,8},{8,10},{10,12},{12,14},{14,16},{16,18},{18... | collective-permute-start | bytes 1572872 | tf_op jit(solution)/shard_map/ppermute | solution.py:263
  24.4 5.1 %copy-start.5 = (f32[3,2,32,3,3,32]{2,4,3,5,0,1:T(4,128)S(1)}, f32[3,2,32,3,3,32]{2,4,3,5,0,1:T(4,128)}, u32[]{:S(2)}) copy-start(f32[3,2,32,3,3,32]{2,4,3,5,0,1:T(4,128)} %fusion.27) | copy-start | bytes 663556
  30.8 1.9 copy-start.6
  37.5 31.1 %copy-start.1 = (f32[32,1,32,128]{3,2,1,0:T(8,128)}, f32[32,1,32,128]{3,2,1,0:T(8,128)S(1)}, u32[]{:S(2)}) copy-start(f32[32,1,32,128]{3,2,1,0:T(8,128)S(1)} %collective-permute-done.1) | copy-start | bytes 1572868
  37.5 0.8 copy-start.3
  38.4 1.6 copy-start
  40.0 1.0 copy-start.4
  68.6 86.0 %collective-permute-start.2 = (f32[32,4,32,128]{3,2,1,0:T(8,128)}, f32[32,4,32,128]{3,2,1,0:T(8,128)}, u32[]{:S(2)}, u32[]{:S(2)}) collective-permute-start(f32[32,4,32,128]{3,2,1,0:T(8,128)} %get-tuple-element.7), channel_id=1, source_target_pairs={{0,1},{1,0},{2,3},{3,2},{4,5},{5,4},{6,7},{7,6},{8,9},{9,8},{10,11... | collective-permute-start | bytes 6291464 | tf_op jit(solution)/shard_map/ppermute | solution.py:304
  69.1 1.0 copy-start.2
  88.5 19.3 %copy-start.7 = (f32[96,288]{1,0:T(8,128)S(1)}, f32[96,288]{1,0:T(8,128)}, u32[]{:S(2)}) copy-start(f32[96,288]{1,0:T(8,128)} %reshape.74) | copy-start | bytes 331780
  107.0 2.0 %collective-permute-start.8 = (f32[2,288,128]{2,1,0:T(8,128)S(1)}, f32[2,288,128]{2,1,0:T(8,128)S(1)}, u32[]{:S(2)}, u32[]{:S(2)}) collective-permute-start(f32[2,288,128]{2,1,0:T(8,128)S(1)} %pad_maximum_fusion), channel_id=1, source_target_pairs={{0,2},{2,0},{4,6},{6,4},{8,10},{10,8},{12,14},{14,12},{16,18},{18,... | collective-permute-start | bytes 884744 | tf_op jit(solution)/shard_map/ppermute | solution.py:274
  109.7 16.0 %collective-permute-start.9 = (f32[2,288,128]{2,1,0:T(8,128)}, f32[2,288,128]{2,1,0:T(8,128)}, u32[]{:S(2)}, u32[]{:S(2)}) collective-permute-start(f32[2,288,128]{2,1,0:T(8,128)} %fusion.21), channel_id=1, source_target_pairs={{0,4},{2,6},{4,0},{6,2},{8,12},{10,14},{12,8},{14,10},{16,20},{18,... | collective-permute-start | bytes 884744 | tf_op jit(solution)/shard_map/ppermute | solution.py:274
  114.4 44.8 %collective-permute-start.5 = (f32[32,1,32,128]{3,2,1,0:T(8,128)S(1)}, f32[32,1,32,128]{3,2,1,0:T(8,128)S(1)}, u32[]{:S(2)}, u32[]{:S(2)}) collective-permute-start(f32[32,1,32,128]{3,2,1,0:T(8,128)S(1)} %get-tuple-element.10), channel_id=1, source_target_pairs={{2,0},{4,2},{6,4},{8,6},{10,8},{12,10},{14,12},{16,14},{18,16},{20... | collective-permute-start | bytes 1572872 | tf_op jit(solution)/shard_map/ppermute | solution.py:264
  125.7 33.5 %collective-permute-start.4 = (f32[32,1,32,128]{3,2,1,0:T(8,128)S(1)}, f32[32,1,32,128]{3,2,1,0:T(8,128)S(1)}, u32[]{:S(2)}, u32[]{:S(2)}) collective-permute-start(f32[32,1,32,128]{3,2,1,0:T(8,128)S(1)} %get-tuple-element.11), channel_id=1, source_target_pairs={{0,2},{2,4},{4,6},{6,8},{8,10},{10,12},{12,14},{14,16},{16,18},{18... | collective-permute-start | bytes 1572872 | tf_op jit(solution)/shard_map/ppermute | solution.py:263
  128.2 29.8 %collective-permute-start.10 = (f32[2,288,128]{2,1,0:T(8,128)S(1)}, f32[2,288,128]{2,1,0:T(8,128)S(1)}, u32[]{:S(2)}, u32[]{:S(2)}) collective-permute-start(f32[2,288,128]{2,1,0:T(8,128)S(1)} %fusion.26), channel_id=1, source_target_pairs={{0,8},{2,10},{4,12},{6,14},{8,0},{10,2},{12,4},{14,6},{16,24},{18,... | collective-permute-start | bytes 884744 | tf_op jit(solution)/shard_map/ppermute | solution.py:274
  158.1 26.2 %collective-permute-start.11 = (f32[2,288,128]{2,1,0:T(8,128)S(1)}, f32[2,288,128]{2,1,0:T(8,128)S(1)}, u32[]{:S(2)}, u32[]{:S(2)}) collective-permute-start(f32[2,288,128]{2,1,0:T(8,128)S(1)} %add.32), channel_id=1, source_target_pairs={{0,16},{2,18},{4,20},{6,22},{8,24},{10,26},{12,28},{14,30},{16,0},... | collective-permute-start | bytes 884744 | tf_op jit(solution)/shard_map/ppermute | solution.py:274

commit v2 on v1

v2 whole, which is shorter than its diff:
```python
import functools
import math

import jax
import jax.numpy as jnp
from jax import lax
from jax.experimental import pallas as pl
from jax.experimental.pallas import tpu as pltpu
from jax.sharding import PartitionSpec as P

F32 = jnp.float32
BF16 = jnp.bfloat16
ROWS = 8
WHOLE = pl.BlockSpec(memory_space=pltpu.VMEM)
SCALAR = pl.BlockSpec(memory_space=pltpu.SMEM)


def up_to(size, unit):
    return -(-size // unit) * unit


def split(x):
    hi = x.astype(BF16)
    return hi, (x - hi.astype(F32)).astype(BF16)


def params(steps=1):
    return pltpu.CompilerParams(
        dimension_semantics=("arbitrary",) * steps or None, vmem_limit_bytes=32 << 20
    )


def fill_plane(dst_hi, dst_lo, plane, load, chans, padded, height):
    width = dst_hi.shape[-1]
    blank = jnp.zeros((padded, width), BF16)
    for dst in (dst_hi, dst_lo):
        dst[plane, pl.ds(0, padded), :] = blank
        dst[plane, pl.ds((height + 1) * padded, padded), :] = blank

    def one_block(block, carry):
        rows = jnp.swapaxes(load(pl.ds(pl.multiple_of(ROWS * block, ROWS), ROWS)), 0, 1)
        if padded != chans:
            fill = jnp.zeros((ROWS, padded - chans, width), F32)
            rows = jnp.concatenate([rows, fill], axis=1)
        hi, lo = split(rows.reshape(ROWS * padded, width))
        start = pl.multiple_of((ROWS * block + 1) * padded, padded)
        dst_hi[plane, pl.ds(start, ROWS * padded), :] = hi
        dst_lo[plane, pl.ds(start, ROWS * padded), :] = lo
        return carry

    lax.fori_loop(0, height // ROWS, one_block, 0, unroll=True)


def fill_field(dst_hi, dst_lo, field, below, above, chans, padded, planes, height):
    fill_plane(dst_hi, dst_lo, 0, lambda s: below[:, 0, s, :], chans, padded, height)
    fill_plane(dst_hi, dst_lo, planes + 1, lambda s: above[:, 0, s, :], chans, padded, height)

    def one_plane(d, carry):
        fill_plane(dst_hi, dst_lo, d + 1, lambda s: field[:, d, s, :], chans, padded, height)
        return carry

    lax.fori_loop(0, planes, one_plane, 0)


def conv_kernel(dims, sizes, unroll, has_acc, *refs):
    chans, padded, planes, height = dims
    field, below, above, weight = refs[:4]
    refs = refs[4:]
    acc = None
    if has_acc:
        acc, refs = refs[0], refs[1:]
    results = refs[: len(sizes)]
    xh, xl = refs[len(sizes) :]
    d = pl.program_id(0)
    width = field.shape[-1]
    rows_out = sum(sizes)
    span = 3 * padded

    @pl.when(d == 0)
    def _():
        fill_field(xh, xl, field, below, above, chans, padded, planes, height)

    lane = lax.broadcasted_iota(jnp.int32, (rows_out, width), 1)
    first = lane == 0
    last = lane == width - 1

    def one_block(block, carry):
        h = ROWS * block
        parts = []
        for src in (xh, xl):
            for i in range(3):
                window = src[
                    d + i, pl.ds(pl.multiple_of(h * padded, padded), (ROWS + 2) * padded), :
                ]
                parts.append(
                    jnp.concatenate(
                        [window[r * padded : r * padded + span] for r in range(ROWS)], axis=1
                    )
                )
        parts = parts + parts[:3]
        extra = weight.shape[1] - 9 * span
        if extra:
            parts.append(jnp.zeros((extra, ROWS * width), BF16))
        y = jnp.dot(
            weight[...], jnp.concatenate(parts, axis=0), preferred_element_type=F32
        )
        rows = []
        for r in range(ROWS):
            z = y[:, r * width : (r + 1) * width]
            left = jnp.where(first, 0.0, pltpu.roll(z[:rows_out], 1, 1))
            right = jnp.where(last, 0.0, pltpu.roll(z[2 * rows_out :], width - 1, 1))
            rows.append(z[rows_out : 2 * rows_out] + left + right)
        swapped = jnp.swapaxes(jnp.stack(rows), 0, 1)
        where = pl.ds(pl.multiple_of(h, ROWS), ROWS)
        start = 0
        for ref, size in zip(results, sizes):
            piece = swapped[start : start + size]
            if acc is not None:
                piece = piece + acc[:, 0, where, :]
            ref[:, 0, where, :] = piece
            start += size
        return carry

    lax.fori_loop(0, height // ROWS, one_block, 0, unroll=unroll)


def conv(field, below, above, weight, sizes, unroll, acc=None):
    chans, planes, height, width = field.shape
    padded = up_to(chans, 16)

    def plane_spec(size):
        return pl.BlockSpec((size, 1, height, width), lambda d: (0, d, 0, 0))

    args = [field, below, above, weight]
    in_specs = [WHOLE] * 4
    if acc is not None:
        args.append(acc)
        in_specs.append(plane_spec(sizes[0]))
    cells = planes * height * width
    return pl.pallas_call(
        functools.partial(
            conv_kernel, (chans, padded, planes, height), sizes, unroll, acc is not None
        ),
        grid=(planes,),
        in_specs=in_specs,
        out_specs=[plane_spec(size) for size in sizes],
        out_shape=[jax.ShapeDtypeStruct((size, planes, height, width), F32) for size in sizes],
        scratch_shapes=[
            pltpu.VMEM((planes + 2, (height + 2) * padded, width), BF16) for _ in range(2)
        ],
        compiler_params=params(),
        cost_estimate=pl.CostEstimate(
            flops=6 * 27 * chans * sum(sizes) * cells * 2 // 20,
            bytes_accessed=4 * (chans + sum(sizes)) * cells // 20,
            transcendentals=0,
        ),
        name="conv",
    )(*args)


def grad_kernel(dims, others, *refs):
    chans, padded, planes, height = dims
    field, below, above, cot = refs[:4]
    done = refs[4 : 4 + others]
    out, xh, xl, total = refs[4 + others :]
    outs = cot.shape[0]
    width = field.shape[-1]
    step = pl.program_id(0)
    span = 3 * padded
    half = 3 * span
    group = up_to(3 * outs, 128)

    @pl.when(step == 0)
    def _():
        fill_field(xh, xl, field, below, above, chans, padded, planes, height)
        total[...] = jnp.zeros_like(total)

    lane = lax.broadcasted_iota(jnp.int32, (outs, width), 1)
    first = lane == 0
    last = lane == width - 1
    lhs = []
    for src in (xh, xl):
        for i in range(3):
            window = src[step + i]
            lhs.append(
                jnp.concatenate(
                    [window[r * padded : r * padded + span] for r in range(height)], axis=1
                )
            )
    columns = []
    for block in range(height // ROWS):
        rows = jnp.swapaxes(cot[:, 0, pl.ds(ROWS * block, ROWS), :], 0, 1)
        for r in range(ROWS):
            c = rows[r]
            moved = [
                jnp.where(last, 0.0, pltpu.roll(c, width - 1, 1)),
                c,
                jnp.where(first, 0.0, pltpu.roll(c, 1, 1)),
            ]
            pieces = [split(m) for m in moved]
            gap = group - 3 * outs
            fill = [jnp.zeros((gap, width), BF16)] if gap else []
            columns.append(
                jnp.concatenate(
                    [p[0] for p in pieces] + fill + [p[1] for p in pieces] + fill, axis=0
                )
            )
    total[...] += lax.dot_general(
        jnp.concatenate(lhs, axis=0),
        jnp.concatenate(columns, axis=1),
        (((1,), (1,)), ((), ())),
        preferred_element_type=F32,
    )

    @pl.when(step == planes - 1)
    def _():
        for index, ref in enumerate(done):
            out[index] = ref[0]
        out[others] = total[:half, :group] + total[:half, group:] + total[half:, :group]


def kernel_grad(field, below, above, cot, done=()):
    chans, planes, height, width = field.shape
    outs = cot.shape[0]
    padded = up_to(chans, 16)
    group = up_to(3 * outs, 128)
    cells = planes * height * width
    count = len(done) + 1
    return pl.pallas_call(
        functools.partial(grad_kernel, (chans, padded, planes, height), len(done)),
        grid=(planes,),
        in_specs=[WHOLE] * 3
        + [pl.BlockSpec((outs, 1, height, width), lambda d: (0, d, 0, 0))]
        + [WHOLE] * len(done),
        out_specs=pl.BlockSpec((count, 9 * padded, group), lambda d: (0, 0, 0)),
        out_shape=jax.ShapeDtypeStruct((count, 9 * padded, group), F32),
        scratch_shapes=[
            pltpu.VMEM((planes + 2, (height + 2) * padded, width), BF16) for _ in range(2)
        ]
        + [pltpu.VMEM((18 * padded, 2 * group), F32)],
        compiler_params=params(),
        cost_estimate=pl.CostEstimate(
            flops=6 * 27 * chans * outs * cells * 2 // 20,
            bytes_accessed=4 * (chans + outs) * cells // 20,
            transcendentals=0,
        ),
        name="kernel_grad",
    )(field, below, above, cot, *done)


def three_parts(matrix, wide):
    hi, lo = split(matrix)
    parts = [hi, hi, lo]
    extra = wide - 3 * matrix.shape[1]
    if extra:
        parts.append(jnp.zeros((matrix.shape[0], extra), BF16))
    return jnp.concatenate(parts, axis=1)


def weight_kernel(groups, me, taps, forward, *refs):
    backward, turned = refs[:groups], refs[groups]
    cin, channels = taps.shape[1:]
    mine = channels // groups
    pad_in = up_to(cin, 16)
    pad_out = up_to(mine, 16)
    for k in range(3):
        blocks = []
        for tap in range(9):
            blocks.append(taps[3 * tap + k])
            if pad_in != cin:
                blocks.append(jnp.zeros((pad_in - cin, channels), F32))
        turned[...] = jnp.concatenate(blocks, axis=0).T
        for g in range(groups):
            owner = lax.rem(me[0] + g, groups)
            rows = turned[pl.ds(pl.multiple_of(owner * mine, mine), mine), :]
            forward[pl.ds(k * channels + g * mine, mine), :] = three_parts(
                rows, forward.shape[1]
            )
    for s in range(groups):
        owner = lax.rem(me[0] + s, groups)
        for k in range(3):
            blocks = []
            for tap in range(9):
                block = taps[26 - 3 * tap - k]
                chosen = block[:, :mine]
                for q in range(1, groups):
                    chosen = jnp.where(owner == q, block[:, q * mine : (q + 1) * mine], chosen)
                blocks.append(chosen)
                if pad_out != mine:
                    blocks.append(jnp.zeros((cin, pad_out - mine), F32))
            backward[s][pl.ds(k * cin, cin), :] = three_parts(
                jnp.concatenate(blocks, axis=1), backward[s].shape[1]
            )


def weight_matrices(me, taps, groups):
    _, cin, channels = taps.shape
    mine = channels // groups
    pad_in = up_to(cin, 16)
    wide_in = up_to(27 * pad_in, 128)
    wide_out = up_to(27 * up_to(mine, 16), 128)
    return pl.pallas_call(
        functools.partial(weight_kernel, groups),
        in_specs=[SCALAR, WHOLE],
        out_specs=[WHOLE] * (groups + 1),
        out_shape=[jax.ShapeDtypeStruct((3 * channels, wide_in), BF16)]
        + [jax.ShapeDtypeStruct((3 * cin, wide_out), BF16)] * groups,
        scratch_shapes=[pltpu.VMEM((channels, 9 * pad_in), F32)],
        compiler_params=params(0),
        name="weights",
    )(me, taps)


def finish_kernel(groups, scale, me, mine_ref, other_ref, out):
    cin, channels = out.shape[1:]
    mine = channels // groups
    padded = mine_ref.shape[1] // 9
    totals = [(mine_ref[s] + other_ref[s]) * scale for s in range(groups)]
    for k in range(3):
        pieces = [t[:, k * mine : (k + 1) * mine] for t in totals]
        blocks = []
        for q in range(groups):
            source = lax.rem(q - me[0] + groups, groups)
            chosen = pieces[0]
            for s in range(1, groups):
                chosen = jnp.where(source == s, pieces[s], chosen)
            blocks.append(chosen)
        wide = jnp.concatenate(blocks, axis=1)
        for tap in range(9):
            out[3 * tap + k] = wide[tap * padded : tap * padded + cin]


def finish(me, value, other, groups, cin, channels, scale):
    return pl.pallas_call(
        functools.partial(finish_kernel, groups, scale),
        in_specs=[SCALAR, WHOLE, WHOLE],
        out_specs=WHOLE,
        out_shape=jax.ShapeDtypeStruct((27, cin, channels), F32),
        compiler_params=params(0),
        name="finish",
    )(me, value, other)


def add_kernel(base, piece, out):
    out[...] = base[...] + piece[...]


def add_into(base, piece, first, block):
    shape = (block,) + base.shape[1:]
    spec = pl.BlockSpec(shape, lambda c: (first // block + c, 0, 0, 0))
    return pl.pallas_call(
        add_kernel,
        grid=(piece.shape[0] // block,),
        in_specs=[spec, pl.BlockSpec(shape, lambda c: (c, 0, 0, 0))],
        out_specs=spec,
        out_shape=jax.ShapeDtypeStruct(base.shape, F32),
        input_output_aliases={0: 0},
        compiler_params=params(),
        cost_estimate=pl.CostEstimate(
            flops=piece.size, bytes_accessed=12 * piece.size, transcendentals=0
        ),
        name="add_into",
    )(base, piece)


def slab_halo(field):
    count = lax.axis_size("slab")
    planes = field.shape[1]
    up = [(i, i + 1) for i in range(count - 1)]
    down = [(i + 1, i) for i in range(count - 1)]
    top, bottom = field[:, planes - 1 :], field[:, :1]
    field, top, bottom = lax.optimization_barrier((field, top, bottom))
    return field, (lax.ppermute(top, "slab", up), lax.ppermute(bottom, "slab", down))


def slab_sum(value):
    count = lax.axis_size("slab")
    if count & (count - 1):
        value = lax.psum(value, "slab")
        return value, jnp.zeros_like(value)
    bit = 1
    other = jnp.zeros_like(value) if count == 1 else None
    while bit < count:
        if other is not None:
            value = value + other
        other = lax.ppermute(value, "slab", [(i, i ^ bit) for i in range(count)])
        bit *= 2
    return value, other


def per_device(activations, kernel, cotangent):
    groups = lax.axis_size("chan")
    me = lax.axis_index("chan").reshape(1)
    channels, taps, cin = kernel.shape
    mine = channels // groups
    planes, height, width = activations.shape[1:]
    tail = max(mine // 4, 1)
    pieces = (mine - tail, tail)

    cots = [cotangent]
    for s in range(1, groups):
        cots.append(
            lax.ppermute(cotangent, "chan", [((i + s) % groups, i) for i in range(groups)])
        )
    activations, act_halo = slab_halo(activations)
    forward, *backward = weight_matrices(me, kernel.transpose(1, 2, 0), groups)

    features, *partial = conv(
        activations, *act_halo, forward, (mine,) + pieces * (groups - 1), 2
    )
    received = []
    for s in range(1, groups):
        for part in partial[2 * (s - 1) : 2 * s]:
            received.append(
                lax.ppermute(part, "chan", [(i, (i + s) % groups) for i in range(groups)])
            )

    own, _ = lax.optimization_barrier((cotangent, partial[0]))
    own, cot_halo = slab_halo(own)
    grads = [kernel_grad(activations, *act_halo, own)]
    (input_grad,) = conv(own, *cot_halo, backward[0], (cin,), 4)
    for s in range(1, groups):
        cots[s], input_grad = lax.optimization_barrier((cots[s], input_grad))
        cots[s], halo = slab_halo(cots[s])
        done = grads if s == groups - 1 else ()
        grads.append(kernel_grad(activations, *act_halo, cots[s], done))
        (input_grad,) = conv(cots[s], *halo, backward[s], (cin,), 4, input_grad)

    cells_all = planes * lax.axis_size("slab") * height * width
    value, other = slab_sum(grads[-1])
    weight_grad = finish(me, value, other, groups, cin, channels, 1.0 / math.sqrt(cells_all))

    *received, input_grad = lax.optimization_barrier((*received, input_grad))
    for index, part in enumerate(received):
        first = 0 if index % 2 == 0 else pieces[0]
        features = add_into(features, part, first, tail)
    return features, input_grad, weight_grad.transpose(2, 0, 1)


def solution(mesh):
    return jax.shard_map(
        per_device,
        mesh=mesh,
        in_specs=(
            P("chan", "slab", None, None),
            P(None, None, "chan"),
            P("chan", "slab", None, None),
        ),
        out_specs=(
            P("chan", "slab", None, None),
            P("chan", "slab", None, None),
            P(None, None, "chan"),
        ),
        check_vma=False,
    )
```

time: 190 us -> 116 us (0.61)
  the two profiles are of different devices: /device:TPU:0 before, /device:TPU:13 now
where the time goes in v2:
time: 116 us; the launch traced here: 115 us
  Pallas kernels  50.3 us (43%)
  waiting for transfers between devices  35.5 us (31%)
  starting transfers between devices  24 us (21%)
  local copies, waits for them, and re-layouts  4.76 us (4%)
    pallas_call x3, Pallas kernels, conv(): pl.pallas_call(functools.partial(conv_kernel, (chans, padded, planes, hei...  27.3 us
    ppermute x3, waiting for transfers between devices, slab_halo(): lax.ppermute(bottom, 'slab', down)  21.6 us
    pallas_call x2, Pallas kernels, kernel_grad(): pl.pallas_call(functools.partial(grad_kernel, (chans, padded, planes, hei...  15.4 us
    ppermute x4, waiting for transfers between devices, slab_sum(): other = lax.ppermute(value, 'slab', [(i, i ^ bit) for i in range(count)])  10.3 us
    ppermute x3, starting transfers between devices, slab_halo(): lax.ppermute(top, 'slab', up)  9.81 us
    ppermute x3, starting transfers between devices, slab_halo(): lax.ppermute(bottom, 'slab', down)  7.33 us
    pallas_call x2, Pallas kernels, add_into(): pl.pallas_call(add_kernel, grid=(piece.shape[0] // block,), in_specs=[spe...  5.31 us
    ppermute x4, starting transfers between devices, slab_sum(): other = lax.ppermute(value, 'slab', [(i, i ^ bit) for i in range(count)])  4.84 us
  transfers between devices with their start and end apart: 13, of which 8 were waited for; matrix products, arithmetic and copies ran while one was open for 3% of the time, Pallas kernels for 43%

profile of v2, /device:TPU:13, one launch (start us, length us, event | category | flops | bytes accessed | tf_op | source)
XLA Modules:
  0.0 115.4 jit_solution(11078342538885639611)
XLA Ops:
  0.6 0.0 copy-start
  0.6 1.3 %collective-permute-start.4 = (f32[32,4,32,128]{3,2,1,0:T(8,128)}, f32[32,4,32,128]{3,2,1,0:T(8,128)}, u32[]{:S(2)}, u32[]{:S(2)}) collective-permute-start(f32[32,4,32,128]{3,2,1,0:T(8,128)} %refs_3_), channel_id=1, source_target_pairs={{1,0},{0,1},{3,2},{2,3},{5,4},{4,5},{7,6},{6,7},{9,8},{8,9},{11,10... | collective-permute-start | bytes 6291464 | tf_op jit(solution)/shard_map/ppermute | solution.py:403
  1.9 2.2 %fusion.2 = (f32[32,1,32,128]{3,2,1,0:T(8,128)}, f32[32,1,32,128]{3,2,1,0:T(8,128)}) fusion(f32[32,4,32,128]{3,2,1,0:T(8,128)} %refs_0_.3), kind=kLoop, calls=%fused_computation.2 | loop fusion | bytes 2097152 | tf_op jit(solution)/shard_map/slice | solution.py:371
  4.2 4.0 %collective-permute-start = (f32[32,1,32,128]{3,2,1,0:T(8,128)}, f32[32,1,32,128]{3,2,1,0:T(8,128)S(1)}, u32[]{:S(2)}, u32[]{:S(2)}) collective-permute-start(f32[32,1,32,128]{3,2,1,0:T(8,128)} %get-tuple-element.25), channel_id=1, source_target_pairs={{0,2},{2,4},{4,6},{6,8},{8,10},{10,12},{12,14},{14,16},{16,18},{18... | collective-permute-start | bytes 1572872 | tf_op jit(solution)/shard_map/ppermute | solution.py:373
  8.1 1.9 %collective-permute-start.1 = (f32[32,1,32,128]{3,2,1,0:T(8,128)}, f32[32,1,32,128]{3,2,1,0:T(8,128)S(1)}, u32[]{:S(2)}, u32[]{:S(2)}) collective-permute-start(f32[32,1,32,128]{3,2,1,0:T(8,128)} %get-tuple-element.26), channel_id=1, source_target_pairs={{2,0},{4,2},{6,4},{8,6},{10,8},{12,10},{14,12},{16,14},{18,16},{20... | collective-permute-start | bytes 1572872 | tf_op jit(solution)/shard_map/ppermute | solution.py:373
  10.1 0.0 copy-start.1
  10.1 0.0 copy-start.2
  10.1 1.2 copy-done.2
  11.2 1.3 %weights.1 = (bf16[192,896]{1,0:T(8,128)(2,1)S(1)}, bf16[96,896]{1,0:T(8,128)(2,1)S(1)}, bf16[96,896]{1,0:T(8,128)(2,1)S(1)}) custom-call(s32[1]{0:T(128)} %bitcast.me, f32[27,32,64]{2,1,0:T(8,128)S(1)} %bitcast.3), custom_call_target="tpu_custom_call" | custom-call | tf_op jit(solution)/shard_map/weights/pallas_call | solution.py:302
  12.6 2.0 %collective-permute-done.refs_1_ = f32[32,1,32,128]{3,2,1,0:T(8,128)S(1)} collective-permute-done((f32[32,1,32,128]{3,2,1,0:T(8,128)}, f32[32,1,32,128]{3,2,1,0:T(8,128)S(1)}, u32[]{:S(2)}, u32[]{:S(2)}) %collective-permute-start) | collective-permute-done | bytes 524320 | tf_op jit(solution)/shard_map/ppermute | solution.py:373
  14.6 5.3 %collective-permute-done.1.refs_2_ = f32[32,1,32,128]{3,2,1,0:T(8,128)S(1)} collective-permute-done((f32[32,1,32,128]{3,2,1,0:T(8,128)}, f32[32,1,32,128]{3,2,1,0:T(8,128)S(1)}, u32[]{:S(2)}, u32[]{:S(2)}) %collective-permute-start.1) | collective-permute-done | bytes 524320 | tf_op jit(solution)/shard_map/ppermute | solution.py:373
  19.9 0.0 copy-done
  19.9 10.9 %conv.3 = (f32[32,4,32,128]{3,2,1,0:T(8,128)}, f32[24,4,32,128]{3,2,1,0:T(8,128)S(1)}, f32[8,4,32,128]{3,2,1,0:T(8,128)S(1)}) custom-call(f32[32,4,32,128]{3,2,1,0:T(8,128)S(1)} %copy-done, f32[32,1,32,128]{3,2,1,0:T(8,128)S(1)} %collective-permute-done.refs_1_, f32[32,1,32,128]{3,2,1,0:T(8,128)S(1)} %collective-permute-done.1.refs_2_, ...), custom_call_target="tpu_custom_call" | custom-call | flops 543581824 | bytes 314572 | tf_op jit(solution)/shard_map/conv/pallas_call | solution.py:140
  30.7 0.0 copy-done.1
  30.7 0.1 fusion.1
  30.8 1.9 %collective-permute-start.5 = (f32[32,1,32,128]{3,2,1,0:T(8,128)S(1)}, f32[32,1,32,128]{3,2,1,0:T(8,128)S(1)}, u32[]{:S(2)}, u32[]{:S(2)}) collective-permute-start(f32[32,1,32,128]{3,2,1,0:T(8,128)S(1)} %get-tuple-element.33), channel_id=1, source_target_pairs={{0,2},{2,4},{4,6},{6,8},{8,10},{10,12},{12,14},{14,16},{16,18},{18... | collective-permute-start | bytes 1572872 | tf_op jit(solution)/shard_map/ppermute | solution.py:373
  32.7 3.5 %collective-permute-start.6 = (f32[32,1,32,128]{3,2,1,0:T(8,128)S(1)}, f32[32,1,32,128]{3,2,1,0:T(8,128)S(1)}, u32[]{:S(2)}, u32[]{:S(2)}) collective-permute-start(f32[32,1,32,128]{3,2,1,0:T(8,128)S(1)} %get-tuple-element.34), channel_id=1, source_target_pairs={{2,0},{4,2},{6,4},{8,6},{10,8},{12,10},{14,12},{16,14},{18,16},{20... | collective-permute-start | bytes 1572872 | tf_op jit(solution)/shard_map/ppermute | solution.py:373
  36.2 0.3 collective-permute-start.2
  36.6 7.2 %kernel_grad.2.refs_4_ = f32[1,288,128]{2,1,0:T(8,128)S(1)} custom-call(f32[32,4,32,128]{3,2,1,0:T(8,128)S(1)} %copy-done, f32[32,1,32,128]{3,2,1,0:T(8,128)S(1)} %collective-permute-done.refs_1_, f32[32,1,32,128]{3,2,1,0:T(8,128)S(1)} %collective-permute-done.1.refs_2_, f32[32,4,32,128]{3,2,1,0:T(8,128)S(1)} %copy-done.1), custom_call_target="tpu_custom_call" | custom-call | flops 271790912 | bytes 209715 | tf_op jit(solution)/shard_map/kernel_grad/pallas_call | solution.py:229
  43.8 0.0 collective-permute-done.5.refs_1_
  43.8 1.6 %collective-permute-done.6.refs_2_ = f32[32,1,32,128]{3,2,1,0:T(8,128)S(1)} collective-permute-done((f32[32,1,32,128]{3,2,1,0:T(8,128)S(1)}, f32[32,1,32,128]{3,2,1,0:T(8,128)S(1)}, u32[]{:S(2)}, u32[]{:S(2)}) %collective-permute-start.6) | collective-permute-done | bytes 524320 | tf_op jit(solution)/shard_map/ppermute | solution.py:373
  45.4 7.0 %conv.4.refs_4_ = f32[32,4,32,128]{3,2,1,0:T(8,128)S(1)} custom-call(f32[32,4,32,128]{3,2,1,0:T(8,128)S(1)} %copy-done.1, f32[32,1,32,128]{3,2,1,0:T(8,128)S(1)} %collective-permute-done.5.refs_1_, f32[32,1,32,128]{3,2,1,0:T(8,128)S(1)} %collective-permute-done.6.refs_2_, bf16[96,896]{1,0:T(8,128)(2,1)S(1)} %get-tuple-element.35.refs_3_), custom_call_target="tpu_custom_call" | custom-call | flops 271790912 | bytes 209715 | tf_op jit(solution)/shard_map/conv/pallas_call | solution.py:140
  52.5 0.0 collective-permute-done.4.refs_0_.refs_3_
  52.5 1.3 %fusion = (f32[32,1,32,128]{3,2,1,0:T(8,128)S(1)}, f32[32,1,32,128]{3,2,1,0:T(8,128)S(1)}) fusion(f32[32,4,32,128]{3,2,1,0:T(8,128)} %collective-permute-done.4.refs_0_.refs_3_), kind=kLoop, calls=%fused_computation | loop fusion | bytes 2097152 | tf_op jit(solution)/shard_map/slice | solution.py:371
  53.7 8.2 %kernel_grad.3 = f32[2,288,128]{2,1,0:T(8,128)S(1)} custom-call(f32[32,4,32,128]{3,2,1,0:T(8,128)S(1)} %copy-done, f32[32,1,32,128]{3,2,1,0:T(8,128)S(1)} %collective-permute-done.refs_1_, f32[32,1,32,128]{3,2,1,0:T(8,128)S(1)} %collective-permute-done.1.refs_2_, f32[32,4,32,128]{3,2,1,0:T(8,128)} %collective-permute-done.4.refs_0_.refs_3_, ...), custom_call_target="tpu_custom_call" | custom-call | flops 271790912 | bytes 209715 | tf_op jit(solution)/shard_map/kernel_grad/pallas_call | solution.py:229
  61.9 3.2 %collective-permute-start.9 = (f32[2,288,128]{2,1,0:T(8,128)S(1)}, f32[2,288,128]{2,1,0:T(8,128)S(1)}, u32[]{:S(2)}, u32[]{:S(2)}) collective-permute-start(f32[2,288,128]{2,1,0:T(8,128)S(1)} %kernel_grad.3), channel_id=1, source_target_pairs={{0,2},{2,0},{4,6},{6,4},{8,10},{10,8},{12,14},{14,12},{16,18},{18,... | collective-permute-start | bytes 884744 | tf_op jit(solution)/shard_map/ppermute | solution.py:386
  65.1 1.2 %collective-permute-done.9 = f32[2,288,128]{2,1,0:T(8,128)S(1)} collective-permute-done((f32[2,288,128]{2,1,0:T(8,128)S(1)}, f32[2,288,128]{2,1,0:T(8,128)S(1)}, u32[]{:S(2)}, u32[]{:S(2)}) %collective-permute-start.9) | collective-permute-done | bytes 294944 | tf_op jit(solution)/shard_map/ppermute | solution.py:386
  66.3 0.1 collective-permute-start.10
  66.4 8.2 %collective-permute-done.10 = f32[2,288,128]{2,1,0:T(8,128)S(1)} collective-permute-done((f32[2,288,128]{2,1,0:T(8,128)S(1)}, f32[2,288,128]{2,1,0:T(8,128)S(1)}, u32[]{:S(2)}, u32[]{:S(2)}) %collective-permute-start.10) | collective-permute-done | bytes 294944 | tf_op jit(solution)/shard_map/ppermute | solution.py:386
  74.7 0.2 collective-permute-start.11
  74.9 3.9 %collective-permute-start.7 = (f32[32,1,32,128]{3,2,1,0:T(8,128)S(1)}, f32[32,1,32,128]{3,2,1,0:T(8,128)S(1)}, u32[]{:S(2)}, u32[]{:S(2)}) collective-permute-start(f32[32,1,32,128]{3,2,1,0:T(8,128)S(1)} %get-tuple-element.38), channel_id=1, source_target_pairs={{0,2},{2,4},{4,6},{6,8},{8,10},{10,12},{12,14},{14,16},{16,18},{18... | collective-permute-start | bytes 1572872 | tf_op jit(solution)/shard_map/ppermute | solution.py:373
  78.8 1.9 %collective-permute-start.8 = (f32[32,1,32,128]{3,2,1,0:T(8,128)S(1)}, f32[32,1,32,128]{3,2,1,0:T(8,128)S(1)}, u32[]{:S(2)}, u32[]{:S(2)}) collective-permute-start(f32[32,1,32,128]{3,2,1,0:T(8,128)S(1)} %get-tuple-element.39), channel_id=1, source_target_pairs={{2,0},{4,2},{6,4},{8,6},{10,8},{12,10},{14,12},{16,14},{18,16},{20... | collective-permute-start | bytes 1572872 | tf_op jit(solution)/shard_map/ppermute | solution.py:373
  80.7 0.4 collective-permute-start.3
  81.1 0.9 collective-permute-done.11
  82.1 1.4 %collective-permute-start.12 = (f32[2,288,128]{2,1,0:T(8,128)S(1)}, f32[2,288,128]{2,1,0:T(8,128)S(1)}, u32[]{:S(2)}, u32[]{:S(2)}) collective-permute-start(f32[2,288,128]{2,1,0:T(8,128)S(1)} %add.11.mine_ref), channel_id=1, source_target_pairs={{0,16},{2,18},{4,20},{6,22},{8,24},{10,26},{12,28},{14,30},{16,0},... | collective-permute-start | bytes 884744 | tf_op jit(solution)/shard_map/ppermute | solution.py:386
  83.4 1.5 %collective-permute-done.7.refs_1_ = f32[32,1,32,128]{3,2,1,0:T(8,128)S(1)} collective-permute-done((f32[32,1,32,128]{3,2,1,0:T(8,128)S(1)}, f32[32,1,32,128]{3,2,1,0:T(8,128)S(1)}, u32[]{:S(2)}, u32[]{:S(2)}) %collective-permute-start.7) | collective-permute-done | bytes 524320 | tf_op jit(solution)/shard_map/ppermute | solution.py:373
  85.0 14.7 %collective-permute-done.8.refs_2_ = f32[32,1,32,128]{3,2,1,0:T(8,128)S(1)} collective-permute-done((f32[32,1,32,128]{3,2,1,0:T(8,128)S(1)}, f32[32,1,32,128]{3,2,1,0:T(8,128)S(1)}, u32[]{:S(2)}, u32[]{:S(2)}) %collective-permute-start.8) | collective-permute-done | bytes 524320 | tf_op jit(solution)/shard_map/ppermute | solution.py:373
  99.7 9.4 %conv.5 = f32[32,4,32,128]{3,2,1,0:T(8,128)} custom-call(f32[32,4,32,128]{3,2,1,0:T(8,128)} %collective-permute-done.4.refs_0_.refs_3_, f32[32,1,32,128]{3,2,1,0:T(8,128)S(1)} %collective-permute-done.7.refs_1_, f32[32,1,32,128]{3,2,1,0:T(8,128)S(1)} %collective-permute-done.8.refs_2_, bf16[96,896]{1,0:T(8,128)(2,1)S(1)} %get-tuple-element.40.refs_3_, ...), custom_call_target="tpu_custom_call" | custom-call | flops 271790912 | bytes 209715 | tf_op jit(solution)/shard_map/conv/pallas_call | solution.py:140
  109.1 0.0 collective-permute-done.3.piece
  109.1 0.0 collective-permute-done.2.piece
  109.1 3.4 %add_into.2.base = f32[32,4,32,128]{3,2,1,0:T(8,128)} custom-call(f32[32,4,32,128]{3,2,1,0:T(8,128)} %get-tuple-element.28.base, f32[24,4,32,128]{3,2,1,0:T(8,128)S(1)} %collective-permute-done.2.piece), custom_call_target="tpu_custom_call", output_to_operand_aliasing={{}: (0, {})} | custom-call | flops 393216 | bytes 4718592 | tf_op jit(solution)/shard_map/add_into/pallas_call | solution.py:351
  112.5 1.9 %add_into.3 = f32[32,4,32,128]{3,2,1,0:T(8,128)} custom-call(f32[32,4,32,128]{3,2,1,0:T(8,128)} %add_into.2.base, f32[8,4,32,128]{3,2,1,0:T(8,128)S(1)} %collective-permute-done.3.piece), custom_call_target="tpu_custom_call", output_to_operand_aliasing={{}: (0, {})} | custom-call | flops 131072 | bytes 1572864 | tf_op jit(solution)/shard_map/add_into/pallas_call | solution.py:351
  114.4 0.0 collective-permute-done.12.other_ref
  114.4 1.0 finish.1
  (3 shorter events, 0.1 us)
Async XLA Ops:
  0.6 19.2 %copy-start = (f32[32,4,32,128]{3,2,1,0:T(8,128)S(1)}, f32[32,4,32,128]{3,2,1,0:T(8,128)}, u32[]{:S(2)}) copy-start(f32[32,4,32,128]{3,2,1,0:T(8,128)} %refs_0_.3) | copy-start | bytes 6291460
  0.6 51.8 %collective-permute-start.4 = (f32[32,4,32,128]{3,2,1,0:T(8,128)}, f32[32,4,32,128]{3,2,1,0:T(8,128)}, u32[]{:S(2)}, u32[]{:S(2)}) collective-permute-start(f32[32,4,32,128]{3,2,1,0:T(8,128)} %refs_3_), channel_id=1, source_target_pairs={{1,0},{0,1},{3,2},{2,3},{5,4},{4,5},{7,6},{6,7},{9,8},{8,9},{11,10... | collective-permute-start | bytes 6291464 | tf_op jit(solution)/shard_map/ppermute | solution.py:403
  4.2 10.4 %collective-permute-start = (f32[32,1,32,128]{3,2,1,0:T(8,128)}, f32[32,1,32,128]{3,2,1,0:T(8,128)S(1)}, u32[]{:S(2)}, u32[]{:S(2)}) collective-permute-start(f32[32,1,32,128]{3,2,1,0:T(8,128)} %get-tuple-element.25), channel_id=1, source_target_pairs={{0,2},{2,4},{4,6},{6,8},{8,10},{10,12},{12,14},{14,16},{16,18},{18... | collective-permute-start | bytes 1572872 | tf_op jit(solution)/shard_map/ppermute | solution.py:373
  8.1 11.7 %collective-permute-start.1 = (f32[32,1,32,128]{3,2,1,0:T(8,128)}, f32[32,1,32,128]{3,2,1,0:T(8,128)S(1)}, u32[]{:S(2)}, u32[]{:S(2)}) collective-permute-start(f32[32,1,32,128]{3,2,1,0:T(8,128)} %get-tuple-element.26), channel_id=1, source_target_pairs={{2,0},{4,2},{6,4},{8,6},{10,8},{12,10},{14,12},{16,14},{18,16},{20... | collective-permute-start | bytes 1572872 | tf_op jit(solution)/shard_map/ppermute | solution.py:373
  10.1 20.7 %copy-start.1 = (f32[32,4,32,128]{3,2,1,0:T(8,128)S(1)}, f32[32,4,32,128]{3,2,1,0:T(8,128)}, u32[]{:S(2)}) copy-start(f32[32,4,32,128]{3,2,1,0:T(8,128)} %refs_3_) | copy-start | bytes 6291460
  10.1 1.2 %copy-start.2 = (f32[64,27,32]{0,2,1:T(8,128)S(1)}, f32[64,27,32]{0,2,1:T(8,128)}, u32[]{:S(2)}) copy-start(f32[64,27,32]{0,2,1:T(8,128)} %param.4) | copy-start | bytes 663556
  30.8 13.0 %collective-permute-start.5 = (f32[32,1,32,128]{3,2,1,0:T(8,128)S(1)}, f32[32,1,32,128]{3,2,1,0:T(8,128)S(1)}, u32[]{:S(2)}, u32[]{:S(2)}) collective-permute-start(f32[32,1,32,128]{3,2,1,0:T(8,128)S(1)} %get-tuple-element.33), channel_id=1, source_target_pairs={{0,2},{2,4},{4,6},{6,8},{8,10},{10,12},{12,14},{14,16},{16,18},{18... | collective-permute-start | bytes 1572872 | tf_op jit(solution)/shard_map/ppermute | solution.py:373
  32.7 12.7 %collective-permute-start.6 = (f32[32,1,32,128]{3,2,1,0:T(8,128)S(1)}, f32[32,1,32,128]{3,2,1,0:T(8,128)S(1)}, u32[]{:S(2)}, u32[]{:S(2)}) collective-permute-start(f32[32,1,32,128]{3,2,1,0:T(8,128)S(1)} %get-tuple-element.34), channel_id=1, source_target_pairs={{2,0},{4,2},{6,4},{8,6},{10,8},{12,10},{14,12},{16,14},{18,16},{20... | collective-permute-start | bytes 1572872 | tf_op jit(solution)/shard_map/ppermute | solution.py:373
  36.2 72.8 %collective-permute-start.2 = (f32[24,4,32,128]{3,2,1,0:T(8,128)S(1)}, f32[24,4,32,128]{3,2,1,0:T(8,128)S(1)}, u32[]{:S(2)}, u32[]{:S(2)}) collective-permute-start(f32[24,4,32,128]{3,2,1,0:T(8,128)S(1)} %get-tuple-element.29), channel_id=1, source_target_pairs={{0,1},{1,0},{2,3},{3,2},{4,5},{5,4},{6,7},{7,6},{8,9},{9,8},{10,11... | collective-permute-start | bytes 4718600 | tf_op jit(solution)/shard_map/ppermute | solution.py:415
  61.9 4.4 %collective-permute-start.9 = (f32[2,288,128]{2,1,0:T(8,128)S(1)}, f32[2,288,128]{2,1,0:T(8,128)S(1)}, u32[]{:S(2)}, u32[]{:S(2)}) collective-permute-start(f32[2,288,128]{2,1,0:T(8,128)S(1)} %kernel_grad.3), channel_id=1, source_target_pairs={{0,2},{2,0},{4,6},{6,4},{8,10},{10,8},{12,14},{14,12},{16,18},{18,... | collective-permute-start | bytes 884744 | tf_op jit(solution)/shard_map/ppermute | solution.py:386
  66.3 8.3 %collective-permute-start.10 = (f32[2,288,128]{2,1,0:T(8,128)S(1)}, f32[2,288,128]{2,1,0:T(8,128)S(1)}, u32[]{:S(2)}, u32[]{:S(2)}) collective-permute-start(f32[2,288,128]{2,1,0:T(8,128)S(1)} %add.9), channel_id=1, source_target_pairs={{0,4},{2,6},{4,0},{6,2},{8,12},{10,14},{12,8},{14,10},{16,20},{18,... | collective-permute-start | bytes 884744 | tf_op jit(solution)/shard_map/ppermute | solution.py:386
  74.7 7.4 %collective-permute-start.11 = (f32[2,288,128]{2,1,0:T(8,128)S(1)}, f32[2,288,128]{2,1,0:T(8,128)S(1)}, u32[]{:S(2)}, u32[]{:S(2)}) collective-permute-start(f32[2,288,128]{2,1,0:T(8,128)S(1)} %add.10), channel_id=1, source_target_pairs={{0,8},{2,10},{4,12},{6,14},{8,0},{10,2},{12,4},{14,6},{16,24},{18,... | collective-permute-start | bytes 884744 | tf_op jit(solution)/shard_map/ppermute | solution.py:386
  74.9 10.1 %collective-permute-start.7 = (f32[32,1,32,128]{3,2,1,0:T(8,128)S(1)}, f32[32,1,32,128]{3,2,1,0:T(8,128)S(1)}, u32[]{:S(2)}, u32[]{:S(2)}) collective-permute-start(f32[32,1,32,128]{3,2,1,0:T(8,128)S(1)} %get-tuple-element.38), channel_id=1, source_target_pairs={{0,2},{2,4},{4,6},{6,8},{8,10},{10,12},{12,14},{14,16},{16,18},{18... | collective-permute-start | bytes 1572872 | tf_op jit(solution)/shard_map/ppermute | solution.py:373
  78.8 20.9 %collective-permute-start.8 = (f32[32,1,32,128]{3,2,1,0:T(8,128)S(1)}, f32[32,1,32,128]{3,2,1,0:T(8,128)S(1)}, u32[]{:S(2)}, u32[]{:S(2)}) collective-permute-start(f32[32,1,32,128]{3,2,1,0:T(8,128)S(1)} %get-tuple-element.39), channel_id=1, source_target_pairs={{2,0},{4,2},{6,4},{8,6},{10,8},{12,10},{14,12},{16,14},{18,16},{20... | collective-permute-start | bytes 1572872 | tf_op jit(solution)/shard_map/ppermute | solution.py:373
  80.7 28.3 %collective-permute-start.3 = (f32[8,4,32,128]{3,2,1,0:T(8,128)S(1)}, f32[8,4,32,128]{3,2,1,0:T(8,128)S(1)}, u32[]{:S(2)}, u32[]{:S(2)}) collective-permute-start(f32[8,4,32,128]{3,2,1,0:T(8,128)S(1)} %get-tuple-element.30), channel_id=1, source_target_pairs={{0,1},{1,0},{2,3},{3,2},{4,5},{5,4},{6,7},{7,6},{8,9},{9,8},{10,11... | collective-permute-start | bytes 1572872 | tf_op jit(solution)/shard_map/ppermute | solution.py:415
  82.1 32.3 %collective-permute-start.12 = (f32[2,288,128]{2,1,0:T(8,128)S(1)}, f32[2,288,128]{2,1,0:T(8,128)S(1)}, u32[]{:S(2)}, u32[]{:S(2)}) collective-permute-start(f32[2,288,128]{2,1,0:T(8,128)S(1)} %add.11.mine_ref), channel_id=1, source_target_pairs={{0,16},{2,18},{4,20},{6,22},{8,24},{10,26},{12,28},{14,30},{16,0},... | collective-permute-start | bytes 884744 | tf_op jit(solution)/shard_map/ppermute | solution.py:386

commit v3 on v2

--- a/solution.py
+++ b/solution.py
@@ -11,6 +11,7 @@
 F32 = jnp.float32
 BF16 = jnp.bfloat16
 ROWS = 8
+VMEM_LIMIT = 16 << 20
 WHOLE = pl.BlockSpec(memory_space=pltpu.VMEM)
 SCALAR = pl.BlockSpec(memory_space=pltpu.SMEM)
 
@@ -26,7 +27,7 @@
 
 def params(steps=1):
     return pltpu.CompilerParams(
-        dimension_semantics=("arbitrary",) * steps or None, vmem_limit_bytes=32 << 20
+        dimension_semantics=("arbitrary",) * steps or None, vmem_limit_bytes=VMEM_LIMIT
     )
 
 
@@ -51,34 +52,31 @@
     lax.fori_loop(0, height // ROWS, one_block, 0, unroll=True)
 
 
-def fill_field(dst_hi, dst_lo, field, below, above, chans, padded, planes, height):
-    fill_plane(dst_hi, dst_lo, 0, lambda s: below[:, 0, s, :], chans, padded, height)
-    fill_plane(dst_hi, dst_lo, planes + 1, lambda s: above[:, 0, s, :], chans, padded, height)
-
-    def one_plane(d, carry):
-        fill_plane(dst_hi, dst_lo, d + 1, lambda s: field[:, d, s, :], chans, padded, height)
-        return carry
-
-    lax.fori_loop(0, planes, one_plane, 0)
-
-
 def conv_kernel(dims, sizes, unroll, has_acc, *refs):
     chans, padded, planes, height = dims
-    field, below, above, weight = refs[:4]
-    refs = refs[4:]
+    field, sibling, neighbour, weight, bit = refs[:5]
+    refs = refs[5:]
     acc = None
     if has_acc:
         acc, refs = refs[0], refs[1:]
     results = refs[: len(sizes)]
     xh, xl = refs[len(sizes) :]
-    d = pl.program_id(0)
+    step = pl.program_id(0)
+    d = step - 1
     width = field.shape[-1]
     rows_out = sum(sizes)
     span = 3 * padded
 
-    @pl.when(d == 0)
+    @pl.when(step == 0)
     def _():
-        fill_field(xh, xl, field, below, above, chans, padded, planes, height)
+        for ref, side in ((sibling, 1 - bit[0]), (neighbour, bit[0])):
+            fill_plane(
+                xh, xl, side * (planes + 1), lambda s, r=ref: r[:, 0, s, :], chans, padded, height
+            )
+
+    @pl.when(step < planes)
+    def _():
+        fill_plane(xh, xl, step + 1, lambda s: field[:, 0, s, :], chans, padded, height)
 
     lane = lax.broadcasted_iota(jnp.int32, (rows_out, width), 1)
     first = lane == 0
@@ -121,33 +119,43 @@
             start += size
         return carry
 
-    lax.fori_loop(0, height // ROWS, one_block, 0, unroll=unroll)
-
-
-def conv(field, below, above, weight, sizes, unroll, acc=None):
+    @pl.when(step > 0)
+    def _():
+        lax.fori_loop(0, height // ROWS, one_block, 0, unroll=unroll)
+
+
+def conv(field, halo, weight, bit, sizes, unroll, acc=None, keep=False):
     chans, planes, height, width = field.shape
     padded = up_to(chans, 16)
 
     def plane_spec(size):
-        return pl.BlockSpec((size, 1, height, width), lambda d: (0, d, 0, 0))
-
-    args = [field, below, above, weight]
-    in_specs = [WHOLE] * 4
+        return pl.BlockSpec(
+            (size, 1, height, width), lambda d: (0, jnp.maximum(d - 1, 0), 0, 0)
+        )
+
+    args = [field, *halo, weight, bit]
+    in_specs = [
+        pl.BlockSpec(
+            (chans, 1, height, width), lambda d: (0, jnp.minimum(d, planes - 1), 0, 0)
+        )
+    ]
+    in_specs += [WHOLE] * 3 + [SCALAR]
     if acc is not None:
         args.append(acc)
         in_specs.append(plane_spec(sizes[0]))
     cells = planes * height * width
+    held = (planes + 2, (height + 2) * padded, width)
+    count = 2 if keep else 0
     return pl.pallas_call(
         functools.partial(
             conv_kernel, (chans, padded, planes, height), sizes, unroll, acc is not None
         ),
-        grid=(planes,),
+        grid=(planes + 1,),
         in_specs=in_specs,
-        out_specs=[plane_spec(size) for size in sizes],
-        out_shape=[jax.ShapeDtypeStruct((size, planes, height, width), F32) for size in sizes],
-        scratch_shapes=[
-            pltpu.VMEM((planes + 2, (height + 2) * padded, width), BF16) for _ in range(2)
-        ],
+        out_specs=[plane_spec(size) for size in sizes] + [WHOLE] * count,
+        out_shape=[jax.ShapeDtypeStruct((size, planes, height, width), F32) for size in sizes]
+        + [jax.ShapeDtypeStruct(held, BF16)] * count,
+        scratch_shapes=[pltpu.VMEM(held, BF16)] * (2 - count),
         compiler_params=params(),
         cost_estimate=pl.CostEstimate(
             flops=6 * 27 * chans * sum(sizes) * cells * 2 // 20,
@@ -159,12 +167,11 @@
 
 
 def grad_kernel(dims, others, *refs):
-    chans, padded, planes, height = dims
-    field, below, above, cot = refs[:4]
+    padded, planes, height, width = dims
+    xh, xl, cot, bit = refs[:4]
     done = refs[4 : 4 + others]
-    out, xh, xl, total = refs[4 + others :]
+    *outs_refs, total = refs[4 + others :]
     outs = cot.shape[0]
-    width = field.shape[-1]
     step = pl.program_id(0)
     span = 3 * padded
     half = 3 * span
@@ -172,7 +179,6 @@
 
     @pl.when(step == 0)
     def _():
-        fill_field(xh, xl, field, below, above, chans, padded, planes, height)
         total[...] = jnp.zeros_like(total)
 
     lane = lax.broadcasted_iota(jnp.int32, (outs, width), 1)
@@ -214,38 +220,46 @@
 
     @pl.when(step == planes - 1)
     def _():
-        for index, ref in enumerate(done):
-            out[index] = ref[0]
-        out[others] = total[:half, :group] + total[:half, group:] + total[half:, :group]
-
-
-def kernel_grad(field, below, above, cot, done=()):
-    chans, planes, height, width = field.shape
-    outs = cot.shape[0]
-    padded = up_to(chans, 16)
+        summed = total[:half, :group] + total[:half, group:] + total[half:, :group]
+        if len(outs_refs) == 1:
+            outs_refs[0][...] = summed
+        else:
+            total[:half, :group] = summed
+            rows = half // 2
+            kept = pl.multiple_of(bit[0] * rows, 8)
+            sent = pl.multiple_of((1 - bit[0]) * rows, 8)
+            for ref, start in zip(outs_refs, (kept, sent)):
+                for index, other in enumerate(done):
+                    ref[index] = other[pl.ds(start, rows), :]
+                ref[others] = total[pl.ds(start, rows), :group]
+
+
+def kernel_grad(xh, xl, cot, bit, done=None):
+    outs, planes, height, width = cot.shape
+    padded = xh.shape[1] // (height + 2)
     group = up_to(3 * outs, 128)
     cells = planes * height * width
-    count = len(done) + 1
+    rows = 9 * padded
+    earlier = () if done is None else tuple(done)
+    shape = (rows, group) if done is None else (len(earlier) + 1, rows // 2, group)
+    shapes = [jax.ShapeDtypeStruct(shape, F32)] * (1 if done is None else 2)
     return pl.pallas_call(
-        functools.partial(grad_kernel, (chans, padded, planes, height), len(done)),
+        functools.partial(grad_kernel, (padded, planes, height, width), len(earlier)),
         grid=(planes,),
-        in_specs=[WHOLE] * 3
-        + [pl.BlockSpec((outs, 1, height, width), lambda d: (0, d, 0, 0))]
-        + [WHOLE] * len(done),
-        out_specs=pl.BlockSpec((count, 9 * padded, group), lambda d: (0, 0, 0)),
-        out_shape=jax.ShapeDtypeStruct((count, 9 * padded, group), F32),
-        scratch_shapes=[
-            pltpu.VMEM((planes + 2, (height + 2) * padded, width), BF16) for _ in range(2)
-        ]
-        + [pltpu.VMEM((18 * padded, 2 * group), F32)],
+        in_specs=[WHOLE] * 2
+        + [pl.BlockSpec((outs, 1, height, width), lambda d: (0, d, 0, 0)), SCALAR]
+        + [WHOLE] * len(earlier),
+        out_specs=[WHOLE] * len(shapes),
+        out_shape=shapes,
+        scratch_shapes=[pltpu.VMEM((2 * rows, 2 * group), F32)],
         compiler_params=params(),
         cost_estimate=pl.CostEstimate(
-            flops=6 * 27 * chans * outs * cells * 2 // 20,
-            bytes_accessed=4 * (chans + outs) * cells // 20,
+            flops=6 * 3 * rows * outs * cells * 2 // 20,
+            bytes_accessed=8 * outs * cells // 20,
             transcendentals=0,
         ),
         name="kernel_grad",
-    )(field, below, above, cot, *done)
+    )(xh, xl, cot, bit, *earlier)
 
 
 def three_parts(matrix, wide):
@@ -311,11 +325,15 @@
     )(me, taps)
 
 
-def finish_kernel(groups, scale, me, mine_ref, other_ref, out):
+def finish_kernel(groups, scale, me, bit, mine_ref, other_ref, out):
     cin, channels = out.shape[1:]
     mine = channels // groups
-    padded = mine_ref.shape[1] // 9
-    totals = [(mine_ref[s] + other_ref[s]) * scale for s in range(groups)]
+    padded = 2 * mine_ref.shape[1] // 9
+    low = bit[0] == 0
+    totals = []
+    for s in range(groups):
+        a, b = mine_ref[s] * scale, other_ref[s] * scale
+        totals.append(jnp.concatenate([jnp.where(low, a, b), jnp.where(low, b, a)], axis=0))
     for k in range(3):
         pieces = [t[:, k * mine : (k + 1) * mine] for t in totals]
         blocks = []
@@ -330,15 +348,15 @@
             out[3 * tap + k] = wide[tap * padded : tap * padded + cin]
 
 
-def finish(me, value, other, groups, cin, channels, scale):
+def finish(me, bit, value, other, groups, cin, channels, scale):
     return pl.pallas_call(
         functools.partial(finish_kernel, groups, scale),
-        in_specs=[SCALAR, WHOLE, WHOLE],
+        in_specs=[SCALAR, SCALAR, WHOLE, WHOLE],
         out_specs=WHOLE,
         out_shape=jax.ShapeDtypeStruct((27, cin, channels), F32),
         compiler_params=params(0),
         name="finish",
-    )(me, value, other)
+    )(me, bit, value, other)
 
 
 def add_kernel(base, piece, out):
@@ -363,50 +381,53 @@
     )(base, piece)
 
 
-def slab_halo(field):
+def cut_edges(field, bit):
+    ends = field.shape[1] - 1
+    to_sibling = lax.dynamic_slice_in_dim(field, (1 - bit[0]) * ends, 1, axis=1)
+    to_neighbour = lax.dynamic_slice_in_dim(field, bit[0] * ends, 1, axis=1)
+    return lax.optimization_barrier((field, to_sibling, to_neighbour))
+
+
+def slab_halo(to_sibling, to_neighbour):
     count = lax.axis_size("slab")
-    planes = field.shape[1]
-    up = [(i, i + 1) for i in range(count - 1)]
-    down = [(i + 1, i) for i in range(count - 1)]
-    top, bottom = field[:, planes - 1 :], field[:, :1]
-    field, top, bottom = lax.optimization_barrier((field, top, bottom))
-    return field, (lax.ppermute(top, "slab", up), lax.ppermute(bottom, "slab", down))
-
-
-def slab_sum(value):
-    count = lax.axis_size("slab")
-    if count & (count - 1):
-        value = lax.psum(value, "slab")
-        return value, jnp.zeros_like(value)
-    bit = 1
-    other = jnp.zeros_like(value) if count == 1 else None
-    while bit < count:
-        if other is not None:
-            value = value + other
-        other = lax.ppermute(value, "slab", [(i, i ^ bit) for i in range(count)])
-        bit *= 2
-    return value, other
+    across = [(i, i + 1) for i in range(1, count - 1, 2)]
+    across += [(j, i) for i, j in across]
+    return slab_swap(to_sibling, 1), lax.ppermute(to_neighbour, "slab", across)
+
+
+def slab_swap(value, bit):
+    return lax.ppermute(
+        value, "slab", [(i, i ^ bit) for i in range(lax.axis_size("slab"))]
+    )
 
 
 def per_device(activations, kernel, cotangent):
     groups = lax.axis_size("chan")
+    slabs = lax.axis_size("slab")
+    assert slabs >= 4 and slabs & (slabs - 1) == 0 and groups > 1
     me = lax.axis_index("chan").reshape(1)
+    bit = lax.rem(lax.axis_index("slab"), 2).reshape(1)
     channels, taps, cin = kernel.shape
     mine = channels // groups
     planes, height, width = activations.shape[1:]
     tail = max(mine // 4, 1)
     pieces = (mine - tail, tail)
+    after = lax.optimization_barrier
 
     cots = [cotangent]
     for s in range(1, groups):
         cots.append(
             lax.ppermute(cotangent, "chan", [((i + s) % groups, i) for i in range(groups)])
         )
-    activations, act_halo = slab_halo(activations)
+    activations, *edges = cut_edges(activations, bit)
+    own, *edges = after((cotangent, *edges))
+    act_halo = slab_halo(*edges)
+    own, *edges = cut_edges(own, bit)
+    cot_halo = slab_halo(*edges)
     forward, *backward = weight_matrices(me, kernel.transpose(1, 2, 0), groups)
 
-    features, *partial = conv(
-        activations, *act_halo, forward, (mine,) + pieces * (groups - 1), 2
+    features, *partial, xh, xl = conv(
+        activations, act_halo, forward, bit, (mine,) + pieces * (groups - 1), 2, keep=True
     )
     received = []
     for s in range(1, groups):
@@ -415,25 +436,41 @@
                 lax.ppermute(part, "chan", [(i, (i + s) % groups) for i in range(groups)])
             )
 
-    own, _ = lax.optimization_barrier((cotangent, partial[0]))
-    own, cot_halo = slab_halo(own)
-    grads = [kernel_grad(activations, *act_halo, own)]
-    (input_grad,) = conv(own, *cot_halo, backward[0], (cin,), 4)
+    grads = list(kernel_grad(xh, xl, own, bit))
+    (input_grad,) = conv(own, cot_halo, backward[0], bit, (cin,), 4)
     for s in range(1, groups):
-        cots[s], input_grad = lax.optimization_barrier((cots[s], input_grad))
-        cots[s], halo = slab_halo(cots[s])
-        done = grads if s == groups - 1 else ()
-        grads.append(kernel_grad(activations, *act_halo, cots[s], done))
-        (input_grad,) = conv(cots[s], *halo, backward[s], (cin,), 4, input_grad)
-
-    cells_all = planes * lax.axis_size("slab") * height * width
-    value, other = slab_sum(grads[-1])
-    weight_grad = finish(me, value, other, groups, cin, channels, 1.0 / math.sqrt(cells_all))
-
-    *received, input_grad = lax.optimization_barrier((*received, input_grad))
-    for index, part in enumerate(received):
-        first = 0 if index % 2 == 0 else pieces[0]
-        features = add_into(features, part, first, tail)
+        cot, input_grad, *grads = after((cots[s], input_grad, *grads))
+        cot, *edges = cut_edges(cot, bit)
+        halo = slab_halo(*edges)
+        if s < groups - 1:
+            grads += kernel_grad(xh, xl, cot, bit)
+        else:
+            kept, sent = kernel_grad(xh, xl, cot, bit, grads)
+            kept, sent, *halo = after((kept, sent, *halo))
+            value = kept + slab_swap(sent, 1)
+            value, cot = after((value, cot))
+            other = slab_swap(value, 2)
+        (input_grad,) = conv(cot, halo, backward[s], bit, (cin,), 4, input_grad)
+
+    other, input_grad = after((other, input_grad))
+    value = value + other
+    step = 4
+    while step < slabs // 2:
+        value = value + slab_swap(value, step)
+        step *= 2
+    first_parts, last_part = received[:-1], received[-1]
+    *first_parts, value = after((*first_parts, value))
+    other = slab_swap(value, step)
+    for index, part in enumerate(first_parts):
+        features = add_into(features, part, 0 if index % 2 == 0 else pieces[0], tail)
+    other, features = after((other, features))
+    value = value + other
+    cells_all = planes * slabs * height * width
+    weight_grad = finish(
+        me, bit, value, slab_swap(value, 1), groups, cin, channels, 1.0 / math.sqrt(cells_all)
+    )
+    weight_grad, features, last_part = after((weight_grad, features, last_part))
+    features = add_into(features, last_part, pieces[0], tail)
     return features, input_grad, weight_grad.transpose(2, 0, 1)
 
 

time: 116 us -> 104 us (0.90)
  the two profiles are of different devices: /device:TPU:13 before, /device:TPU:0 now
where the time goes in v3:
time: 104 us; the launch traced here: 103 us
  Pallas kernels  48.1 us (46%)
  starting transfers between devices  32 us (31%)
  waiting for transfers between devices  16.2 us (16%)
  local copies, waits for them, and re-layouts  6.3 us (6%)
    pallas_call x3, Pallas kernels, conv(): pl.pallas_call(functools.partial(conv_kernel, (chans, padded, planes, hei...  27.8 us
    ppermute x8, starting transfers between devices, slab_swap(): lax.ppermute(value, 'slab', [(i, i ^ bit) for i in range(lax.axis_size('s...  24.1 us
    pallas_call x2, Pallas kernels, kernel_grad(): pl.pallas_call(functools.partial(grad_kernel, (padded, planes, height, wi...  12.6 us
    ppermute x8, waiting for transfers between devices, slab_swap(): lax.ppermute(value, 'slab', [(i, i ^ bit) for i in range(lax.axis_size('s...  8.64 us
    ppermute x1, waiting for transfers between devices, per_device(): lax.ppermute(cotangent, 'chan', [((i + s) % groups, i) for i in range(gro...  7.54 us
    pallas_call x2, Pallas kernels, add_into(): pl.pallas_call(add_kernel, grid=(piece.shape[0] // block,), in_specs=[spe...  5.28 us
    dynamic_slice x3, local copies, waits for them, and re-layouts, cut_edges(): to_neighbour = lax.dynamic_slice_in_dim(field, bit[0] * ends, 1, axis=1)  3.54 us
    ppermute x1, starting transfers between devices, per_device(): lax.ppermute(cotangent, 'chan', [((i + s) % groups, i) for i in range(gro...  3 us
  transfers between devices with their start and end apart: 14, of which 5 were waited for; matrix products, arithmetic and copies ran while one was open for 3% of the time, Pallas kernels for 45%

profile of v3, /device:TPU:0, one launch (start us, length us, event | category | flops | bytes accessed | tf_op | source)
XLA Modules:
  0.0 103.4 jit_solution(3749474358168542571)
XLA Ops:
  0.6 3.0 %collective-permute-start.3 = (f32[32,4,32,128]{3,2,1,0:T(8,128)}, f32[32,4,32,128]{3,2,1,0:T(8,128)S(1)}, u32[]{:S(2)}, u32[]{:S(2)}) collective-permute-start(f32[32,4,32,128]{3,2,1,0:T(8,128)} %refs_2_), channel_id=1, source_target_pairs={{1,0},{0,1},{3,2},{2,3},{5,4},{4,5},{7,6},{6,7},{9,8},{8,9},{11,10... | collective-permute-start | bytes 6291464 | tf_op jit(solution)/shard_map/ppermute | solution.py:420
  3.6 0.0 copy-start
  3.6 2.4 %constant_dynamic-slice_fusion.4 = (f32[32,1,32,128]{3,2,1,0:T(8,128)}, f32[32,1,32,128]{3,2,1,0:T(8,128)}) fusion(f32[32,4,32,128]{3,2,1,0:T(8,128)} %refs_0_, s32[]{:T(128)S(6)} %select_n.5, s32[]{:T(128)S(6)} %select_n.4), kind=kLoop, calls=%fused_computation.4 | loop fusion | bytes 2097160 | tf_op jit(solution)/shard_map/dynamic_slice | solution.py:387
  6.0 0.0 collective-permute-start
  6.0 0.7 collective-permute-start.1
  6.7 0.0 copy-done
  6.7 1.1 %constant_dynamic-slice_fusion.2 = (f32[32,1,32,128]{3,2,1,0:T(8,128)}, f32[32,1,32,128]{3,2,1,0:T(8,128)}) fusion(f32[32,4,32,128]{3,2,1,0:T(8,128)S(1)} %copy-done, s32[]{:T(128)S(6)} %select_n.5, s32[]{:T(128)S(6)} %select_n.4), kind=kLoop, calls=%fused_computation.2 | loop fusion | bytes 2097160 | tf_op jit(solution)/shard_map/dynamic_slice | solution.py:387
  7.8 2.8 %collective-permute-start.4 = (f32[32,1,32,128]{3,2,1,0:T(8,128)}, f32[32,1,32,128]{3,2,1,0:T(8,128)}, u32[]{:S(2)}, u32[]{:S(2)}) collective-permute-start(f32[32,1,32,128]{3,2,1,0:T(8,128)} %get-tuple-element.54), channel_id=1, source_target_pairs={{0,2},{2,0},{4,6},{6,4},{8,10},{10,8},{12,14},{14,12},{16,18},{18,... | collective-permute-start | bytes 1572872 | tf_op jit(solution)/shard_map/ppermute | solution.py:399
  10.7 1.5 %collective-permute-start.5 = (f32[32,1,32,128]{3,2,1,0:T(8,128)}, f32[32,1,32,128]{3,2,1,0:T(8,128)}, u32[]{:S(2)}, u32[]{:S(2)}) collective-permute-start(f32[32,1,32,128]{3,2,1,0:T(8,128)} %get-tuple-element.55), channel_id=1, source_target_pairs={{2,4},{6,8},{10,12},{14,16},{18,20},{22,24},{26,28},{4,2},{8,6},{1... | collective-permute-start | bytes 1572872 | tf_op jit(solution)/shard_map/ppermute | solution.py:395
  12.1 0.0 copy-start.1
  12.1 0.0 copy-start.3
  12.1 1.2 %copy-done.3 = f32[64,27,32]{0,2,1:T(8,128)S(1)} copy-done((f32[64,27,32]{0,2,1:T(8,128)S(1)}, f32[64,27,32]{0,2,1:T(8,128)}, u32[]{:S(2)}) %copy-start.3) | copy-done | bytes 221208
  13.3 1.3 %weights.1 = (bf16[192,896]{1,0:T(8,128)(2,1)S(1)}, bf16[96,896]{1,0:T(8,128)(2,1)S(1)}, bf16[96,896]{1,0:T(8,128)(2,1)S(1)}) custom-call(s32[1]{0:T(128)} %bitcast.me, f32[27,32,64]{2,1,0:T(8,128)S(1)} %bitcast.4), custom_call_target="tpu_custom_call" | custom-call | tf_op jit(solution)/shard_map/weights/pallas_call | solution.py:316
  14.6 0.0 collective-permute-done.refs_1_
  14.6 0.0 collective-permute-done.1.refs_2_
  14.7 0.0 copy-start.2
  14.7 1.6 %copy-done.2 = f32[32,4,32,128]{3,2,1,0:T(8,128)S(1)} copy-done((f32[32,4,32,128]{3,2,1,0:T(8,128)S(1)}, f32[32,4,32,128]{3,2,1,0:T(8,128)}, u32[]{:S(2)}) %copy-start.2) | copy-done | bytes 2097176
  16.2 11.1 %conv.3 = (f32[32,4,32,128]{3,2,1,0:T(8,128)}, f32[24,4,32,128]{3,2,1,0:T(8,128)S(1)}, f32[8,4,32,128]{3,2,1,0:T(8,128)S(1)}, bf16[6,1088,128]{2,1,0:T(8,128)(2,1)S(1)}, bf16[6,1088,128]{2,1,0:T(8,128)(2,1)S(1)}) custom-call(f32[32,4,32,128]{3,2,1,0:T(8,128)S(1)} %copy-done.2, f32[32,1,32,128]{3,2,1,0:T(8,128)S(1)} %collective-permute-done.refs_1_, ...), custom_call_target="tpu_custom_call" | custom-call | flops 543581824 | bytes 314572 | tf_op jit(solution)/shard_map/conv/pallas_call | solution.py:149
  27.3 0.5 collective-permute-start.2
  27.9 0.0 copy-done.1
  27.9 6.3 %kernel_grad.2.refs_4_ = f32[288,128]{1,0:T(8,128)S(1)} custom-call(bf16[6,1088,128]{2,1,0:T(8,128)(2,1)S(1)} %get-tuple-element.50.refs_0_, bf16[6,1088,128]{2,1,0:T(8,128)(2,1)S(1)} %get-tuple-element.51.refs_1_, f32[32,4,32,128]{3,2,1,0:T(8,128)S(1)} %copy-done.1, s32[1]{0:T(128)} %bitcast.1.refs_4_.refs_3_.bit), custom_call_target="tpu_custom_call" | custom-call | flops 271790912 | bytes 209715 | tf_op jit(solution)/shard_map/kernel_grad/pallas_call | solution.py:246
  34.2 0.0 collective-permute-done.4.refs_1_
  34.2 0.0 collective-permute-done.5.refs_2_
  34.2 8.6 %conv.4.refs_5_ = f32[32,4,32,128]{3,2,1,0:T(8,128)S(1)} custom-call(f32[32,4,32,128]{3,2,1,0:T(8,128)S(1)} %copy-done.1, f32[32,1,32,128]{3,2,1,0:T(8,128)} %collective-permute-done.4.refs_1_, f32[32,1,32,128]{3,2,1,0:T(8,128)} %collective-permute-done.5.refs_2_, bf16[96,896]{1,0:T(8,128)(2,1)S(1)} %get-tuple-element.56.refs_3_, s32[1]{0:T(128)} %bitcast.1.refs_4_.refs_3_.bit), custom_call_target="tpu_custom_call" | custom-call | flops 271790912 | bytes 209715 | tf_op jit(solution)/shard_map/conv/pallas_call | solution.py:149
  42.8 7.5 %collective-permute-done.3.refs_2_.refs_0_ = f32[32,4,32,128]{3,2,1,0:T(8,128)S(1)} collective-permute-done((f32[32,4,32,128]{3,2,1,0:T(8,128)}, f32[32,4,32,128]{3,2,1,0:T(8,128)S(1)}, u32[]{:S(2)}, u32[]{:S(2)}) %collective-permute-start.3) | collective-permute-done | bytes 2097184 | tf_op jit(solution)/shard_map/ppermute | solution.py:420
  50.3 0.1 constant_dynamic-slice_fusion
  50.4 4.8 %collective-permute-start.6 = (f32[32,1,32,128]{3,2,1,0:T(8,128)S(1)}, f32[32,1,32,128]{3,2,1,0:T(8,128)S(1)}, u32[]{:S(2)}, u32[]{:S(2)}) collective-permute-start(f32[32,1,32,128]{3,2,1,0:T(8,128)S(1)} %get-tuple-element.62), channel_id=1, source_target_pairs={{0,2},{2,0},{4,6},{6,4},{8,10},{10,8},{12,14},{14,12},{16,18},{18,... | collective-permute-start | bytes 1572872 | tf_op jit(solution)/shard_map/ppermute | solution.py:399
  55.2 0.7 collective-permute-start.7
  55.9 6.3 %kernel_grad.3 = (f32[2,144,128]{2,1,0:T(8,128)S(1)}, f32[2,144,128]{2,1,0:T(8,128)S(1)}) custom-call(bf16[6,1088,128]{2,1,0:T(8,128)(2,1)S(1)} %get-tuple-element.50.refs_0_, bf16[6,1088,128]{2,1,0:T(8,128)(2,1)S(1)} %get-tuple-element.51.refs_1_, f32[32,4,32,128]{3,2,1,0:T(8,128)S(1)} %collective-permute-done.3.refs_2_.refs_0_, ...), custom_call_target="tpu_custom_call" | custom-call | flops 271790912 | bytes 209715 | tf_op jit(solution)/shard_map/kernel_grad/pallas_call | solution.py:246
  62.2 0.0 collective-permute-done.6.refs_1_
  62.2 0.0 collective-permute-done.7.refs_2_
  62.2 9.3 %collective-permute-start.8 = (f32[2,144,128]{2,1,0:T(8,128)S(1)}, f32[2,144,128]{2,1,0:T(8,128)S(1)}, u32[]{:S(2)}, u32[]{:S(2)}) collective-permute-start(f32[2,144,128]{2,1,0:T(8,128)S(1)} %get-tuple-element.65), channel_id=1, source_target_pairs={{0,2},{2,0},{4,6},{6,4},{8,10},{10,8},{12,14},{14,12},{16,18},{18,... | collective-permute-start | bytes 442376 | tf_op jit(solution)/shard_map/ppermute | solution.py:399
  71.5 1.0 collective-permute-done.8
  72.5 2.8 %collective-permute-start.9 = (f32[2,144,128]{2,1,0:T(8,128)S(1)}, f32[2,144,128]{2,1,0:T(8,128)S(1)}, u32[]{:S(2)}, u32[]{:S(2)}) collective-permute-start(f32[2,144,128]{2,1,0:T(8,128)S(1)} %add.24), channel_id=1, source_target_pairs={{0,4},{2,6},{4,0},{6,2},{8,12},{10,14},{12,8},{14,10},{16,20},{18,... | collective-permute-start | bytes 442376 | tf_op jit(solution)/shard_map/ppermute | solution.py:399
  75.3 1.5 %collective-permute-start.13 = (f32[8,4,32,128]{3,2,1,0:T(8,128)S(1)}, f32[8,4,32,128]{3,2,1,0:T(8,128)S(1)}, u32[]{:S(2)}, u32[]{:S(2)}) collective-permute-start(f32[8,4,32,128]{3,2,1,0:T(8,128)S(1)} %get-tuple-element.78), channel_id=1, source_target_pairs={{0,1},{1,0},{2,3},{3,2},{4,5},{5,4},{6,7},{7,6},{8,9},{9,8},{10,11... | collective-permute-start | bytes 1572872 | tf_op jit(solution)/shard_map/ppermute | solution.py:436
  76.8 8.2 %conv.5 = f32[32,4,32,128]{3,2,1,0:T(8,128)} custom-call(f32[32,4,32,128]{3,2,1,0:T(8,128)S(1)} %collective-permute-done.3.refs_2_.refs_0_, f32[32,1,32,128]{3,2,1,0:T(8,128)S(1)} %collective-permute-done.6.refs_1_, f32[32,1,32,128]{3,2,1,0:T(8,128)S(1)} %collective-permute-done.7.refs_2_, bf16[96,896]{1,0:T(8,128)(2,1)S(1)} %get-tuple-element.70.refs_3_, ...), custom_call_target="tpu_custom_call" | custom-call | flops 271790912 | bytes 209715 | tf_op jit(solution)/shard_map/conv/pallas_call | solution.py:149
  85.0 0.0 collective-permute-done.9
  85.0 1.6 %collective-permute-start.10 = (f32[2,144,128]{2,1,0:T(8,128)S(1)}, f32[2,144,128]{2,1,0:T(8,128)S(1)}, u32[]{:S(2)}, u32[]{:S(2)}) collective-permute-start(f32[2,144,128]{2,1,0:T(8,128)S(1)} %add.25), channel_id=1, source_target_pairs={{0,8},{2,10},{4,12},{6,14},{8,0},{10,2},{12,4},{14,6},{16,24},{18,... | collective-permute-start | bytes 442376 | tf_op jit(solution)/shard_map/ppermute | solution.py:399
  86.7 3.8 %collective-permute-done.10 = f32[2,144,128]{2,1,0:T(8,128)S(1)} collective-permute-done((f32[2,144,128]{2,1,0:T(8,128)S(1)}, f32[2,144,128]{2,1,0:T(8,128)S(1)}, u32[]{:S(2)}, u32[]{:S(2)}) %collective-permute-start.10) | collective-permute-done | bytes 147488 | tf_op jit(solution)/shard_map/ppermute | solution.py:399
  90.4 0.0 collective-permute-done.2.piece
  90.5 2.7 %collective-permute-start.11 = (f32[2,144,128]{2,1,0:T(8,128)S(1)}, f32[2,144,128]{2,1,0:T(8,128)S(1)}, u32[]{:S(2)}, u32[]{:S(2)}) collective-permute-start(f32[2,144,128]{2,1,0:T(8,128)S(1)} %add.26), channel_id=1, source_target_pairs={{0,16},{2,18},{4,20},{6,22},{8,24},{10,26},{12,28},{14,30},{16,0},... | collective-permute-start | bytes 442376 | tf_op jit(solution)/shard_map/ppermute | solution.py:399
  93.1 3.4 %add_into.2.base = f32[32,4,32,128]{3,2,1,0:T(8,128)} custom-call(f32[32,4,32,128]{3,2,1,0:T(8,128)} %get-tuple-element.74.base, f32[24,4,32,128]{3,2,1,0:T(8,128)S(1)} %collective-permute-done.2.piece), custom_call_target="tpu_custom_call", output_to_operand_aliasing={{}: (0, {})} | custom-call | flops 393216 | bytes 4718592 | tf_op jit(solution)/shard_map/add_into/pallas_call | solution.py:369
  96.5 2.5 %collective-permute-done.11 = f32[2,144,128]{2,1,0:T(8,128)S(1)} collective-permute-done((f32[2,144,128]{2,1,0:T(8,128)S(1)}, f32[2,144,128]{2,1,0:T(8,128)S(1)}, u32[]{:S(2)}, u32[]{:S(2)}) %collective-permute-start.11) | collective-permute-done | bytes 147488 | tf_op jit(solution)/shard_map/ppermute | solution.py:399
  99.0 0.1 collective-permute-start.12
  99.1 1.4 %collective-permute-done.12.other_ref = f32[2,144,128]{2,1,0:T(8,128)S(1)} collective-permute-done((f32[2,144,128]{2,1,0:T(8,128)S(1)}, f32[2,144,128]{2,1,0:T(8,128)S(1)}, u32[]{:S(2)}, u32[]{:S(2)}) %collective-permute-start.12) | collective-permute-done | bytes 147488 | tf_op jit(solution)/shard_map/ppermute | solution.py:399
  100.5 1.0 finish.1
  101.5 0.0 collective-permute-done.13.piece
  101.5 1.9 %add_into.3 = f32[32,4,32,128]{3,2,1,0:T(8,128)} custom-call(f32[32,4,32,128]{3,2,1,0:T(8,128)} %add_into.2.base, f32[8,4,32,128]{3,2,1,0:T(8,128)S(1)} %collective-permute-done.13.piece), custom_call_target="tpu_custom_call", output_to_operand_aliasing={{}: (0, {})} | custom-call | flops 131072 | bytes 1572864 | tf_op jit(solution)/shard_map/add_into/pallas_call | solution.py:369
  (4 shorter events, 0.1 us)
Async XLA Ops:
  0.6 49.7 %collective-permute-start.3 = (f32[32,4,32,128]{3,2,1,0:T(8,128)}, f32[32,4,32,128]{3,2,1,0:T(8,128)S(1)}, u32[]{:S(2)}, u32[]{:S(2)}) collective-permute-start(f32[32,4,32,128]{3,2,1,0:T(8,128)} %refs_2_), channel_id=1, source_target_pairs={{1,0},{0,1},{3,2},{2,3},{5,4},{4,5},{7,6},{6,7},{9,8},{8,9},{11,10... | collective-permute-start | bytes 6291464 | tf_op jit(solution)/shard_map/ppermute | solution.py:420
  3.6 3.1 %copy-start = (f32[32,4,32,128]{3,2,1,0:T(8,128)S(1)}, f32[32,4,32,128]{3,2,1,0:T(8,128)}, u32[]{:S(2)}) copy-start(f32[32,4,32,128]{3,2,1,0:T(8,128)} %refs_2_) | copy-start | bytes 6291460
  6.0 8.6 %collective-permute-start = (f32[32,1,32,128]{3,2,1,0:T(8,128)}, f32[32,1,32,128]{3,2,1,0:T(8,128)S(1)}, u32[]{:S(2)}, u32[]{:S(2)}) collective-permute-start(f32[32,1,32,128]{3,2,1,0:T(8,128)} %get-tuple-element.46), channel_id=1, source_target_pairs={{0,2},{2,0},{4,6},{6,4},{8,10},{10,8},{12,14},{14,12},{16,18},{18,... | collective-permute-start | bytes 1572872 | tf_op jit(solution)/shard_map/ppermute | solution.py:399
  6.0 8.6 %collective-permute-start.1 = (f32[32,1,32,128]{3,2,1,0:T(8,128)}, f32[32,1,32,128]{3,2,1,0:T(8,128)S(1)}, u32[]{:S(2)}, u32[]{:S(2)}) collective-permute-start(f32[32,1,32,128]{3,2,1,0:T(8,128)} %get-tuple-element.47), channel_id=1, source_target_pairs={{2,4},{6,8},{10,12},{14,16},{18,20},{22,24},{26,28},{4,2},{8,6},{1... | collective-permute-start | bytes 1572872 | tf_op jit(solution)/shard_map/ppermute | solution.py:395
  7.8 26.4 %collective-permute-start.4 = (f32[32,1,32,128]{3,2,1,0:T(8,128)}, f32[32,1,32,128]{3,2,1,0:T(8,128)}, u32[]{:S(2)}, u32[]{:S(2)}) collective-permute-start(f32[32,1,32,128]{3,2,1,0:T(8,128)} %get-tuple-element.54), channel_id=1, source_target_pairs={{0,2},{2,0},{4,6},{6,4},{8,10},{10,8},{12,14},{14,12},{16,18},{18,... | collective-permute-start | bytes 1572872 | tf_op jit(solution)/shard_map/ppermute | solution.py:399
  10.7 23.5 %collective-permute-start.5 = (f32[32,1,32,128]{3,2,1,0:T(8,128)}, f32[32,1,32,128]{3,2,1,0:T(8,128)}, u32[]{:S(2)}, u32[]{:S(2)}) collective-permute-start(f32[32,1,32,128]{3,2,1,0:T(8,128)} %get-tuple-element.55), channel_id=1, source_target_pairs={{2,4},{6,8},{10,12},{14,16},{18,20},{22,24},{26,28},{4,2},{8,6},{1... | collective-permute-start | bytes 1572872 | tf_op jit(solution)/shard_map/ppermute | solution.py:395
  12.1 15.7 %copy-start.1 = (f32[32,4,32,128]{3,2,1,0:T(8,128)S(1)}, f32[32,4,32,128]{3,2,1,0:T(8,128)}, u32[]{:S(2)}) copy-start(f32[32,4,32,128]{3,2,1,0:T(8,128)} %refs_2_) | copy-start | bytes 6291460
  12.1 1.2 %copy-start.3 = (f32[64,27,32]{0,2,1:T(8,128)S(1)}, f32[64,27,32]{0,2,1:T(8,128)}, u32[]{:S(2)}) copy-start(f32[64,27,32]{0,2,1:T(8,128)} %param.4) | copy-start | bytes 663556
  14.7 1.6 %copy-start.2 = (f32[32,4,32,128]{3,2,1,0:T(8,128)S(1)}, f32[32,4,32,128]{3,2,1,0:T(8,128)}, u32[]{:S(2)}) copy-start(f32[32,4,32,128]{3,2,1,0:T(8,128)} %refs_0_) | copy-start | bytes 6291460
  27.3 63.1 %collective-permute-start.2 = (f32[24,4,32,128]{3,2,1,0:T(8,128)S(1)}, f32[24,4,32,128]{3,2,1,0:T(8,128)S(1)}, u32[]{:S(2)}, u32[]{:S(2)}) collective-permute-start(f32[24,4,32,128]{3,2,1,0:T(8,128)S(1)} %get-tuple-element.49), channel_id=1, source_target_pairs={{0,1},{1,0},{2,3},{3,2},{4,5},{5,4},{6,7},{7,6},{8,9},{9,8},{10,11... | collective-permute-start | bytes 4718600 | tf_op jit(solution)/shard_map/ppermute | solution.py:436
  50.4 11.8 %collective-permute-start.6 = (f32[32,1,32,128]{3,2,1,0:T(8,128)S(1)}, f32[32,1,32,128]{3,2,1,0:T(8,128)S(1)}, u32[]{:S(2)}, u32[]{:S(2)}) collective-permute-start(f32[32,1,32,128]{3,2,1,0:T(8,128)S(1)} %get-tuple-element.62), channel_id=1, source_target_pairs={{0,2},{2,0},{4,6},{6,4},{8,10},{10,8},{12,14},{14,12},{16,18},{18,... | collective-permute-start | bytes 1572872 | tf_op jit(solution)/shard_map/ppermute | solution.py:399
  55.2 7.0 %collective-permute-start.7 = (f32[32,1,32,128]{3,2,1,0:T(8,128)S(1)}, f32[32,1,32,128]{3,2,1,0:T(8,128)S(1)}, u32[]{:S(2)}, u32[]{:S(2)}) collective-permute-start(f32[32,1,32,128]{3,2,1,0:T(8,128)S(1)} %get-tuple-element.63), channel_id=1, source_target_pairs={{2,4},{6,8},{10,12},{14,16},{18,20},{22,24},{26,28},{4,2},{8,6},{1... | collective-permute-start | bytes 1572872 | tf_op jit(solution)/shard_map/ppermute | solution.py:395
  62.2 10.3 %collective-permute-start.8 = (f32[2,144,128]{2,1,0:T(8,128)S(1)}, f32[2,144,128]{2,1,0:T(8,128)S(1)}, u32[]{:S(2)}, u32[]{:S(2)}) collective-permute-start(f32[2,144,128]{2,1,0:T(8,128)S(1)} %get-tuple-element.65), channel_id=1, source_target_pairs={{0,2},{2,0},{4,6},{6,4},{8,10},{10,8},{12,14},{14,12},{16,18},{18,... | collective-permute-start | bytes 442376 | tf_op jit(solution)/shard_map/ppermute | solution.py:399
  72.5 12.4 %collective-permute-start.9 = (f32[2,144,128]{2,1,0:T(8,128)S(1)}, f32[2,144,128]{2,1,0:T(8,128)S(1)}, u32[]{:S(2)}, u32[]{:S(2)}) collective-permute-start(f32[2,144,128]{2,1,0:T(8,128)S(1)} %add.24), channel_id=1, source_target_pairs={{0,4},{2,6},{4,0},{6,2},{8,12},{10,14},{12,8},{14,10},{16,20},{18,... | collective-permute-start | bytes 442376 | tf_op jit(solution)/shard_map/ppermute | solution.py:399
  75.3 26.1 %collective-permute-start.13 = (f32[8,4,32,128]{3,2,1,0:T(8,128)S(1)}, f32[8,4,32,128]{3,2,1,0:T(8,128)S(1)}, u32[]{:S(2)}, u32[]{:S(2)}) collective-permute-start(f32[8,4,32,128]{3,2,1,0:T(8,128)S(1)} %get-tuple-element.78), channel_id=1, source_target_pairs={{0,1},{1,0},{2,3},{3,2},{4,5},{5,4},{6,7},{7,6},{8,9},{9,8},{10,11... | collective-permute-start | bytes 1572872 | tf_op jit(solution)/shard_map/ppermute | solution.py:436
  85.0 5.4 %collective-permute-start.10 = (f32[2,144,128]{2,1,0:T(8,128)S(1)}, f32[2,144,128]{2,1,0:T(8,128)S(1)}, u32[]{:S(2)}, u32[]{:S(2)}) collective-permute-start(f32[2,144,128]{2,1,0:T(8,128)S(1)} %add.25), channel_id=1, source_target_pairs={{0,8},{2,10},{4,12},{6,14},{8,0},{10,2},{12,4},{14,6},{16,24},{18,... | collective-permute-start | bytes 442376 | tf_op jit(solution)/shard_map/ppermute | solution.py:399
  90.5 8.6 %collective-permute-start.11 = (f32[2,144,128]{2,1,0:T(8,128)S(1)}, f32[2,144,128]{2,1,0:T(8,128)S(1)}, u32[]{:S(2)}, u32[]{:S(2)}) collective-permute-start(f32[2,144,128]{2,1,0:T(8,128)S(1)} %add.26), channel_id=1, source_target_pairs={{0,16},{2,18},{4,20},{6,22},{8,24},{10,26},{12,28},{14,30},{16,0},... | collective-permute-start | bytes 442376 | tf_op jit(solution)/shard_map/ppermute | solution.py:399
  99.0 1.4 %collective-permute-start.12 = (f32[2,144,128]{2,1,0:T(8,128)S(1)}, f32[2,144,128]{2,1,0:T(8,128)S(1)}, u32[]{:S(2)}, u32[]{:S(2)}) collective-permute-start(f32[2,144,128]{2,1,0:T(8,128)S(1)} %add.27.mine_ref), channel_id=1, source_target_pairs={{0,2},{2,0},{4,6},{6,4},{8,10},{10,8},{12,14},{14,12},{16,18},{18,... | collective-permute-start | bytes 442376 | tf_op jit(solution)/shard_map/ppermute | solution.py:399

commit v4 on v3

--- a/solution.py
+++ b/solution.py
@@ -12,6 +12,7 @@
 BF16 = jnp.bfloat16
 ROWS = 8
 VMEM_LIMIT = 16 << 20
+COST_SHARE = 20
 WHOLE = pl.BlockSpec(memory_space=pltpu.VMEM)
 SCALAR = pl.BlockSpec(memory_space=pltpu.SMEM)
 
@@ -52,31 +53,46 @@
     lax.fori_loop(0, height // ROWS, one_block, 0, unroll=True)
 
 
-def conv_kernel(dims, sizes, unroll, has_acc, *refs):
+def conv_kernel(dims, mode, sizes, unroll, counts, *refs):
     chans, padded, planes, height = dims
-    field, sibling, neighbour, weight, bit = refs[:5]
-    refs = refs[5:]
-    acc = None
-    if has_acc:
-        acc, refs = refs[0], refs[1:]
-    results = refs[: len(sizes)]
-    xh, xl = refs[len(sizes) :]
+    ins, accs = counts
+    weight, *fields = refs[:ins]
+    acc = refs[ins] if accs else None
+    results = refs[ins + accs : ins + accs + len(sizes)]
+    xh, xl = refs[ins + accs + len(sizes) :]
     step = pl.program_id(0)
-    d = step - 1
-    width = field.shape[-1]
+    width = xh.shape[-1]
     rows_out = sum(sizes)
     span = 3 * padded
-
-    @pl.when(step == 0)
-    def _():
-        for ref, side in ((sibling, 1 - bit[0]), (neighbour, bit[0])):
-            fill_plane(
-                xh, xl, side * (planes + 1), lambda s, r=ref: r[:, 0, s, :], chans, padded, height
-            )
-
-    @pl.when(step < planes)
-    def _():
-        fill_plane(xh, xl, step + 1, lambda s: field[:, 0, s, :], chans, padded, height)
+    if mode == "outer":
+        bit, d, active = fields[2], step * (planes - 1), None
+    elif mode == "inner":
+        bit, d, active = None, step - 1, step > 1
+    else:
+        bit, d, active = fields[3], step - 1, step > 0
+
+    if bit is not None:
+        sibling, neighbour = fields[:2] if mode == "outer" else fields[1:3]
+
+        @pl.when(step == 0)
+        def _():
+            for ref, side in ((sibling, 1 - bit[0]), (neighbour, bit[0])):
+                fill_plane(
+                    xh,
+                    xl,
+                    side * (planes + 1),
+                    lambda s, r=ref: r[:, 0, s, :],
+                    chans,
+                    padded,
+                    height,
+                )
+
+    if mode != "outer":
+        field = fields[0]
+
+        @pl.when(step < planes)
+        def _():
+            fill_plane(xh, xl, step + 1, lambda s: field[:, 0, s, :], chans, padded, height)
 
     lane = lax.broadcasted_iota(jnp.int32, (rows_out, width), 1)
     first = lane == 0
@@ -119,50 +135,98 @@
             start += size
         return carry
 
-    @pl.when(step > 0)
-    def _():
+    def plane_sums():
         lax.fori_loop(0, height // ROWS, one_block, 0, unroll=unroll)
 
-
-def conv(field, halo, weight, bit, sizes, unroll, acc=None, keep=False):
-    chans, planes, height, width = field.shape
+    if active is None:
+        plane_sums()
+    else:
+        pl.when(active)(plane_sums)
+
+
+def conv(mode, fields, halo, weight, bit, sizes, unroll, acc=None, keep=False):
+    width = fields[0].shape[-1]
+    if mode == "outer":
+        chans = halo[0].shape[0]
+        planes, height = fields[0].shape[0] - 2, halo[0].shape[2]
+    else:
+        chans, planes, height, _ = fields[0].shape
     padded = up_to(chans, 16)
+    held = (planes + 2, (height + 2) * padded, width)
+    if mode == "outer":
+        steps, out_planes = 2, 2
+        plane_of, place_of = (lambda d: d * (planes - 1)), (lambda d: d)
+    elif mode == "inner":
+        steps, out_planes = planes, planes - 2
+        plane_of = lambda d: jnp.maximum(d - 1, 1)
+        place_of = lambda d: jnp.maximum(d - 2, 0)
+    else:
+        steps, out_planes = planes + 1, planes
+        plane_of = place_of = lambda d: jnp.maximum(d - 1, 0)
+    if acc is not None:
+        out_planes, place_of = planes, plane_of
 
     def plane_spec(size):
-        return pl.BlockSpec(
-            (size, 1, height, width), lambda d: (0, jnp.maximum(d - 1, 0), 0, 0)
-        )
-
-    args = [field, *halo, weight, bit]
-    in_specs = [
-        pl.BlockSpec(
-            (chans, 1, height, width), lambda d: (0, jnp.minimum(d, planes - 1), 0, 0)
-        )
-    ]
-    in_specs += [WHOLE] * 3 + [SCALAR]
+        return pl.BlockSpec((size, 1, height, width), lambda d: (0, place_of(d), 0, 0))
+
+    args, in_specs = [weight], [WHOLE]
+    if mode != "outer":
+        args.append(fields[0])
+        in_specs.append(
+            pl.BlockSpec(
+                (chans, 1, height, width), lambda d: (0, jnp.minimum(d, planes - 1), 0, 0)
+            )
+        )
+    if mode != "inner":
+        args += [*halo, bit]
+        in_specs += [WHOLE, WHOLE, SCALAR]
+    ins = len(args)
+    aliases = {}
     if acc is not None:
+        aliases[ins] = 0
         args.append(acc)
         in_specs.append(plane_spec(sizes[0]))
+    outs = [jax.ShapeDtypeStruct((size, out_planes, height, width), F32) for size in sizes]
+    out_specs = [plane_spec(size) for size in sizes]
+    scratch = []
+    parts = [jax.ShapeDtypeStruct(held, BF16)] * 2
+    if mode == "outer":
+        for index in range(2):
+            aliases[len(args)] = len(outs)
+            args.append(fields[index])
+            in_specs.append(WHOLE)
+            outs.append(parts[index])
+            out_specs.append(WHOLE)
+    elif keep:
+        outs += parts
+        out_specs += [WHOLE] * 2
+    else:
+        scratch = [pltpu.VMEM(held, BF16)] * 2
+    skip = 2 if mode == "outer" else 0
+    accs = 0 if acc is None else 1
+
+    def kernel(*refs):
+        refs = refs[: ins + accs] + refs[ins + accs + skip :]
+        conv_kernel(
+            (chans, padded, planes, height), mode, sizes, unroll, (ins, accs), *refs
+        )
+
     cells = planes * height * width
-    held = (planes + 2, (height + 2) * padded, width)
-    count = 2 if keep else 0
     return pl.pallas_call(
-        functools.partial(
-            conv_kernel, (chans, padded, planes, height), sizes, unroll, acc is not None
-        ),
-        grid=(planes + 1,),
+        kernel,
+        grid=(steps,),
         in_specs=in_specs,
-        out_specs=[plane_spec(size) for size in sizes] + [WHOLE] * count,
-        out_shape=[jax.ShapeDtypeStruct((size, planes, height, width), F32) for size in sizes]
-        + [jax.ShapeDtypeStruct(held, BF16)] * count,
-        scratch_shapes=[pltpu.VMEM(held, BF16)] * (2 - count),
+        out_specs=out_specs,
+        out_shape=outs,
+        scratch_shapes=scratch,
+        input_output_aliases=aliases,
         compiler_params=params(),
         cost_estimate=pl.CostEstimate(
-            flops=6 * 27 * chans * sum(sizes) * cells * 2 // 20,
-            bytes_accessed=4 * (chans + sum(sizes)) * cells // 20,
+            flops=6 * 27 * chans * sum(sizes) * cells * 2 // COST_SHARE,
+            bytes_accessed=4 * (chans + sum(sizes)) * cells // COST_SHARE,
             transcendentals=0,
         ),
-        name="conv",
+        name="conv_" + mode,
     )(*args)
 
 
@@ -254,8 +318,8 @@
         scratch_shapes=[pltpu.VMEM((2 * rows, 2 * group), F32)],
         compiler_params=params(),
         cost_estimate=pl.CostEstimate(
-            flops=6 * 3 * rows * outs * cells * 2 // 20,
-            bytes_accessed=8 * outs * cells // 20,
+            flops=6 * 3 * rows * outs * cells * 2 // COST_SHARE,
+            bytes_accessed=8 * outs * cells // COST_SHARE,
             transcendentals=0,
         ),
         name="kernel_grad",
@@ -359,26 +423,38 @@
     )(me, bit, value, other)
 
 
-def add_kernel(base, piece, out):
-    out[...] = base[...] + piece[...]
-
-
-def add_into(base, piece, first, block):
-    shape = (block,) + base.shape[1:]
-    spec = pl.BlockSpec(shape, lambda c: (first // block + c, 0, 0, 0))
+def add_kernel(count, *refs):
+    total = refs[0][...]
+    for ref in refs[1:count]:
+        total = total + ref[...]
+    refs[-1][...] = total
+
+
+def add_pieces(own, pieces, whole, shape, first, block, plane_of):
+    channels, out_planes, height, width = pieces[0].shape
+    size = (block, 1, height, width)
+    start = first // block
+    here = pl.BlockSpec(size, lambda p, c: (c, p, 0, 0))
+    args = [own, *pieces]
+    specs = [pl.BlockSpec(size, lambda p, c: (start + c, p, 0, 0))] + [here] * len(pieces)
+    aliases = {}
+    if whole is not None:
+        aliases[len(args)] = 0
+        args.append(whole)
+        specs.append(pl.BlockSpec(memory_space=pl.ANY))
     return pl.pallas_call(
-        add_kernel,
-        grid=(piece.shape[0] // block,),
-        in_specs=[spec, pl.BlockSpec(shape, lambda c: (c, 0, 0, 0))],
-        out_specs=spec,
-        out_shape=jax.ShapeDtypeStruct(base.shape, F32),
-        input_output_aliases={0: 0},
-        compiler_params=params(),
+        functools.partial(add_kernel, 1 + len(pieces)),
+        grid=(out_planes, channels // block),
+        in_specs=specs,
+        out_specs=pl.BlockSpec(size, lambda p, c: (start + c, plane_of(p), 0, 0)),
+        out_shape=jax.ShapeDtypeStruct(shape, F32),
+        input_output_aliases=aliases,
+        compiler_params=params(2),
         cost_estimate=pl.CostEstimate(
-            flops=piece.size, bytes_accessed=12 * piece.size, transcendentals=0
+            flops=pieces[0].size, bytes_accessed=12 * pieces[0].size, transcendentals=0
         ),
-        name="add_into",
-    )(base, piece)
+        name="add_pieces",
+    )(*args)
 
 
 def cut_edges(field, bit):
@@ -404,14 +480,14 @@
 def per_device(activations, kernel, cotangent):
     groups = lax.axis_size("chan")
     slabs = lax.axis_size("slab")
-    assert slabs >= 4 and slabs & (slabs - 1) == 0 and groups > 1
+    assert slabs >= 16 and slabs & (slabs - 1) == 0 and groups > 1
     me = lax.axis_index("chan").reshape(1)
     bit = lax.rem(lax.axis_index("slab"), 2).reshape(1)
     channels, taps, cin = kernel.shape
     mine = channels // groups
     planes, height, width = activations.shape[1:]
-    tail = max(mine // 4, 1)
-    pieces = (mine - tail, tail)
+    quarter = mine // 4
+    pieces = (mine - 2 * quarter, quarter, quarter)
     after = lax.optimization_barrier
 
     cots = [cotangent]
@@ -420,24 +496,31 @@
             lax.ppermute(cotangent, "chan", [((i + s) % groups, i) for i in range(groups)])
         )
     activations, *edges = cut_edges(activations, bit)
-    own, *edges = after((cotangent, *edges))
     act_halo = slab_halo(*edges)
+    forward, *backward = weight_matrices(me, kernel.transpose(1, 2, 0), groups)
+
+    own_inner, *inner, xh, xl = conv(
+        "inner", [activations], None, forward, bit, (mine,) * groups, 2, keep=True
+    )
+    own, xh, *act_halo = after((cotangent, xh, *act_halo))
     own, *edges = cut_edges(own, bit)
+    *edges, xh = after((*edges, xh))
     cot_halo = slab_halo(*edges)
-    forward, *backward = weight_matrices(me, kernel.transpose(1, 2, 0), groups)
-
-    features, *partial, xh, xl = conv(
-        activations, act_halo, forward, bit, (mine,) + pieces * (groups - 1), 2, keep=True
-    )
-    received = []
-    for s in range(1, groups):
-        for part in partial[2 * (s - 1) : 2 * s]:
-            received.append(
-                lax.ppermute(part, "chan", [(i, (i + s) % groups) for i in range(groups)])
-            )
+    own_outer, *outer, xh, xl = conv(
+        "outer", [xh, xl], act_halo, forward, bit, (mine,) + pieces * (groups - 1), 2
+    )
+
+    def to_owner(part, s):
+        return lax.ppermute(part, "chan", [(i, (i + s) % groups) for i in range(groups)])
+
+    got_inner = [to_owner(inner[s - 1], s) for s in range(1, groups)]
+    got_outer = []
+    for index in range(len(pieces)):
+        parts = outer[index :: len(pieces)]
+        got_outer.append([to_owner(parts[s - 1], s) for s in range(1, groups)])
 
     grads = list(kernel_grad(xh, xl, own, bit))
-    (input_grad,) = conv(own, cot_halo, backward[0], bit, (cin,), 4)
+    (input_grad,) = conv("all", [own], cot_halo, backward[0], bit, (cin,), 4)
     for s in range(1, groups):
         cot, input_grad, *grads = after((cots[s], input_grad, *grads))
         cot, *edges = cut_edges(cot, bit)
@@ -446,31 +529,47 @@
             grads += kernel_grad(xh, xl, cot, bit)
         else:
             kept, sent = kernel_grad(xh, xl, cot, bit, grads)
-            kept, sent, *halo = after((kept, sent, *halo))
             value = kept + slab_swap(sent, 1)
             value, cot = after((value, cot))
             other = slab_swap(value, 2)
-        (input_grad,) = conv(cot, halo, backward[s], bit, (cin,), 4, input_grad)
+        input_grad, ch, cl = conv(
+            "inner", [cot], None, backward[s], bit, (cin,), 4, input_grad, keep=True
+        )
+        if s == groups - 1:
+            other, ch, *halo = after((other, ch, *halo))
+            value = value + other
+            other = slab_swap(value, 4)
+        input_grad, _, _ = conv(
+            "outer", [ch, cl], halo, backward[s], bit, (cin,), 4, input_grad
+        )
 
     other, input_grad = after((other, input_grad))
     value = value + other
-    step = 4
+    step = 8
     while step < slabs // 2:
         value = value + slab_swap(value, step)
         step *= 2
-    first_parts, last_part = received[:-1], received[-1]
-    *first_parts, value = after((*first_parts, value))
+    *got_inner, value = after((*got_inner, value))
     other = slab_swap(value, step)
-    for index, part in enumerate(first_parts):
-        features = add_into(features, part, 0 if index % 2 == 0 else pieces[0], tail)
+    features = add_pieces(
+        own_inner, got_inner, None, (mine, planes, height, width), 0,
+        mine // 2, lambda p: p + 1,
+    )
     other, features = after((other, features))
     value = value + other
     cells_all = planes * slabs * height * width
     weight_grad = finish(
         me, bit, value, slab_swap(value, 1), groups, cin, channels, 1.0 / math.sqrt(cells_all)
     )
-    weight_grad, features, last_part = after((weight_grad, features, last_part))
-    features = add_into(features, last_part, pieces[0], tail)
+    weight_grad, features = after((weight_grad, features))
+    first = 0
+    for got, size in zip(got_outer, pieces):
+        *got, features = after((*got, features))
+        features = add_pieces(
+            own_outer, got, features, features.shape, first, size,
+            lambda p: p * (planes - 1),
+        )
+        first += size
     return features, input_grad, weight_grad.transpose(2, 0, 1)
 
 

time: 104 us -> 97 us (0.933)
  starting transfers between devices: 32 us -> 24.7 us
  Pallas kernels: 48.1 us -> 51.4 us
  waiting for transfers between devices: 16.2 us -> 14.4 us
    ppermute x8, starting transfers between devices: 24.1 us -> 14.5 us  [slab_swap(): lax.ppermute(value, 'slab', [(i, i ^ bit) for i in range(lax.axis_size('s...]
    ppermute x8, waiting for transfers between devices: 8.64 us -> 5.94 us  [slab_swap(): lax.ppermute(value, 'slab', [(i, i ^ bit) for i in range(lax.axis_size('s...]
    pallas_call x5 -> x9, Pallas kernels: 33.1 us -> 35.5 us  [the longest x5 31.3 us: conv(): pl.pallas_call(kernel, grid=(steps,), in_specs=in_specs, out_specs=out_sp...]
    ppermute x2 -> x4, starting transfers between devices: 2.02 us -> 4.12 us  [to_owner(): lax.ppermute(part, 'chan', [(i, (i + s) % groups) for i in range(groups)])]
    ppermute x2 -> x4, waiting for transfers between devices: 0.01 us -> 1.4 us  [to_owner(): lax.ppermute(part, 'chan', [(i, (i + s) % groups) for i in range(groups)])]
    unnamed x8 -> x6, local copies, waits for them, and re-layouts: 2.76 us -> 1.59 us
  transfers between devices with their start and end apart: 14 -> 16, of which waited for: 5 -> 5; matrix products, arithmetic and copies ran while one was open for 3% -> 4% of each run, Pallas kernels for 45% -> 52%
where the time goes in v4:
time: 97 us; the launch traced here: 96.6 us
  Pallas kernels  51.4 us (53%)
  starting transfers between devices  24.7 us (25%)
  waiting for transfers between devices  14.4 us (15%)
  local copies, waits for them, and re-layouts  5.34 us (6%)
    pallas_call x5, Pallas kernels, conv(): pl.pallas_call(kernel, grid=(steps,), in_specs=in_specs, out_specs=out_sp...  31.3 us
    ppermute x8, starting transfers between devices, slab_swap(): lax.ppermute(value, 'slab', [(i, i ^ bit) for i in range(lax.axis_size('s...  14.5 us
    pallas_call x2, Pallas kernels, kernel_grad(): pl.pallas_call(functools.partial(grad_kernel, (padded, planes, height, wi...  13.5 us
    ppermute x1, waiting for transfers between devices, per_device(): lax.ppermute(cotangent, 'chan', [((i + s) % groups, i) for i in range(gro...  7.01 us
    ppermute x8, waiting for transfers between devices, slab_swap(): lax.ppermute(value, 'slab', [(i, i ^ bit) for i in range(lax.axis_size('s...  5.94 us
    pallas_call x4, Pallas kernels, add_pieces(): pl.pallas_call(functools.partial(add_kernel, 1 + len(pieces)), grid=(out_...  4.17 us
    ppermute x4, starting transfers between devices, to_owner(): lax.ppermute(part, 'chan', [(i, (i + s) % groups) for i in range(groups)])  4.12 us
    dynamic_slice x3, local copies, waits for them, and re-layouts, cut_edges(): to_neighbour = lax.dynamic_slice_in_dim(field, bit[0] * ends, 1, axis=1)  3.75 us
  transfers between devices with their start and end apart: 16, of which 5 were waited for; matrix products, arithmetic and copies ran while one was open for 4% of the time, Pallas kernels for 52%

profile of v4, /device:TPU:0, one launch (start us, length us, event | category | flops | bytes accessed | tf_op | source)
XLA Modules:
  0.0 96.6 jit_solution(11170436017616582682)
XLA Ops:
  0.6 0.0 copy-start.2
  0.6 3.0 %collective-permute-start.6 = (f32[32,4,32,128]{3,2,1,0:T(8,128)}, f32[32,4,32,128]{3,2,1,0:T(8,128)}, u32[]{:S(2)}, u32[]{:S(2)}) collective-permute-start(f32[32,4,32,128]{3,2,1,0:T(8,128)} %refs_2_), channel_id=1, source_target_pairs={{1,0},{0,1},{3,2},{2,3},{5,4},{4,5},{7,6},{6,7},{9,8},{8,9},{11,10... | collective-permute-start | bytes 6291464 | tf_op jit(solution)/shard_map/ppermute | solution.py:496
  3.6 0.0 copy-start
  3.6 2.4 %constant_dynamic-slice_fusion.4 = (f32[32,1,32,128]{3,2,1,0:T(8,128)}, f32[32,1,32,128]{3,2,1,0:T(8,128)}) fusion(f32[32,4,32,128]{3,2,1,0:T(8,128)} %refs_1_, s32[]{:T(128)S(6)} %select_n.5, s32[]{:T(128)S(6)} %select_n.4), kind=kLoop, calls=%fused_computation.4 | loop fusion | bytes 2097160 | tf_op jit(solution)/shard_map/dynamic_slice | solution.py:463
  6.0 0.0 collective-permute-start
  6.0 1.4 %collective-permute-start.1 = (f32[32,1,32,128]{3,2,1,0:T(8,128)}, f32[32,1,32,128]{3,2,1,0:T(8,128)}, u32[]{:S(2)}, u32[]{:S(2)}) collective-permute-start(f32[32,1,32,128]{3,2,1,0:T(8,128)} %get-tuple-element.65), channel_id=1, source_target_pairs={{2,4},{6,8},{10,12},{14,16},{18,20},{22,24},{26,28},{4,2},{8,6},{1... | collective-permute-start | bytes 1572872 | tf_op jit(solution)/shard_map/ppermute | solution.py:471
  7.5 0.0 copy-done.2
  7.5 1.3 %weights.1 = (bf16[192,896]{1,0:T(8,128)(2,1)S(1)}, bf16[96,896]{1,0:T(8,128)(2,1)S(1)}, bf16[96,896]{1,0:T(8,128)(2,1)S(1)}) custom-call(s32[1]{0:T(128)} %bitcast.me, f32[27,32,64]{2,1,0:T(8,128)S(1)} %bitcast.4), custom_call_target="tpu_custom_call" | custom-call | tf_op jit(solution)/shard_map/weights/pallas_call | solution.py:380
  8.8 0.0 copy-start.1
  8.8 1.6 %copy-done.1 = f32[32,4,32,128]{3,2,1,0:T(8,128)S(1)} copy-done((f32[32,4,32,128]{3,2,1,0:T(8,128)S(1)}, f32[32,4,32,128]{3,2,1,0:T(8,128)}, u32[]{:S(2)}) %copy-start.1) | copy-done | bytes 2097176
  10.4 5.5 %conv_inner.2 = (f32[32,2,32,128]{3,2,1,0:T(8,128)S(1)}, f32[32,2,32,128]{3,2,1,0:T(8,128)S(1)}, bf16[6,1088,128]{2,1,0:T(8,128)(2,1)S(1)}, bf16[6,1088,128]{2,1,0:T(8,128)(2,1)S(1)}) custom-call(bf16[192,896]{1,0:T(8,128)(2,1)S(1)} %get-tuple-element.61.refs_0_, f32[32,4,32,128]{3,2,1,0:T(8,128)S(1)} %copy-done.1), custom_call_target="tpu_custom_call" | custom-call | flops 543581824 | bytes 314572 | tf_op jit(solution)/shard_map/conv_inner/pallas_call | solution.py:215
  15.9 0.0 collective-permute-done.refs_1_
  15.9 0.0 collective-permute-done.1.refs_2_
  16.0 0.0 copy-done
  16.0 0.1 constant_dynamic-slice_fusion.2
  16.1 5.7 %collective-permute-start.7 = (f32[32,1,32,128]{3,2,1,0:T(8,128)S(1)}, f32[32,1,32,128]{3,2,1,0:T(8,128)S(1)}, u32[]{:S(2)}, u32[]{:S(2)}) collective-permute-start(f32[32,1,32,128]{3,2,1,0:T(8,128)S(1)} %get-tuple-element.83), channel_id=1, source_target_pairs={{0,2},{2,0},{4,6},{6,4},{8,10},{10,8},{12,14},{14,12},{16,18},{18,... | collective-permute-start | bytes 1572872 | tf_op jit(solution)/shard_map/ppermute | solution.py:475
  21.8 0.7 collective-permute-start.8
  22.5 0.6 collective-permute-start.5
  23.1 6.1 %conv_outer.2 = (f32[32,2,32,128]{3,2,1,0:T(8,128)S(1)}, f32[16,2,32,128]{3,2,1,0:T(8,128)S(1)}, f32[8,2,32,128]{3,2,1,0:T(8,128)S(1)}, f32[8,2,32,128]{3,2,1,0:...) custom-call(bf16[192,896]{1,0:T(8,128)(2,1)S(1)} %get-tuple-element., ...), custom_call_target="tpu_custom_call", output_to_operand_aliasing={{4}: (4, {}), {5}: (5, {})} | custom-call | flops 543581824 | bytes 314572 | tf_op jit(solution)/shard_map/conv_outer/pallas_call | solution.py:215
  29.2 6.3 %kernel_grad.2.refs_4_ = f32[288,128]{1,0:T(8,128)S(1)} custom-call(bf16[6,1088,128]{2,1,0:T(8,128)(2,1)S(1)} %get-tuple-element.79.refs_0_, bf16[6,1088,128]{2,1,0:T(8,128)(2,1)S(1)} %get-tuple-element.80.refs_1_, f32[32,4,32,128]{3,2,1,0:T(8,128)S(1)} %copy-done, s32[1]{0:T(128)} %bitcast.2.refs_3_.refs_4_.bit), custom_call_target="tpu_custom_call" | custom-call | flops 271790912 | bytes 209715 | tf_op jit(solution)/shard_map/kernel_grad/pallas_call | solution.py:310
  35.5 0.0 collective-permute-done.7.refs_2_
  35.5 0.0 collective-permute-done.8.refs_3_
  35.5 7.9 %conv_all.1.refs_2_ = f32[32,4,32,128]{3,2,1,0:T(8,128)} custom-call(bf16[96,896]{1,0:T(8,128)(2,1)S(1)} %get-tuple-element.81.refs_0_, f32[32,4,32,128]{3,2,1,0:T(8,128)S(1)} %copy-done, f32[32,1,32,128]{3,2,1,0:T(8,128)S(1)} %collective-permute-done.7.refs_2_, f32[32,1,32,128]{3,2,1,0:T(8,128)S(1)} %collective-permute-done.8.refs_3_, ...), custom_call_target="tpu_custom_call" | custom-call | flops 271790912 | bytes 209715 | tf_op jit(solution)/shard_map/conv_all/pallas_call | solution.py:215
  43.4 7.0 %collective-permute-done.6.refs_2_.refs_1_ = f32[32,4,32,128]{3,2,1,0:T(8,128)} collective-permute-done((f32[32,4,32,128]{3,2,1,0:T(8,128)}, f32[32,4,32,128]{3,2,1,0:T(8,128)}, u32[]{:S(2)}, u32[]{:S(2)}) %collective-permute-start.6) | collective-permute-done | bytes 2097184 | tf_op jit(solution)/shard_map/ppermute | solution.py:496
  50.4 1.3 %constant_dynamic-slice_fusion = (f32[32,1,32,128]{3,2,1,0:T(8,128)S(1)}, f32[32,1,32,128]{3,2,1,0:T(8,128)S(1)}) fusion(f32[32,4,32,128]{3,2,1,0:T(8,128)} %collective-permute-done.6.refs_2_.refs_1_, s32[]{:T(128)S(6)} %select_n.5, s32[]{:T(128)S(6)} %select_n.4), kind=kLoop, calls=%fused_computation | loop fusion | bytes 2097160 | tf_op jit(solution)/shard_map/dynamic_slice | solution.py:463
  51.7 0.1 collective-permute-start.11
  51.8 0.9 collective-permute-start.12
  52.7 7.2 %kernel_grad.3 = (f32[2,144,128]{2,1,0:T(8,128)S(1)}, f32[2,144,128]{2,1,0:T(8,128)S(1)}) custom-call(bf16[6,1088,128]{2,1,0:T(8,128)(2,1)S(1)} %get-tuple-element.79.refs_0_, bf16[6,1088,128]{2,1,0:T(8,128)(2,1)S(1)} %get-tuple-element.80.refs_1_, f32[32,4,32,128]{3,2,1,0:T(8,128)} %collective-permute-done.6.refs_2_.refs_1_, s32[1]{0:T(128)} %bitcast.2.refs_3_.refs_4_.bit, ...), custom_call_target="tpu_custom_call" | custom-call | flops 271790912 | bytes 209715 | tf_op jit(solution)/shard_map/kernel_grad/pallas_call | solution.py:310
  59.9 3.5 %collective-permute-start.9 = (f32[2,144,128]{2,1,0:T(8,128)S(1)}, f32[2,144,128]{2,1,0:T(8,128)S(1)}, u32[]{:S(2)}, u32[]{:S(2)}) collective-permute-start(f32[2,144,128]{2,1,0:T(8,128)S(1)} %get-tuple-element.89), channel_id=1, source_target_pairs={{0,2},{2,0},{4,6},{6,4},{8,10},{10,8},{12,14},{14,12},{16,18},{18,... | collective-permute-start | bytes 442376 | tf_op jit(solution)/shard_map/ppermute | solution.py:475
  63.4 1.0 %collective-permute-done.9 = f32[2,144,128]{2,1,0:T(8,128)S(1)} collective-permute-done((f32[2,144,128]{2,1,0:T(8,128)S(1)}, f32[2,144,128]{2,1,0:T(8,128)S(1)}, u32[]{:S(2)}, u32[]{:S(2)}) %collective-permute-start.9) | collective-permute-done | bytes 147488 | tf_op jit(solution)/shard_map/ppermute | solution.py:475
  64.4 1.6 %collective-permute-start.10 = (f32[2,144,128]{2,1,0:T(8,128)S(1)}, f32[2,144,128]{2,1,0:T(8,128)S(1)}, u32[]{:S(2)}, u32[]{:S(2)}) collective-permute-start(f32[2,144,128]{2,1,0:T(8,128)S(1)} %add.24), channel_id=1, source_target_pairs={{0,4},{2,6},{4,0},{6,2},{8,12},{10,14},{12,8},{14,10},{16,20},{18,... | collective-permute-start | bytes 442376 | tf_op jit(solution)/shard_map/ppermute | solution.py:475
  66.0 1.5 %collective-permute-start.4 = (f32[16,2,32,128]{3,2,1,0:T(8,128)S(1)}, f32[16,2,32,128]{3,2,1,0:T(8,128)S(1)}, u32[]{:S(2)}, u32[]{:S(2)}) collective-permute-start(f32[16,2,32,128]{3,2,1,0:T(8,128)S(1)} %get-tuple-element.77), channel_id=1, source_target_pairs={{0,1},{1,0},{2,3},{3,2},{4,5},{5,4},{6,7},{7,6},{8,9},{9,8},{10,11... | collective-permute-start | bytes 1572872 | tf_op jit(solution)/shard_map/ppermute | solution.py:514
  67.5 6.6 %conv_inner.3 = (f32[32,4,32,128]{3,2,1,0:T(8,128)}, bf16[6,1088,128]{2,1,0:T(8,128)(2,1)S(1)}, bf16[6,1088,128]{2,1,0:T(8,128)(2,1)S(1)}) custom-call(bf16[96,896]{1,0:T(8,128)(2,1)S(1)} %get-tuple-element.91.refs_0_, f32[32,4,32,128]{3,2,1,0:T(8,128)} %collective-permute-done.6.refs_2_.refs_1_, ...), custom_call_target="tpu_custom_call", output_to_operand_aliasing={{0}: (2, {})} | custom-call | flops 271790912 | bytes 209715 | tf_op jit(solution)/shard_map/conv_inner/pallas_call | solution.py:215
  74.1 0.0 collective-permute-done.10
  74.1 0.0 collective-permute-done.11.refs_1_
  74.1 0.0 collective-permute-done.12.refs_2_
  74.2 1.6 %collective-permute-start.13 = (f32[2,144,128]{2,1,0:T(8,128)S(1)}, f32[2,144,128]{2,1,0:T(8,128)S(1)}, u32[]{:S(2)}, u32[]{:S(2)}) collective-permute-start(f32[2,144,128]{2,1,0:T(8,128)S(1)} %add.25), channel_id=1, source_target_pairs={{0,8},{2,10},{4,12},{6,14},{8,0},{10,2},{12,4},{14,6},{16,24},{18,... | collective-permute-start | bytes 442376 | tf_op jit(solution)/shard_map/ppermute | solution.py:475
  75.8 5.2 %conv_outer.3 = (f32[32,4,32,128]{3,2,1,0:T(8,128)}, bf16[6,1088,128]{2,1,0:T(8,128)(2,1)S(1)}, bf16[6,1088,128]{2,1,0:T(8,128)(2,1)S(1)}) custom-call(bf16[96,896]{1,0:T(8,128)(2,1)S(1)} %get-tuple-element.91.refs_0_, f32[32,1,32,128]{3,2,1,0:T(8,128)S(1)} %collective-permute-done.11.refs_1_, ...), custom_call_target="tpu_custom_call", output_to_operand_aliasing={{0}: (4, {}), {1}: (5, {}), {2}: (6, {})} | custom-call | flops 271790912 | bytes 209715 | tf_op jit(solution)/shard_map/conv_outer/pallas_call | solution.py:215
  81.0 0.0 collective-permute-done.13
  81.0 0.0 collective-permute-done.5.refs_1_
  81.0 2.0 %collective-permute-start.14 = (f32[2,144,128]{2,1,0:T(8,128)S(1)}, f32[2,144,128]{2,1,0:T(8,128)S(1)}, u32[]{:S(2)}, u32[]{:S(2)}) collective-permute-start(f32[2,144,128]{2,1,0:T(8,128)S(1)} %add.26), channel_id=1, source_target_pairs={{0,16},{2,18},{4,20},{6,22},{8,24},{10,26},{12,28},{14,30},{16,0},... | collective-permute-start | bytes 442376 | tf_op jit(solution)/shard_map/ppermute | solution.py:475
  83.0 0.5 collective-permute-start.3
  83.5 1.5 %collective-permute-start.2 = (f32[8,2,32,128]{3,2,1,0:T(8,128)S(1)}, f32[8,2,32,128]{3,2,1,0:T(8,128)S(1)}, u32[]{:S(2)}, u32[]{:S(2)}) collective-permute-start(f32[8,2,32,128]{3,2,1,0:T(8,128)S(1)} %get-tuple-element.75), channel_id=1, source_target_pairs={{0,1},{1,0},{2,3},{3,2},{4,5},{5,4},{6,7},{7,6},{8,9},{9,8},{10,11... | collective-permute-start | bytes 786440 | tf_op jit(solution)/shard_map/ppermute | solution.py:514
  85.0 1.7 %add_pieces.4.refs_2_ = f32[32,4,32,128]{3,2,1,0:T(8,128)} custom-call(f32[32,2,32,128]{3,2,1,0:T(8,128)S(1)} %get-tuple-element.106.refs_0_, f32[32,2,32,128]{3,2,1,0:T(8,128)S(1)} %collective-permute-done.5.refs_1_), custom_call_target="tpu_custom_call" | custom-call | flops 262144 | bytes 3145728 | tf_op jit(solution)/shard_map/add_pieces/pallas_call | solution.py:445
  86.7 3.6 %collective-permute-done.14 = f32[2,144,128]{2,1,0:T(8,128)S(1)} collective-permute-done((f32[2,144,128]{2,1,0:T(8,128)S(1)}, f32[2,144,128]{2,1,0:T(8,128)S(1)}, u32[]{:S(2)}, u32[]{:S(2)}) %collective-permute-start.14) | collective-permute-done | bytes 147488 | tf_op jit(solution)/shard_map/ppermute | solution.py:475
  90.3 0.1 collective-permute-start.15
  90.4 1.4 %collective-permute-done.15.other_ref = f32[2,144,128]{2,1,0:T(8,128)S(1)} collective-permute-done((f32[2,144,128]{2,1,0:T(8,128)S(1)}, f32[2,144,128]{2,1,0:T(8,128)S(1)}, u32[]{:S(2)}, u32[]{:S(2)}) %collective-permute-start.15) | collective-permute-done | bytes 147488 | tf_op jit(solution)/shard_map/ppermute | solution.py:475
  91.8 1.0 %finish.1 = f32[27,32,64]{2,1,0:T(8,128)} custom-call(s32[1]{0:T(128)} %bitcast.me, s32[1]{0:T(128)} %bitcast.2.refs_3_.refs_4_.bit, f32[2,144,128]{2,1,0:T(8,128)S(1)} %add.27.mine_ref, f32[2,144,128]{2,1,0:T(8,128)S(1)} %collective-permute-done.15.other_ref), custom_call_target="tpu_custom_call" | custom-call | tf_op jit(solution)/shard_map/finish/pallas_call | solution.py:416
  92.8 0.0 collective-permute-done.4.refs_1_
  92.8 0.9 add_pieces.5.refs_2_
  93.7 0.0 collective-permute-done.3.refs_1_
  93.7 0.8 add_pieces.6.refs_2_
  94.5 1.4 %collective-permute-done.2.refs_1_ = f32[8,2,32,128]{3,2,1,0:T(8,128)S(1)} collective-permute-done((f32[8,2,32,128]{3,2,1,0:T(8,128)S(1)}, f32[8,2,32,128]{3,2,1,0:T(8,128)S(1)}, u32[]{:S(2)}, u32[]{:S(2)}) %collective-permute-start.2) | collective-permute-done | bytes 262176 | tf_op jit(solution)/shard_map/ppermute | solution.py:514
  95.9 0.8 add_pieces.7
  (4 shorter events, 0.1 us)
Async XLA Ops:
  0.6 6.9 %copy-start.2 = (f32[64,27,32]{0,2,1:T(8,128)S(1)}, f32[64,27,32]{0,2,1:T(8,128)}, u32[]{:S(2)}) copy-start(f32[64,27,32]{0,2,1:T(8,128)} %param.4) | copy-start | bytes 663556
  0.6 49.8 %collective-permute-start.6 = (f32[32,4,32,128]{3,2,1,0:T(8,128)}, f32[32,4,32,128]{3,2,1,0:T(8,128)}, u32[]{:S(2)}, u32[]{:S(2)}) collective-permute-start(f32[32,4,32,128]{3,2,1,0:T(8,128)} %refs_2_), channel_id=1, source_target_pairs={{1,0},{0,1},{3,2},{2,3},{5,4},{4,5},{7,6},{6,7},{9,8},{8,9},{11,10... | collective-permute-start | bytes 6291464 | tf_op jit(solution)/shard_map/ppermute | solution.py:496
  3.6 12.3 %copy-start = (f32[32,4,32,128]{3,2,1,0:T(8,128)S(1)}, f32[32,4,32,128]{3,2,1,0:T(8,128)}, u32[]{:S(2)}) copy-start(f32[32,4,32,128]{3,2,1,0:T(8,128)} %refs_2_) | copy-start | bytes 6291460
  6.0 9.9 %collective-permute-start = (f32[32,1,32,128]{3,2,1,0:T(8,128)}, f32[32,1,32,128]{3,2,1,0:T(8,128)}, u32[]{:S(2)}, u32[]{:S(2)}) collective-permute-start(f32[32,1,32,128]{3,2,1,0:T(8,128)} %get-tuple-element.64), channel_id=1, source_target_pairs={{0,2},{2,0},{4,6},{6,4},{8,10},{10,8},{12,14},{14,12},{16,18},{18,... | collective-permute-start | bytes 1572872 | tf_op jit(solution)/shard_map/ppermute | solution.py:475
  6.0 9.9 %collective-permute-start.1 = (f32[32,1,32,128]{3,2,1,0:T(8,128)}, f32[32,1,32,128]{3,2,1,0:T(8,128)}, u32[]{:S(2)}, u32[]{:S(2)}) collective-permute-start(f32[32,1,32,128]{3,2,1,0:T(8,128)} %get-tuple-element.65), channel_id=1, source_target_pairs={{2,4},{6,8},{10,12},{14,16},{18,20},{22,24},{26,28},{4,2},{8,6},{1... | collective-permute-start | bytes 1572872 | tf_op jit(solution)/shard_map/ppermute | solution.py:471
  8.8 1.6 %copy-start.1 = (f32[32,4,32,128]{3,2,1,0:T(8,128)S(1)}, f32[32,4,32,128]{3,2,1,0:T(8,128)}, u32[]{:S(2)}) copy-start(f32[32,4,32,128]{3,2,1,0:T(8,128)} %refs_1_) | copy-start | bytes 6291460
  16.1 19.4 %collective-permute-start.7 = (f32[32,1,32,128]{3,2,1,0:T(8,128)S(1)}, f32[32,1,32,128]{3,2,1,0:T(8,128)S(1)}, u32[]{:S(2)}, u32[]{:S(2)}) collective-permute-start(f32[32,1,32,128]{3,2,1,0:T(8,128)S(1)} %get-tuple-element.83), channel_id=1, source_target_pairs={{0,2},{2,0},{4,6},{6,4},{8,10},{10,8},{12,14},{14,12},{16,18},{18,... | collective-permute-start | bytes 1572872 | tf_op jit(solution)/shard_map/ppermute | solution.py:475
  21.8 13.7 %collective-permute-start.8 = (f32[32,1,32,128]{3,2,1,0:T(8,128)S(1)}, f32[32,1,32,128]{3,2,1,0:T(8,128)S(1)}, u32[]{:S(2)}, u32[]{:S(2)}) collective-permute-start(f32[32,1,32,128]{3,2,1,0:T(8,128)S(1)} %get-tuple-element.84), channel_id=1, source_target_pairs={{2,4},{6,8},{10,12},{14,16},{18,20},{22,24},{26,28},{4,2},{8,6},{1... | collective-permute-start | bytes 1572872 | tf_op jit(solution)/shard_map/ppermute | solution.py:471
  22.5 58.6 %collective-permute-start.5 = (f32[32,2,32,128]{3,2,1,0:T(8,128)S(1)}, f32[32,2,32,128]{3,2,1,0:T(8,128)S(1)}, u32[]{:S(2)}, u32[]{:S(2)}) collective-permute-start(f32[32,2,32,128]{3,2,1,0:T(8,128)S(1)} %get-tuple-element.78), channel_id=1, source_target_pairs={{0,1},{1,0},{2,3},{3,2},{4,5},{5,4},{6,7},{7,6},{8,9},{9,8},{10,11... | collective-permute-start | bytes 3145736 | tf_op jit(solution)/shard_map/ppermute | solution.py:514
  51.7 22.4 %collective-permute-start.11 = (f32[32,1,32,128]{3,2,1,0:T(8,128)S(1)}, f32[32,1,32,128]{3,2,1,0:T(8,128)S(1)}, u32[]{:S(2)}, u32[]{:S(2)}) collective-permute-start(f32[32,1,32,128]{3,2,1,0:T(8,128)S(1)} %get-tuple-element.95), channel_id=1, source_target_pairs={{0,2},{2,0},{4,6},{6,4},{8,10},{10,8},{12,14},{14,12},{16,18},{18,... | collective-permute-start | bytes 1572872 | tf_op jit(solution)/shard_map/ppermute | solution.py:475
  51.8 22.4 %collective-permute-start.12 = (f32[32,1,32,128]{3,2,1,0:T(8,128)S(1)}, f32[32,1,32,128]{3,2,1,0:T(8,128)S(1)}, u32[]{:S(2)}, u32[]{:S(2)}) collective-permute-start(f32[32,1,32,128]{3,2,1,0:T(8,128)S(1)} %get-tuple-element.96), channel_id=1, source_target_pairs={{2,4},{6,8},{10,12},{14,16},{18,20},{22,24},{26,28},{4,2},{8,6},{1... | collective-permute-start | bytes 1572872 | tf_op jit(solution)/shard_map/ppermute | solution.py:471
  59.9 4.5 %collective-permute-start.9 = (f32[2,144,128]{2,1,0:T(8,128)S(1)}, f32[2,144,128]{2,1,0:T(8,128)S(1)}, u32[]{:S(2)}, u32[]{:S(2)}) collective-permute-start(f32[2,144,128]{2,1,0:T(8,128)S(1)} %get-tuple-element.89), channel_id=1, source_target_pairs={{0,2},{2,0},{4,6},{6,4},{8,10},{10,8},{12,14},{14,12},{16,18},{18,... | collective-permute-start | bytes 442376 | tf_op jit(solution)/shard_map/ppermute | solution.py:475
  64.4 9.7 %collective-permute-start.10 = (f32[2,144,128]{2,1,0:T(8,128)S(1)}, f32[2,144,128]{2,1,0:T(8,128)S(1)}, u32[]{:S(2)}, u32[]{:S(2)}) collective-permute-start(f32[2,144,128]{2,1,0:T(8,128)S(1)} %add.24), channel_id=1, source_target_pairs={{0,4},{2,6},{4,0},{6,2},{8,12},{10,14},{12,8},{14,10},{16,20},{18,... | collective-permute-start | bytes 442376 | tf_op jit(solution)/shard_map/ppermute | solution.py:475
  66.0 26.8 %collective-permute-start.4 = (f32[16,2,32,128]{3,2,1,0:T(8,128)S(1)}, f32[16,2,32,128]{3,2,1,0:T(8,128)S(1)}, u32[]{:S(2)}, u32[]{:S(2)}) collective-permute-start(f32[16,2,32,128]{3,2,1,0:T(8,128)S(1)} %get-tuple-element.77), channel_id=1, source_target_pairs={{0,1},{1,0},{2,3},{3,2},{4,5},{5,4},{6,7},{7,6},{8,9},{9,8},{10,11... | collective-permute-start | bytes 1572872 | tf_op jit(solution)/shard_map/ppermute | solution.py:514
  74.2 6.8 %collective-permute-start.13 = (f32[2,144,128]{2,1,0:T(8,128)S(1)}, f32[2,144,128]{2,1,0:T(8,128)S(1)}, u32[]{:S(2)}, u32[]{:S(2)}) collective-permute-start(f32[2,144,128]{2,1,0:T(8,128)S(1)} %add.25), channel_id=1, source_target_pairs={{0,8},{2,10},{4,12},{6,14},{8,0},{10,2},{12,4},{14,6},{16,24},{18,... | collective-permute-start | bytes 442376 | tf_op jit(solution)/shard_map/ppermute | solution.py:475
  81.0 9.3 %collective-permute-start.14 = (f32[2,144,128]{2,1,0:T(8,128)S(1)}, f32[2,144,128]{2,1,0:T(8,128)S(1)}, u32[]{:S(2)}, u32[]{:S(2)}) collective-permute-start(f32[2,144,128]{2,1,0:T(8,128)S(1)} %add.26), channel_id=1, source_target_pairs={{0,16},{2,18},{4,20},{6,22},{8,24},{10,26},{12,28},{14,30},{16,0},... | collective-permute-start | bytes 442376 | tf_op jit(solution)/shard_map/ppermute | solution.py:475
  83.0 10.7 %collective-permute-start.3 = (f32[8,2,32,128]{3,2,1,0:T(8,128)S(1)}, f32[8,2,32,128]{3,2,1,0:T(8,128)S(1)}, u32[]{:S(2)}, u32[]{:S(2)}) collective-permute-start(f32[8,2,32,128]{3,2,1,0:T(8,128)S(1)} %get-tuple-element.76), channel_id=1, source_target_pairs={{0,1},{1,0},{2,3},{3,2},{4,5},{5,4},{6,7},{7,6},{8,9},{9,8},{10,11... | collective-permute-start | bytes 786440 | tf_op jit(solution)/shard_map/ppermute | solution.py:514
  83.5 12.3 %collective-permute-start.2 = (f32[8,2,32,128]{3,2,1,0:T(8,128)S(1)}, f32[8,2,32,128]{3,2,1,0:T(8,128)S(1)}, u32[]{:S(2)}, u32[]{:S(2)}) collective-permute-start(f32[8,2,32,128]{3,2,1,0:T(8,128)S(1)} %get-tuple-element.75), channel_id=1, source_target_pairs={{0,1},{1,0},{2,3},{3,2},{4,5},{5,4},{6,7},{7,6},{8,9},{9,8},{10,11... | collective-permute-start | bytes 786440 | tf_op jit(solution)/shard_map/ppermute | solution.py:514
  90.3 1.4 %collective-permute-start.15 = (f32[2,144,128]{2,1,0:T(8,128)S(1)}, f32[2,144,128]{2,1,0:T(8,128)S(1)}, u32[]{:S(2)}, u32[]{:S(2)}) collective-permute-start(f32[2,144,128]{2,1,0:T(8,128)S(1)} %add.27.mine_ref), channel_id=1, source_target_pairs={{0,2},{2,0},{4,6},{6,4},{8,10},{10,8},{12,14},{14,12},{16,18},{18,... | collective-permute-start | bytes 442376 | tf_op jit(solution)/shard_map/ppermute | solution.py:475

commit v5 on v4

--- a/solution.py
+++ b/solution.py
@@ -486,8 +486,9 @@
     channels, taps, cin = kernel.shape
     mine = channels // groups
     planes, height, width = activations.shape[1:]
-    quarter = mine // 4
-    pieces = (mine - 2 * quarter, quarter, quarter)
+
+    quarter = max(mine // 4, 1)
+    pieces = (mine - quarter, quarter)
     after = lax.optimization_barrier
 
     cots = [cotangent]

time: 97 us -> 95.5 us (0.985)
  starting transfers between devices: 24.7 us -> 22.2 us
  Pallas kernels: 51.4 us -> 49.6 us
  waiting for transfers between devices: 14.4 us -> 16.1 us
  local copies, waits for them, and re-layouts: 5.34 us -> 6.34 us
    ppermute x8, waiting for transfers between devices: 5.94 us -> 7.45 us  [slab_swap(): lax.ppermute(value, 'slab', [(i, i ^ bit) for i in range(lax.axis_size('s...]
    ppermute x1, waiting for transfers between devices: 7.01 us -> 8.19 us  [per_device(): lax.ppermute(cotangent, 'chan', [((i + s) % groups, i) for i in range(gro...]
    pallas_call x5, Pallas kernels: 31.3 us -> 30.2 us  [conv(): pl.pallas_call(kernel, grid=(steps,), in_specs=in_specs, out_specs=out_sp...]
    unnamed x6, local copies, waits for them, and re-layouts: 1.59 us -> 2.6 us
    ppermute x4 -> x3, starting transfers between devices: 4.12 us -> 3.26 us  [to_owner(): lax.ppermute(part, 'chan', [(i, (i + s) % groups) for i in range(groups)])]
    pallas_call x4 -> x3, Pallas kernels: 4.17 us -> 3.59 us  [add_pieces(): pl.pallas_call(functools.partial(add_kernel, 1 + len(pieces)), grid=(out_...]
  transfers between devices with their start and end apart: 16 -> 15, of which waited for: 5 -> 5; matrix products, arithmetic and copies ran while one was open for 4% -> 4% of each run, Pallas kernels for 52% -> 51%
where the time goes in v5:
time: 95.5 us; the launch traced here: 95.2 us
  Pallas kernels  49.6 us (52%)
  starting transfers between devices  22.2 us (23%)
  waiting for transfers between devices  16.1 us (17%)
  local copies, waits for them, and re-layouts  6.34 us (7%)
    pallas_call x5, Pallas kernels, conv(): pl.pallas_call(kernel, grid=(steps,), in_specs=in_specs, out_specs=out_sp...  30.2 us
    ppermute x8, starting transfers between devices, slab_swap(): lax.ppermute(value, 'slab', [(i, i ^ bit) for i in range(lax.axis_size('s...  13.7 us
    pallas_call x2, Pallas kernels, kernel_grad(): pl.pallas_call(functools.partial(grad_kernel, (padded, planes, height, wi...  13.5 us
    ppermute x1, waiting for transfers between devices, per_device(): lax.ppermute(cotangent, 'chan', [((i + s) % groups, i) for i in range(gro...  8.19 us
    ppermute x8, waiting for transfers between devices, slab_swap(): lax.ppermute(value, 'slab', [(i, i ^ bit) for i in range(lax.axis_size('s...  7.45 us
    dynamic_slice x3, local copies, waits for them, and re-layouts, cut_edges(): to_neighbour = lax.dynamic_slice_in_dim(field, bit[0] * ends, 1, axis=1)  3.74 us
    pallas_call x3, Pallas kernels, add_pieces(): pl.pallas_call(functools.partial(add_kernel, 1 + len(pieces)), grid=(out_...  3.59 us
    ppermute x3, starting transfers between devices, to_owner(): lax.ppermute(part, 'chan', [(i, (i + s) % groups) for i in range(groups)])  3.26 us
  transfers between devices with their start and end apart: 15, of which 5 were waited for; matrix products, arithmetic and copies ran while one was open for 4% of the time, Pallas kernels for 51%

profile of v5, /device:TPU:0, one launch (start us, length us, event | category | flops | bytes accessed | tf_op | source)
XLA Modules:
  0.0 95.2 jit_solution(3336770689348539926)
XLA Ops:
  0.6 3.0 %collective-permute-start.5 = (f32[32,4,32,128]{3,2,1,0:T(8,128)}, f32[32,4,32,128]{3,2,1,0:T(8,128)}, u32[]{:S(2)}, u32[]{:S(2)}) collective-permute-start(f32[32,4,32,128]{3,2,1,0:T(8,128)} %refs_2_), channel_id=1, source_target_pairs={{1,0},{0,1},{3,2},{2,3},{5,4},{4,5},{7,6},{6,7},{9,8},{8,9},{11,10... | collective-permute-start | bytes 6291464 | tf_op jit(solution)/shard_map/ppermute | solution.py:497
  3.6 0.0 copy-start
  3.6 2.4 %constant_dynamic-slice_fusion.4 = (f32[32,1,32,128]{3,2,1,0:T(8,128)}, f32[32,1,32,128]{3,2,1,0:T(8,128)}) fusion(f32[32,4,32,128]{3,2,1,0:T(8,128)} %refs_1_, s32[]{:T(128)S(6)} %select_n.5, s32[]{:T(128)S(6)} %select_n.4), kind=kLoop, calls=%fused_computation.4 | loop fusion | bytes 2097160 | tf_op jit(solution)/shard_map/dynamic_slice | solution.py:463
  6.0 0.0 collective-permute-start
  6.0 0.7 collective-permute-start.1
  6.7 0.0 copy-start.2
  6.7 1.0 %copy-done.2 = f32[64,27,32]{0,2,1:T(8,128)S(1)} copy-done((f32[64,27,32]{0,2,1:T(8,128)S(1)}, f32[64,27,32]{0,2,1:T(8,128)}, u32[]{:S(2)}) %copy-start.2) | copy-done | bytes 221208
  7.7 1.3 %weights.1 = (bf16[192,896]{1,0:T(8,128)(2,1)S(1)}, bf16[96,896]{1,0:T(8,128)(2,1)S(1)}, bf16[96,896]{1,0:T(8,128)(2,1)S(1)}) custom-call(s32[1]{0:T(128)} %bitcast.me, f32[27,32,64]{2,1,0:T(8,128)S(1)} %bitcast.4), custom_call_target="tpu_custom_call" | custom-call | tf_op jit(solution)/shard_map/weights/pallas_call | solution.py:380
  9.1 0.0 copy-start.1
  9.1 1.6 %copy-done.1 = f32[32,4,32,128]{3,2,1,0:T(8,128)S(1)} copy-done((f32[32,4,32,128]{3,2,1,0:T(8,128)S(1)}, f32[32,4,32,128]{3,2,1,0:T(8,128)}, u32[]{:S(2)}) %copy-start.1) | copy-done | bytes 2097176
  10.7 5.6 %conv_inner.2 = (f32[32,2,32,128]{3,2,1,0:T(8,128)S(1)}, f32[32,2,32,128]{3,2,1,0:T(8,128)S(1)}, bf16[6,1088,128]{2,1,0:T(8,128)(2,1)S(1)}, bf16[6,1088,128]{2,1,0:T(8,128)(2,1)S(1)}) custom-call(bf16[192,896]{1,0:T(8,128)(2,1)S(1)} %get-tuple-element.58.refs_0_, f32[32,4,32,128]{3,2,1,0:T(8,128)S(1)} %copy-done.1), custom_call_target="tpu_custom_call" | custom-call | flops 543581824 | bytes 314572 | tf_op jit(solution)/shard_map/conv_inner/pallas_call | solution.py:215
  16.2 0.0 collective-permute-done.refs_1_
  16.2 0.0 collective-permute-done.1.refs_2_
  16.3 0.0 copy-done
  16.3 0.1 constant_dynamic-slice_fusion.2
  16.3 5.4 %collective-permute-start.6 = (f32[32,1,32,128]{3,2,1,0:T(8,128)S(1)}, f32[32,1,32,128]{3,2,1,0:T(8,128)S(1)}, u32[]{:S(2)}, u32[]{:S(2)}) collective-permute-start(f32[32,1,32,128]{3,2,1,0:T(8,128)S(1)} %get-tuple-element.79), channel_id=1, source_target_pairs={{0,2},{2,0},{4,6},{6,4},{8,10},{10,8},{12,14},{14,12},{16,18},{18,... | collective-permute-start | bytes 1572872 | tf_op jit(solution)/shard_map/ppermute | solution.py:475
  21.7 0.7 collective-permute-start.7
  22.4 0.6 collective-permute-start.4
  23.0 5.0 %conv_outer.2 = (f32[32,2,32,128]{3,2,1,0:T(8,128)S(1)}, f32[24,2,32,128]{3,2,1,0:T(8,128)S(1)}, f32[8,2,32,128]{3,2,1,0:T(8,128)S(1)}, bf16[6,1088,128]{2,1,0:T(8,128)(2,1)S(1)}, bf16[6,1088,128]{2,1,0:T(8,128)(2,1)S(1)}) custom-call(bf16[192,896]{1,0:T(8,128)(2,1)S(1)} %get-tuple-element.58.refs_0_, ...), custom_call_target="tpu_custom_call", output_to_operand_aliasing={{3}: (4, {}), {4}: (5, {})} | custom-call | flops 543581824 | bytes 314572 | tf_op jit(solution)/shard_map/conv_outer/pallas_call | solution.py:215
  28.0 6.3 %kernel_grad.2.refs_4_ = f32[288,128]{1,0:T(8,128)S(1)} custom-call(bf16[6,1088,128]{2,1,0:T(8,128)(2,1)S(1)} %get-tuple-element.75.refs_0_, bf16[6,1088,128]{2,1,0:T(8,128)(2,1)S(1)} %get-tuple-element.76.refs_1_, f32[32,4,32,128]{3,2,1,0:T(8,128)S(1)} %copy-done, s32[1]{0:T(128)} %bitcast.2.refs_3_.refs_4_.bit), custom_call_target="tpu_custom_call" | custom-call | flops 271790912 | bytes 209715 | tf_op jit(solution)/shard_map/kernel_grad/pallas_call | solution.py:310
  34.3 0.0 collective-permute-done.6.refs_2_
  34.3 0.0 collective-permute-done.7.refs_3_
  34.3 7.9 %conv_all.1.refs_2_ = f32[32,4,32,128]{3,2,1,0:T(8,128)} custom-call(bf16[96,896]{1,0:T(8,128)(2,1)S(1)} %get-tuple-element.77.refs_0_, f32[32,4,32,128]{3,2,1,0:T(8,128)S(1)} %copy-done, f32[32,1,32,128]{3,2,1,0:T(8,128)S(1)} %collective-permute-done.6.refs_2_, f32[32,1,32,128]{3,2,1,0:T(8,128)S(1)} %collective-permute-done.7.refs_3_, ...), custom_call_target="tpu_custom_call" | custom-call | flops 271790912 | bytes 209715 | tf_op jit(solution)/shard_map/conv_all/pallas_call | solution.py:215
  42.2 8.2 %collective-permute-done.5.refs_2_.refs_1_ = f32[32,4,32,128]{3,2,1,0:T(8,128)} collective-permute-done((f32[32,4,32,128]{3,2,1,0:T(8,128)}, f32[32,4,32,128]{3,2,1,0:T(8,128)}, u32[]{:S(2)}, u32[]{:S(2)}) %collective-permute-start.5) | collective-permute-done | bytes 2097184 | tf_op jit(solution)/shard_map/ppermute | solution.py:497
  50.4 1.3 %constant_dynamic-slice_fusion = (f32[32,1,32,128]{3,2,1,0:T(8,128)S(1)}, f32[32,1,32,128]{3,2,1,0:T(8,128)S(1)}) fusion(f32[32,4,32,128]{3,2,1,0:T(8,128)} %collective-permute-done.5.refs_2_.refs_1_, s32[]{:T(128)S(6)} %select_n.5, s32[]{:T(128)S(6)} %select_n.4), kind=kLoop, calls=%fused_computation | loop fusion | bytes 2097160 | tf_op jit(solution)/shard_map/dynamic_slice | solution.py:463
  51.7 0.1 collective-permute-start.10
  51.8 0.9 collective-permute-start.11
  52.6 2.1 %collective-permute-start.3 = (f32[24,2,32,128]{3,2,1,0:T(8,128)S(1)}, f32[24,2,32,128]{3,2,1,0:T(8,128)S(1)}, u32[]{:S(2)}, u32[]{:S(2)}) collective-permute-start(f32[24,2,32,128]{3,2,1,0:T(8,128)S(1)} %get-tuple-element.73), channel_id=1, source_target_pairs={{0,1},{1,0},{2,3},{3,2},{4,5},{5,4},{6,7},{7,6},{8,9},{9,8},{10,11... | collective-permute-start | bytes 2359304 | tf_op jit(solution)/shard_map/ppermute | solution.py:515
  54.8 7.2 %kernel_grad.3 = (f32[2,144,128]{2,1,0:T(8,128)S(1)}, f32[2,144,128]{2,1,0:T(8,128)S(1)}) custom-call(bf16[6,1088,128]{2,1,0:T(8,128)(2,1)S(1)} %get-tuple-element.75.refs_0_, bf16[6,1088,128]{2,1,0:T(8,128)(2,1)S(1)} %get-tuple-element.76.refs_1_, f32[32,4,32,128]{3,2,1,0:T(8,128)} %collective-permute-done.5.refs_2_.refs_1_, s32[1]{0:T(128)} %bitcast.2.refs_3_.refs_4_.bit, ...), custom_call_target="tpu_custom_call" | custom-call | flops 271790912 | bytes 209715 | tf_op jit(solution)/shard_map/kernel_grad/pallas_call | solution.py:310
  62.0 2.6 %collective-permute-start.8 = (f32[2,144,128]{2,1,0:T(8,128)S(1)}, f32[2,144,128]{2,1,0:T(8,128)S(1)}, u32[]{:S(2)}, u32[]{:S(2)}) collective-permute-start(f32[2,144,128]{2,1,0:T(8,128)S(1)} %get-tuple-element.85), channel_id=1, source_target_pairs={{0,2},{2,0},{4,6},{6,4},{8,10},{10,8},{12,14},{14,12},{16,18},{18,... | collective-permute-start | bytes 442376 | tf_op jit(solution)/shard_map/ppermute | solution.py:475
  64.6 1.0 %collective-permute-done.8 = f32[2,144,128]{2,1,0:T(8,128)S(1)} collective-permute-done((f32[2,144,128]{2,1,0:T(8,128)S(1)}, f32[2,144,128]{2,1,0:T(8,128)S(1)}, u32[]{:S(2)}, u32[]{:S(2)}) %collective-permute-start.8) | collective-permute-done | bytes 147488 | tf_op jit(solution)/shard_map/ppermute | solution.py:475
  65.7 1.6 %collective-permute-start.9 = (f32[2,144,128]{2,1,0:T(8,128)S(1)}, f32[2,144,128]{2,1,0:T(8,128)S(1)}, u32[]{:S(2)}, u32[]{:S(2)}) collective-permute-start(f32[2,144,128]{2,1,0:T(8,128)S(1)} %add.24), channel_id=1, source_target_pairs={{0,4},{2,6},{4,0},{6,2},{8,12},{10,14},{12,8},{14,10},{16,20},{18,... | collective-permute-start | bytes 442376 | tf_op jit(solution)/shard_map/ppermute | solution.py:475
  67.3 6.6 %conv_inner.3 = (f32[32,4,32,128]{3,2,1,0:T(8,128)}, bf16[6,1088,128]{2,1,0:T(8,128)(2,1)S(1)}, bf16[6,1088,128]{2,1,0:T(8,128)(2,1)S(1)}) custom-call(bf16[96,896]{1,0:T(8,128)(2,1)S(1)} %get-tuple-element.87.refs_0_, f32[32,4,32,128]{3,2,1,0:T(8,128)} %collective-permute-done.5.refs_2_.refs_1_, ...), custom_call_target="tpu_custom_call", output_to_operand_aliasing={{0}: (2, {})} | custom-call | flops 271790912 | bytes 209715 | tf_op jit(solution)/shard_map/conv_inner/pallas_call | solution.py:215
  73.9 0.0 collective-permute-done.9
  73.9 0.0 collective-permute-done.10.refs_1_
  73.9 0.0 collective-permute-done.11.refs_2_
  73.9 1.6 %collective-permute-start.12 = (f32[2,144,128]{2,1,0:T(8,128)S(1)}, f32[2,144,128]{2,1,0:T(8,128)S(1)}, u32[]{:S(2)}, u32[]{:S(2)}) collective-permute-start(f32[2,144,128]{2,1,0:T(8,128)S(1)} %add.25), channel_id=1, source_target_pairs={{0,8},{2,10},{4,12},{6,14},{8,0},{10,2},{12,4},{14,6},{16,24},{18,... | collective-permute-start | bytes 442376 | tf_op jit(solution)/shard_map/ppermute | solution.py:475
  75.5 5.2 %conv_outer.3 = (f32[32,4,32,128]{3,2,1,0:T(8,128)}, bf16[6,1088,128]{2,1,0:T(8,128)(2,1)S(1)}, bf16[6,1088,128]{2,1,0:T(8,128)(2,1)S(1)}) custom-call(bf16[96,896]{1,0:T(8,128)(2,1)S(1)} %get-tuple-element.87.refs_0_, f32[32,1,32,128]{3,2,1,0:T(8,128)S(1)} %collective-permute-done.10.refs_1_, ...), custom_call_target="tpu_custom_call", output_to_operand_aliasing={{0}: (4, {}), {1}: (5, {}), {2}: (6, {})} | custom-call | flops 271790912 | bytes 209715 | tf_op jit(solution)/shard_map/conv_outer/pallas_call | solution.py:215
  80.7 0.0 collective-permute-done.12
  80.8 0.0 collective-permute-done.4.refs_1_
  80.8 2.3 %collective-permute-start.13 = (f32[2,144,128]{2,1,0:T(8,128)S(1)}, f32[2,144,128]{2,1,0:T(8,128)S(1)}, u32[]{:S(2)}, u32[]{:S(2)}) collective-permute-start(f32[2,144,128]{2,1,0:T(8,128)S(1)} %add.26), channel_id=1, source_target_pairs={{0,16},{2,18},{4,20},{6,22},{8,24},{10,26},{12,28},{14,30},{16,0},... | collective-permute-start | bytes 442376 | tf_op jit(solution)/shard_map/ppermute | solution.py:475
  83.0 0.5 collective-permute-start.2
  83.6 1.7 %add_pieces.3.refs_2_ = f32[32,4,32,128]{3,2,1,0:T(8,128)} custom-call(f32[32,2,32,128]{3,2,1,0:T(8,128)S(1)} %get-tuple-element.102.refs_0_, f32[32,2,32,128]{3,2,1,0:T(8,128)S(1)} %collective-permute-done.4.refs_1_), custom_call_target="tpu_custom_call" | custom-call | flops 262144 | bytes 3145728 | tf_op jit(solution)/shard_map/add_pieces/pallas_call | solution.py:445
  85.3 5.1 %collective-permute-done.13 = f32[2,144,128]{2,1,0:T(8,128)S(1)} collective-permute-done((f32[2,144,128]{2,1,0:T(8,128)S(1)}, f32[2,144,128]{2,1,0:T(8,128)S(1)}, u32[]{:S(2)}, u32[]{:S(2)}) %collective-permute-start.13) | collective-permute-done | bytes 147488 | tf_op jit(solution)/shard_map/ppermute | solution.py:475
  90.3 0.1 collective-permute-start.14
  90.4 1.4 %collective-permute-done.14.other_ref = f32[2,144,128]{2,1,0:T(8,128)S(1)} collective-permute-done((f32[2,144,128]{2,1,0:T(8,128)S(1)}, f32[2,144,128]{2,1,0:T(8,128)S(1)}, u32[]{:S(2)}, u32[]{:S(2)}) %collective-permute-start.14) | collective-permute-done | bytes 147488 | tf_op jit(solution)/shard_map/ppermute | solution.py:475
  91.8 1.0 %finish.1 = f32[27,32,64]{2,1,0:T(8,128)} custom-call(s32[1]{0:T(128)} %bitcast.me, s32[1]{0:T(128)} %bitcast.2.refs_3_.refs_4_.bit, f32[2,144,128]{2,1,0:T(8,128)S(1)} %add.27.mine_ref, f32[2,144,128]{2,1,0:T(8,128)S(1)} %collective-permute-done.14.other_ref), custom_call_target="tpu_custom_call" | custom-call | tf_op jit(solution)/shard_map/finish/pallas_call | solution.py:416
  92.8 0.0 collective-permute-done.3.refs_1_
  92.8 1.1 %add_pieces.4.refs_2_ = f32[32,4,32,128]{3,2,1,0:T(8,128)} custom-call(f32[32,2,32,128]{3,2,1,0:T(8,128)S(1)} %get-tuple-element.71.refs_0_, f32[24,2,32,128]{3,2,1,0:T(8,128)S(1)} %collective-permute-done.3.refs_1_, f32[32,4,32,128]{3,2,1,0:T(8,128)} %add_pieces.3.refs_2_), custom_call_target="tpu_custom_call", output_to_operand_aliasing={{}: (2, {})} | custom-call | flops 196608 | bytes 2359296 | tf_op jit(solution)/shard_map/add_pieces/pallas_call | solution.py:445
  93.9 0.5 collective-permute-done.2.refs_1_
  94.4 0.8 add_pieces.5
  (4 shorter events, 0.1 us)
Async XLA Ops:
  0.6 49.8 %collective-permute-start.5 = (f32[32,4,32,128]{3,2,1,0:T(8,128)}, f32[32,4,32,128]{3,2,1,0:T(8,128)}, u32[]{:S(2)}, u32[]{:S(2)}) collective-permute-start(f32[32,4,32,128]{3,2,1,0:T(8,128)} %refs_2_), channel_id=1, source_target_pairs={{1,0},{0,1},{3,2},{2,3},{5,4},{4,5},{7,6},{6,7},{9,8},{8,9},{11,10... | collective-permute-start | bytes 6291464 | tf_op jit(solution)/shard_map/ppermute | solution.py:497
  3.6 12.6 %copy-start = (f32[32,4,32,128]{3,2,1,0:T(8,128)S(1)}, f32[32,4,32,128]{3,2,1,0:T(8,128)}, u32[]{:S(2)}) copy-start(f32[32,4,32,128]{3,2,1,0:T(8,128)} %refs_2_) | copy-start | bytes 6291460
  6.0 10.2 %collective-permute-start = (f32[32,1,32,128]{3,2,1,0:T(8,128)}, f32[32,1,32,128]{3,2,1,0:T(8,128)S(1)}, u32[]{:S(2)}, u32[]{:S(2)}) collective-permute-start(f32[32,1,32,128]{3,2,1,0:T(8,128)} %get-tuple-element.61), channel_id=1, source_target_pairs={{0,2},{2,0},{4,6},{6,4},{8,10},{10,8},{12,14},{14,12},{16,18},{18,... | collective-permute-start | bytes 1572872 | tf_op jit(solution)/shard_map/ppermute | solution.py:475
  6.0 10.2 %collective-permute-start.1 = (f32[32,1,32,128]{3,2,1,0:T(8,128)}, f32[32,1,32,128]{3,2,1,0:T(8,128)S(1)}, u32[]{:S(2)}, u32[]{:S(2)}) collective-permute-start(f32[32,1,32,128]{3,2,1,0:T(8,128)} %get-tuple-element.62), channel_id=1, source_target_pairs={{2,4},{6,8},{10,12},{14,16},{18,20},{22,24},{26,28},{4,2},{8,6},{1... | collective-permute-start | bytes 1572872 | tf_op jit(solution)/shard_map/ppermute | solution.py:471
  6.7 1.0 %copy-start.2 = (f32[64,27,32]{0,2,1:T(8,128)S(1)}, f32[64,27,32]{0,2,1:T(8,128)}, u32[]{:S(2)}) copy-start(f32[64,27,32]{0,2,1:T(8,128)} %param.4) | copy-start | bytes 663556
  9.1 1.6 %copy-start.1 = (f32[32,4,32,128]{3,2,1,0:T(8,128)S(1)}, f32[32,4,32,128]{3,2,1,0:T(8,128)}, u32[]{:S(2)}) copy-start(f32[32,4,32,128]{3,2,1,0:T(8,128)} %refs_1_) | copy-start | bytes 6291460
  16.3 18.0 %collective-permute-start.6 = (f32[32,1,32,128]{3,2,1,0:T(8,128)S(1)}, f32[32,1,32,128]{3,2,1,0:T(8,128)S(1)}, u32[]{:S(2)}, u32[]{:S(2)}) collective-permute-start(f32[32,1,32,128]{3,2,1,0:T(8,128)S(1)} %get-tuple-element.79), channel_id=1, source_target_pairs={{0,2},{2,0},{4,6},{6,4},{8,10},{10,8},{12,14},{14,12},{16,18},{18,... | collective-permute-start | bytes 1572872 | tf_op jit(solution)/shard_map/ppermute | solution.py:475
  21.7 12.6 %collective-permute-start.7 = (f32[32,1,32,128]{3,2,1,0:T(8,128)S(1)}, f32[32,1,32,128]{3,2,1,0:T(8,128)S(1)}, u32[]{:S(2)}, u32[]{:S(2)}) collective-permute-start(f32[32,1,32,128]{3,2,1,0:T(8,128)S(1)} %get-tuple-element.80), channel_id=1, source_target_pairs={{2,4},{6,8},{10,12},{14,16},{18,20},{22,24},{26,28},{4,2},{8,6},{1... | collective-permute-start | bytes 1572872 | tf_op jit(solution)/shard_map/ppermute | solution.py:471
  22.4 58.3 %collective-permute-start.4 = (f32[32,2,32,128]{3,2,1,0:T(8,128)S(1)}, f32[32,2,32,128]{3,2,1,0:T(8,128)S(1)}, u32[]{:S(2)}, u32[]{:S(2)}) collective-permute-start(f32[32,2,32,128]{3,2,1,0:T(8,128)S(1)} %get-tuple-element.74), channel_id=1, source_target_pairs={{0,1},{1,0},{2,3},{3,2},{4,5},{5,4},{6,7},{7,6},{8,9},{9,8},{10,11... | collective-permute-start | bytes 3145736 | tf_op jit(solution)/shard_map/ppermute | solution.py:515
  51.7 22.2 %collective-permute-start.10 = (f32[32,1,32,128]{3,2,1,0:T(8,128)S(1)}, f32[32,1,32,128]{3,2,1,0:T(8,128)S(1)}, u32[]{:S(2)}, u32[]{:S(2)}) collective-permute-start(f32[32,1,32,128]{3,2,1,0:T(8,128)S(1)} %get-tuple-element.91), channel_id=1, source_target_pairs={{0,2},{2,0},{4,6},{6,4},{8,10},{10,8},{12,14},{14,12},{16,18},{18,... | collective-permute-start | bytes 1572872 | tf_op jit(solution)/shard_map/ppermute | solution.py:475
  51.8 22.1 %collective-permute-start.11 = (f32[32,1,32,128]{3,2,1,0:T(8,128)S(1)}, f32[32,1,32,128]{3,2,1,0:T(8,128)S(1)}, u32[]{:S(2)}, u32[]{:S(2)}) collective-permute-start(f32[32,1,32,128]{3,2,1,0:T(8,128)S(1)} %get-tuple-element.92), channel_id=1, source_target_pairs={{2,4},{6,8},{10,12},{14,16},{18,20},{22,24},{26,28},{4,2},{8,6},{1... | collective-permute-start | bytes 1572872 | tf_op jit(solution)/shard_map/ppermute | solution.py:471
  52.6 40.1 %collective-permute-start.3 = (f32[24,2,32,128]{3,2,1,0:T(8,128)S(1)}, f32[24,2,32,128]{3,2,1,0:T(8,128)S(1)}, u32[]{:S(2)}, u32[]{:S(2)}) collective-permute-start(f32[24,2,32,128]{3,2,1,0:T(8,128)S(1)} %get-tuple-element.73), channel_id=1, source_target_pairs={{0,1},{1,0},{2,3},{3,2},{4,5},{5,4},{6,7},{7,6},{8,9},{9,8},{10,11... | collective-permute-start | bytes 2359304 | tf_op jit(solution)/shard_map/ppermute | solution.py:515
  62.0 3.6 %collective-permute-start.8 = (f32[2,144,128]{2,1,0:T(8,128)S(1)}, f32[2,144,128]{2,1,0:T(8,128)S(1)}, u32[]{:S(2)}, u32[]{:S(2)}) collective-permute-start(f32[2,144,128]{2,1,0:T(8,128)S(1)} %get-tuple-element.85), channel_id=1, source_target_pairs={{0,2},{2,0},{4,6},{6,4},{8,10},{10,8},{12,14},{14,12},{16,18},{18,... | collective-permute-start | bytes 442376 | tf_op jit(solution)/shard_map/ppermute | solution.py:475
  65.7 8.2 %collective-permute-start.9 = (f32[2,144,128]{2,1,0:T(8,128)S(1)}, f32[2,144,128]{2,1,0:T(8,128)S(1)}, u32[]{:S(2)}, u32[]{:S(2)}) collective-permute-start(f32[2,144,128]{2,1,0:T(8,128)S(1)} %add.24), channel_id=1, source_target_pairs={{0,4},{2,6},{4,0},{6,2},{8,12},{10,14},{12,8},{14,10},{16,20},{18,... | collective-permute-start | bytes 442376 | tf_op jit(solution)/shard_map/ppermute | solution.py:475
  73.9 6.8 %collective-permute-start.12 = (f32[2,144,128]{2,1,0:T(8,128)S(1)}, f32[2,144,128]{2,1,0:T(8,128)S(1)}, u32[]{:S(2)}, u32[]{:S(2)}) collective-permute-start(f32[2,144,128]{2,1,0:T(8,128)S(1)} %add.25), channel_id=1, source_target_pairs={{0,8},{2,10},{4,12},{6,14},{8,0},{10,2},{12,4},{14,6},{16,24},{18,... | collective-permute-start | bytes 442376 | tf_op jit(solution)/shard_map/ppermute | solution.py:475
  80.8 9.6 %collective-permute-start.13 = (f32[2,144,128]{2,1,0:T(8,128)S(1)}, f32[2,144,128]{2,1,0:T(8,128)S(1)}, u32[]{:S(2)}, u32[]{:S(2)}) collective-permute-start(f32[2,144,128]{2,1,0:T(8,128)S(1)} %add.26), channel_id=1, source_target_pairs={{0,16},{2,18},{4,20},{6,22},{8,24},{10,26},{12,28},{14,30},{16,0},... | collective-permute-start | bytes 442376 | tf_op jit(solution)/shard_map/ppermute | solution.py:475
  83.0 11.4 %collective-permute-start.2 = (f32[8,2,32,128]{3,2,1,0:T(8,128)S(1)}, f32[8,2,32,128]{3,2,1,0:T(8,128)S(1)}, u32[]{:S(2)}, u32[]{:S(2)}) collective-permute-start(f32[8,2,32,128]{3,2,1,0:T(8,128)S(1)} %get-tuple-element.72), channel_id=1, source_target_pairs={{0,1},{1,0},{2,3},{3,2},{4,5},{5,4},{6,7},{7,6},{8,9},{9,8},{10,11... | collective-permute-start | bytes 786440 | tf_op jit(solution)/shard_map/ppermute | solution.py:515
  90.3 1.4 %collective-permute-start.14 = (f32[2,144,128]{2,1,0:T(8,128)S(1)}, f32[2,144,128]{2,1,0:T(8,128)S(1)}, u32[]{:S(2)}, u32[]{:S(2)}) collective-permute-start(f32[2,144,128]{2,1,0:T(8,128)S(1)} %add.27.mine_ref), channel_id=1, source_target_pairs={{0,2},{2,0},{4,6},{6,4},{8,10},{10,8},{12,14},{14,12},{16,18},{18,... | collective-permute-start | bytes 442376 | tf_op jit(solution)/shard_map/ppermute | solution.py:475

commit v6 on v5

--- a/solution.py
+++ b/solution.py
@@ -53,13 +53,13 @@
     lax.fori_loop(0, height // ROWS, one_block, 0, unroll=True)
 
 
-def conv_kernel(dims, mode, sizes, unroll, counts, *refs):
+def conv_kernel(dims, mode, sizes, unroll, counts, inner, *refs):
     chans, padded, planes, height = dims
     ins, accs = counts
     weight, *fields = refs[:ins]
     acc = refs[ins] if accs else None
     results = refs[ins + accs : ins + accs + len(sizes)]
-    xh, xl = refs[ins + accs + len(sizes) :]
+    xh, xl = refs[ins + accs + len(sizes) :][:2]
     step = pl.program_id(0)
     width = xh.shape[-1]
     rows_out = sum(sizes)
@@ -76,6 +76,9 @@
 
         @pl.when(step == 0)
         def _():
+            for src, dst in zip(inner, (xh, xl)):
+                for plane in range(1, planes + 1):
+                    dst[plane] = src[plane]
             for ref, side in ((sibling, 1 - bit[0]), (neighbour, bit[0])):
                 fill_plane(
                     xh,
@@ -190,25 +193,22 @@
     out_specs = [plane_spec(size) for size in sizes]
     scratch = []
     parts = [jax.ShapeDtypeStruct(held, BF16)] * 2
-    if mode == "outer":
-        for index in range(2):
-            aliases[len(args)] = len(outs)
-            args.append(fields[index])
-            in_specs.append(WHOLE)
-            outs.append(parts[index])
-            out_specs.append(WHOLE)
-    elif keep:
+    skip = 2 if mode == "outer" else 0
+    if skip:
+        args += fields
+        in_specs += [WHOLE] * 2
+    if keep:
         outs += parts
         out_specs += [WHOLE] * 2
     else:
         scratch = [pltpu.VMEM(held, BF16)] * 2
-    skip = 2 if mode == "outer" else 0
     accs = 0 if acc is None else 1
 
     def kernel(*refs):
+        inner = refs[ins + accs : ins + accs + skip]
         refs = refs[: ins + accs] + refs[ins + accs + skip :]
         conv_kernel(
-            (chans, padded, planes, height), mode, sizes, unroll, (ins, accs), *refs
+            (chans, padded, planes, height), mode, sizes, unroll, (ins, accs), inner, *refs
         )
 
     cells = planes * height * width
@@ -480,7 +480,8 @@
 def per_device(activations, kernel, cotangent):
     groups = lax.axis_size("chan")
     slabs = lax.axis_size("slab")
-    assert slabs >= 16 and slabs & (slabs - 1) == 0 and groups > 1
+    assert slabs > 1 and slabs & (slabs - 1) == 0 and groups > 1
+    bits = [1 << b for b in range(1, slabs.bit_length() - 1)]
     me = lax.axis_index("chan").reshape(1)
     bit = lax.rem(lax.axis_index("slab"), 2).reshape(1)
     channels, taps, cin = kernel.shape
@@ -508,8 +509,18 @@
     *edges, xh = after((*edges, xh))
     cot_halo = slab_halo(*edges)
     own_outer, *outer, xh, xl = conv(
-        "outer", [xh, xl], act_halo, forward, bit, (mine,) + pieces * (groups - 1), 2
-    )
+        "outer",
+        [xh, xl],
+        act_halo,
+        forward,
+        bit,
+        (mine,) + pieces * (groups - 1),
+        2,
+        keep=True,
+    )
+
+    def next_swap(value):
+        return slab_swap(value, bits.pop(0)) if bits else jnp.zeros_like(value)
 
     def to_owner(part, s):
         return lax.ppermute(part, "chan", [(i, (i + s) % groups) for i in range(groups)])
@@ -532,26 +543,24 @@
             kept, sent = kernel_grad(xh, xl, cot, bit, grads)
             value = kept + slab_swap(sent, 1)
             value, cot = after((value, cot))
-            other = slab_swap(value, 2)
+            other = next_swap(value)
         input_grad, ch, cl = conv(
             "inner", [cot], None, backward[s], bit, (cin,), 4, input_grad, keep=True
         )
         if s == groups - 1:
             other, ch, *halo = after((other, ch, *halo))
             value = value + other
-            other = slab_swap(value, 4)
-        input_grad, _, _ = conv(
+            other = next_swap(value)
+        (input_grad,) = conv(
             "outer", [ch, cl], halo, backward[s], bit, (cin,), 4, input_grad
         )
 
     other, input_grad = after((other, input_grad))
     value = value + other
-    step = 8
-    while step < slabs // 2:
-        value = value + slab_swap(value, step)
-        step *= 2
+    while len(bits) > 1:
+        value = value + next_swap(value)
     *got_inner, value = after((*got_inner, value))
-    other = slab_swap(value, step)
+    other = next_swap(value)
     features = add_pieces(
         own_inner, got_inner, None, (mine, planes, height, width), 0,
         mine // 2, lambda p: p + 1,

time: 95.5 us -> 95.5 us (level)
  transfers between devices with their start and end apart: 15 -> 15, of which waited for: 5 -> 5; matrix products, arithmetic and copies ran while one was open for 4% -> 4% of each run, Pallas kernels for 51% -> 52%
where the time goes in v6:
time: 95.5 us; the launch traced here: 95.2 us
  Pallas kernels  49.9 us (52%)
  starting transfers between devices  22.2 us (23%)
  waiting for transfers between devices  15.9 us (17%)
  local copies, waits for them, and re-layouts  6.35 us (7%)
    pallas_call x5, Pallas kernels, conv(): pl.pallas_call(kernel, grid=(steps,), in_specs=in_specs, out_specs=out_sp...  30.4 us
    ppermute x8, starting transfers between devices, slab_swap(): lax.ppermute(value, 'slab', [(i, i ^ bit) for i in range(lax.axis_size('s...  13.7 us
    pallas_call x2, Pallas kernels, kernel_grad(): pl.pallas_call(functools.partial(grad_kernel, (padded, planes, height, wi...  13.5 us
    ppermute x1, waiting for transfers between devices, per_device(): lax.ppermute(cotangent, 'chan', [((i + s) % groups, i) for i in range(gro...  8.07 us
    ppermute x8, waiting for transfers between devices, slab_swap(): lax.ppermute(value, 'slab', [(i, i ^ bit) for i in range(lax.axis_size('s...  7.45 us
    dynamic_slice x3, local copies, waits for them, and re-layouts, cut_edges(): to_neighbour = lax.dynamic_slice_in_dim(field, bit[0] * ends, 1, axis=1)  3.75 us
    pallas_call x3, Pallas kernels, add_pieces(): pl.pallas_call(functools.partial(add_kernel, 1 + len(pieces)), grid=(out_...  3.59 us
    ppermute x3, starting transfers between devices, to_owner(): lax.ppermute(part, 'chan', [(i, (i + s) % groups) for i in range(groups)])  3.26 us
  transfers between devices with their start and end apart: 15, of which 5 were waited for; matrix products, arithmetic and copies ran while one was open for 4% of the time, Pallas kernels for 52%

profile of v6, /device:TPU:0, one launch (start us, length us, event | category | flops | bytes accessed | tf_op | source)
XLA Modules:
  0.0 95.2 jit_solution(5084389763820429566)
XLA Ops:
  0.6 3.0 %collective-permute-start.5 = (f32[32,4,32,128]{3,2,1,0:T(8,128)}, f32[32,4,32,128]{3,2,1,0:T(8,128)}, u32[]{:S(2)}, u32[]{:S(2)}) collective-permute-start(f32[32,4,32,128]{3,2,1,0:T(8,128)} %refs_2_), channel_id=1, source_target_pairs={{1,0},{0,1},{3,2},{2,3},{5,4},{4,5},{7,6},{6,7},{9,8},{8,9},{11,10... | collective-permute-start | bytes 6291464 | tf_op jit(solution)/shard_map/ppermute | solution.py:498
  3.6 0.0 copy-start
  3.6 2.4 %constant_dynamic-slice_fusion.4 = (f32[32,1,32,128]{3,2,1,0:T(8,128)}, f32[32,1,32,128]{3,2,1,0:T(8,128)}) fusion(f32[32,4,32,128]{3,2,1,0:T(8,128)} %refs_1_, s32[]{:T(128)S(6)} %select_n.5, s32[]{:T(128)S(6)} %select_n.4), kind=kLoop, calls=%fused_computation.4 | loop fusion | bytes 2097160 | tf_op jit(solution)/shard_map/dynamic_slice | solution.py:463
  6.0 0.0 collective-permute-start
  6.0 0.7 collective-permute-start.1
  6.7 0.0 copy-start.2
  6.7 1.0 %copy-done.2 = f32[64,27,32]{0,2,1:T(8,128)S(1)} copy-done((f32[64,27,32]{0,2,1:T(8,128)S(1)}, f32[64,27,32]{0,2,1:T(8,128)}, u32[]{:S(2)}) %copy-start.2) | copy-done | bytes 221208
  7.7 1.3 %weights.1 = (bf16[192,896]{1,0:T(8,128)(2,1)S(1)}, bf16[96,896]{1,0:T(8,128)(2,1)S(1)}, bf16[96,896]{1,0:T(8,128)(2,1)S(1)}) custom-call(s32[1]{0:T(128)} %bitcast.me, f32[27,32,64]{2,1,0:T(8,128)S(1)} %bitcast.4), custom_call_target="tpu_custom_call" | custom-call | tf_op jit(solution)/shard_map/weights/pallas_call | solution.py:380
  9.1 0.0 copy-start.1
  9.1 1.6 %copy-done.1 = f32[32,4,32,128]{3,2,1,0:T(8,128)S(1)} copy-done((f32[32,4,32,128]{3,2,1,0:T(8,128)S(1)}, f32[32,4,32,128]{3,2,1,0:T(8,128)}, u32[]{:S(2)}) %copy-start.1) | copy-done | bytes 2097176
  10.7 5.5 %conv_inner.2 = (f32[32,2,32,128]{3,2,1,0:T(8,128)S(1)}, f32[32,2,32,128]{3,2,1,0:T(8,128)S(1)}, bf16[6,1088,128]{2,1,0:T(8,128)(2,1)S(1)}, bf16[6,1088,128]{2,1,0:T(8,128)(2,1)S(1)}) custom-call(bf16[192,896]{1,0:T(8,128)(2,1)S(1)} %get-tuple-element.57.refs_0_, f32[32,4,32,128]{3,2,1,0:T(8,128)S(1)} %copy-done.1), custom_call_target="tpu_custom_call" | custom-call | flops 543581824 | bytes 314572 | tf_op jit(solution)/shard_map/conv_inner/pallas_call | solution.py:215
  16.2 0.0 collective-permute-done.refs_1_
  16.2 0.0 collective-permute-done.1.refs_2_
  16.2 0.0 copy-done
  16.2 0.1 constant_dynamic-slice_fusion.2
  16.3 5.4 %collective-permute-start.6 = (f32[32,1,32,128]{3,2,1,0:T(8,128)S(1)}, f32[32,1,32,128]{3,2,1,0:T(8,128)S(1)}, u32[]{:S(2)}, u32[]{:S(2)}) collective-permute-start(f32[32,1,32,128]{3,2,1,0:T(8,128)S(1)} %get-tuple-element.78), channel_id=1, source_target_pairs={{0,2},{2,0},{4,6},{6,4},{8,10},{10,8},{12,14},{14,12},{16,18},{18,... | collective-permute-start | bytes 1572872 | tf_op jit(solution)/shard_map/ppermute | solution.py:475
  21.8 0.7 collective-permute-start.7
  22.4 0.6 collective-permute-start.4
  23.0 5.1 %conv_outer.2 = (f32[32,2,32,128]{3,2,1,0:T(8,128)S(1)}, f32[24,2,32,128]{3,2,1,0:T(8,128)S(1)}, f32[8,2,32,128]{3,2,1,0:T(8,128)S(1)}, bf16[6,1088,128]{2,1,0:T(8,128)(2,1)S(1)}, bf16[6,1088,128]{2,1,0:T(8,128)(2,1)S(1)}) custom-call(bf16[192,896]{1,0:T(8,128)(2,1)S(1)} %get-tuple-element.57.refs_0_, f32[32,1,32,128]{3,2,1,0:T(8,128)S(1)} %collective-permute-done.refs_1_, ...), custom_call_target="tpu_custom_call" | custom-call | flops 543581824 | bytes 314572 | tf_op jit(solution)/shard_map/conv_outer/pallas_call | solution.py:215
  28.1 6.3 %kernel_grad.2.refs_4_ = f32[288,128]{1,0:T(8,128)S(1)} custom-call(bf16[6,1088,128]{2,1,0:T(8,128)(2,1)S(1)} %get-tuple-element.74.refs_0_, bf16[6,1088,128]{2,1,0:T(8,128)(2,1)S(1)} %get-tuple-element.75.refs_1_, f32[32,4,32,128]{3,2,1,0:T(8,128)S(1)} %copy-done, s32[1]{0:T(128)} %bitcast.2.refs_3_.refs_4_.bit), custom_call_target="tpu_custom_call" | custom-call | flops 271790912 | bytes 209715 | tf_op jit(solution)/shard_map/kernel_grad/pallas_call | solution.py:310
  34.4 0.0 collective-permute-done.6.refs_2_
  34.4 0.0 collective-permute-done.7.refs_3_
  34.4 7.9 %conv_all.1.refs_2_ = f32[32,4,32,128]{3,2,1,0:T(8,128)} custom-call(bf16[96,896]{1,0:T(8,128)(2,1)S(1)} %get-tuple-element.76.refs_0_, f32[32,4,32,128]{3,2,1,0:T(8,128)S(1)} %copy-done, f32[32,1,32,128]{3,2,1,0:T(8,128)S(1)} %collective-permute-done.6.refs_2_, f32[32,1,32,128]{3,2,1,0:T(8,128)S(1)} %collective-permute-done.7.refs_3_, ...), custom_call_target="tpu_custom_call" | custom-call | flops 271790912 | bytes 209715 | tf_op jit(solution)/shard_map/conv_all/pallas_call | solution.py:215
  42.3 8.1 %collective-permute-done.5.refs_2_.refs_1_ = f32[32,4,32,128]{3,2,1,0:T(8,128)} collective-permute-done((f32[32,4,32,128]{3,2,1,0:T(8,128)}, f32[32,4,32,128]{3,2,1,0:T(8,128)}, u32[]{:S(2)}, u32[]{:S(2)}) %collective-permute-start.5) | collective-permute-done | bytes 2097184 | tf_op jit(solution)/shard_map/ppermute | solution.py:498
  50.4 1.3 %constant_dynamic-slice_fusion = (f32[32,1,32,128]{3,2,1,0:T(8,128)S(1)}, f32[32,1,32,128]{3,2,1,0:T(8,128)S(1)}) fusion(f32[32,4,32,128]{3,2,1,0:T(8,128)} %collective-permute-done.5.refs_2_.refs_1_, s32[]{:T(128)S(6)} %select_n.5, s32[]{:T(128)S(6)} %select_n.4), kind=kLoop, calls=%fused_computation | loop fusion | bytes 2097160 | tf_op jit(solution)/shard_map/dynamic_slice | solution.py:463
  51.7 0.1 collective-permute-start.10
  51.8 0.9 collective-permute-start.11
  52.6 2.1 %collective-permute-start.3 = (f32[24,2,32,128]{3,2,1,0:T(8,128)S(1)}, f32[24,2,32,128]{3,2,1,0:T(8,128)S(1)}, u32[]{:S(2)}, u32[]{:S(2)}) collective-permute-start(f32[24,2,32,128]{3,2,1,0:T(8,128)S(1)} %get-tuple-element.72), channel_id=1, source_target_pairs={{0,1},{1,0},{2,3},{3,2},{4,5},{5,4},{6,7},{7,6},{8,9},{9,8},{10,11... | collective-permute-start | bytes 2359304 | tf_op jit(solution)/shard_map/ppermute | solution.py:526
  54.8 7.2 %kernel_grad.3 = (f32[2,144,128]{2,1,0:T(8,128)S(1)}, f32[2,144,128]{2,1,0:T(8,128)S(1)}) custom-call(bf16[6,1088,128]{2,1,0:T(8,128)(2,1)S(1)} %get-tuple-element.74.refs_0_, bf16[6,1088,128]{2,1,0:T(8,128)(2,1)S(1)} %get-tuple-element.75.refs_1_, f32[32,4,32,128]{3,2,1,0:T(8,128)} %collective-permute-done.5.refs_2_.refs_1_, s32[1]{0:T(128)} %bitcast.2.refs_3_.refs_4_.bit, ...), custom_call_target="tpu_custom_call" | custom-call | flops 271790912 | bytes 209715 | tf_op jit(solution)/shard_map/kernel_grad/pallas_call | solution.py:310
  62.0 2.6 %collective-permute-start.8 = (f32[2,144,128]{2,1,0:T(8,128)S(1)}, f32[2,144,128]{2,1,0:T(8,128)S(1)}, u32[]{:S(2)}, u32[]{:S(2)}) collective-permute-start(f32[2,144,128]{2,1,0:T(8,128)S(1)} %get-tuple-element.84), channel_id=1, source_target_pairs={{0,2},{2,0},{4,6},{6,4},{8,10},{10,8},{12,14},{14,12},{16,18},{18,... | collective-permute-start | bytes 442376 | tf_op jit(solution)/shard_map/ppermute | solution.py:475
  64.6 1.0 %collective-permute-done.8 = f32[2,144,128]{2,1,0:T(8,128)S(1)} collective-permute-done((f32[2,144,128]{2,1,0:T(8,128)S(1)}, f32[2,144,128]{2,1,0:T(8,128)S(1)}, u32[]{:S(2)}, u32[]{:S(2)}) %collective-permute-start.8) | collective-permute-done | bytes 147488 | tf_op jit(solution)/shard_map/ppermute | solution.py:475
  65.7 1.6 %collective-permute-start.9 = (f32[2,144,128]{2,1,0:T(8,128)S(1)}, f32[2,144,128]{2,1,0:T(8,128)S(1)}, u32[]{:S(2)}, u32[]{:S(2)}) collective-permute-start(f32[2,144,128]{2,1,0:T(8,128)S(1)} %add.24), channel_id=1, source_target_pairs={{0,4},{2,6},{4,0},{6,2},{8,12},{10,14},{12,8},{14,10},{16,20},{18,... | collective-permute-start | bytes 442376 | tf_op jit(solution)/shard_map/ppermute | solution.py:475
  67.3 6.6 %conv_inner.3 = (f32[32,4,32,128]{3,2,1,0:T(8,128)}, bf16[6,1088,128]{2,1,0:T(8,128)(2,1)S(1)}, bf16[6,1088,128]{2,1,0:T(8,128)(2,1)S(1)}) custom-call(bf16[96,896]{1,0:T(8,128)(2,1)S(1)} %get-tuple-element.86.refs_0_, f32[32,4,32,128]{3,2,1,0:T(8,128)} %collective-permute-done.5.refs_2_.refs_1_, ...), custom_call_target="tpu_custom_call", output_to_operand_aliasing={{0}: (2, {})} | custom-call | flops 271790912 | bytes 209715 | tf_op jit(solution)/shard_map/conv_inner/pallas_call | solution.py:215
  73.9 0.0 collective-permute-done.9
  73.9 0.0 collective-permute-done.10.refs_1_
  73.9 0.0 collective-permute-done.11.refs_2_
  73.9 1.6 %collective-permute-start.12 = (f32[2,144,128]{2,1,0:T(8,128)S(1)}, f32[2,144,128]{2,1,0:T(8,128)S(1)}, u32[]{:S(2)}, u32[]{:S(2)}) collective-permute-start(f32[2,144,128]{2,1,0:T(8,128)S(1)} %add.25), channel_id=1, source_target_pairs={{0,8},{2,10},{4,12},{6,14},{8,0},{10,2},{12,4},{14,6},{16,24},{18,... | collective-permute-start | bytes 442376 | tf_op jit(solution)/shard_map/ppermute | solution.py:475
  75.5 5.3 %conv_outer.3 = f32[32,4,32,128]{3,2,1,0:T(8,128)} custom-call(bf16[96,896]{1,0:T(8,128)(2,1)S(1)} %get-tuple-element.86.refs_0_, f32[32,1,32,128]{3,2,1,0:T(8,128)S(1)} %collective-permute-done.10.refs_1_, f32[32,1,32,128]{3,2,1,0:T(8,128)S(1)} %collective-permute-done.11.refs_2_, s32[1]{0:T(128)} %bitcast.2.refs_3_.refs_4_.bit, ...), custom_call_target="tpu_custom_call", output_to_operand_aliasing={{}: (4, {})} | custom-call | flops 271790912 | bytes 209715 | tf_op jit(solution)/shard_map/conv_outer/pallas_call | solution.py:215
  80.9 0.0 collective-permute-done.12
  80.9 0.0 collective-permute-done.4.refs_1_
  80.9 2.2 %collective-permute-start.13 = (f32[2,144,128]{2,1,0:T(8,128)S(1)}, f32[2,144,128]{2,1,0:T(8,128)S(1)}, u32[]{:S(2)}, u32[]{:S(2)}) collective-permute-start(f32[2,144,128]{2,1,0:T(8,128)S(1)} %add.26), channel_id=1, source_target_pairs={{0,16},{2,18},{4,20},{6,22},{8,24},{10,26},{12,28},{14,30},{16,0},... | collective-permute-start | bytes 442376 | tf_op jit(solution)/shard_map/ppermute | solution.py:475
  83.1 0.5 collective-permute-start.2
  83.7 1.7 %add_pieces.3.refs_2_ = f32[32,4,32,128]{3,2,1,0:T(8,128)} custom-call(f32[32,2,32,128]{3,2,1,0:T(8,128)S(1)} %get-tuple-element.100.refs_0_, f32[32,2,32,128]{3,2,1,0:T(8,128)S(1)} %collective-permute-done.4.refs_1_), custom_call_target="tpu_custom_call" | custom-call | flops 262144 | bytes 3145728 | tf_op jit(solution)/shard_map/add_pieces/pallas_call | solution.py:445
  85.4 5.1 %collective-permute-done.13 = f32[2,144,128]{2,1,0:T(8,128)S(1)} collective-permute-done((f32[2,144,128]{2,1,0:T(8,128)S(1)}, f32[2,144,128]{2,1,0:T(8,128)S(1)}, u32[]{:S(2)}, u32[]{:S(2)}) %collective-permute-start.13) | collective-permute-done | bytes 147488 | tf_op jit(solution)/shard_map/ppermute | solution.py:475
  90.5 0.1 collective-permute-start.14
  90.5 1.4 %collective-permute-done.14.other_ref = f32[2,144,128]{2,1,0:T(8,128)S(1)} collective-permute-done((f32[2,144,128]{2,1,0:T(8,128)S(1)}, f32[2,144,128]{2,1,0:T(8,128)S(1)}, u32[]{:S(2)}, u32[]{:S(2)}) %collective-permute-start.14) | collective-permute-done | bytes 147488 | tf_op jit(solution)/shard_map/ppermute | solution.py:475
  91.9 1.0 %finish.1 = f32[27,32,64]{2,1,0:T(8,128)} custom-call(s32[1]{0:T(128)} %bitcast.me, s32[1]{0:T(128)} %bitcast.2.refs_3_.refs_4_.bit, f32[2,144,128]{2,1,0:T(8,128)S(1)} %add.27.mine_ref, f32[2,144,128]{2,1,0:T(8,128)S(1)} %collective-permute-done.14.other_ref), custom_call_target="tpu_custom_call" | custom-call | tf_op jit(solution)/shard_map/finish/pallas_call | solution.py:416
  92.9 0.0 collective-permute-done.3.refs_1_
  92.9 1.1 %add_pieces.4.refs_2_ = f32[32,4,32,128]{3,2,1,0:T(8,128)} custom-call(f32[32,2,32,128]{3,2,1,0:T(8,128)S(1)} %get-tuple-element.70.refs_0_, f32[24,2,32,128]{3,2,1,0:T(8,128)S(1)} %collective-permute-done.3.refs_1_, f32[32,4,32,128]{3,2,1,0:T(8,128)} %add_pieces.3.refs_2_), custom_call_target="tpu_custom_call", output_to_operand_aliasing={{}: (2, {})} | custom-call | flops 196608 | bytes 2359296 | tf_op jit(solution)/shard_map/add_pieces/pallas_call | solution.py:445
  94.0 0.4 collective-permute-done.2.refs_1_
  94.4 0.8 add_pieces.5
  (4 shorter events, 0.1 us)
Async XLA Ops:
  0.6 49.8 %collective-permute-start.5 = (f32[32,4,32,128]{3,2,1,0:T(8,128)}, f32[32,4,32,128]{3,2,1,0:T(8,128)}, u32[]{:S(2)}, u32[]{:S(2)}) collective-permute-start(f32[32,4,32,128]{3,2,1,0:T(8,128)} %refs_2_), channel_id=1, source_target_pairs={{1,0},{0,1},{3,2},{2,3},{5,4},{4,5},{7,6},{6,7},{9,8},{8,9},{11,10... | collective-permute-start | bytes 6291464 | tf_op jit(solution)/shard_map/ppermute | solution.py:498
  3.6 12.6 %copy-start = (f32[32,4,32,128]{3,2,1,0:T(8,128)S(1)}, f32[32,4,32,128]{3,2,1,0:T(8,128)}, u32[]{:S(2)}) copy-start(f32[32,4,32,128]{3,2,1,0:T(8,128)} %refs_2_) | copy-start | bytes 6291460
  6.0 10.2 %collective-permute-start = (f32[32,1,32,128]{3,2,1,0:T(8,128)}, f32[32,1,32,128]{3,2,1,0:T(8,128)S(1)}, u32[]{:S(2)}, u32[]{:S(2)}) collective-permute-start(f32[32,1,32,128]{3,2,1,0:T(8,128)} %get-tuple-element.60), channel_id=1, source_target_pairs={{0,2},{2,0},{4,6},{6,4},{8,10},{10,8},{12,14},{14,12},{16,18},{18,... | collective-permute-start | bytes 1572872 | tf_op jit(solution)/shard_map/ppermute | solution.py:475
  6.0 10.2 %collective-permute-start.1 = (f32[32,1,32,128]{3,2,1,0:T(8,128)}, f32[32,1,32,128]{3,2,1,0:T(8,128)S(1)}, u32[]{:S(2)}, u32[]{:S(2)}) collective-permute-start(f32[32,1,32,128]{3,2,1,0:T(8,128)} %get-tuple-element.61), channel_id=1, source_target_pairs={{2,4},{6,8},{10,12},{14,16},{18,20},{22,24},{26,28},{4,2},{8,6},{1... | collective-permute-start | bytes 1572872 | tf_op jit(solution)/shard_map/ppermute | solution.py:471
  6.7 1.0 %copy-start.2 = (f32[64,27,32]{0,2,1:T(8,128)S(1)}, f32[64,27,32]{0,2,1:T(8,128)}, u32[]{:S(2)}) copy-start(f32[64,27,32]{0,2,1:T(8,128)} %param.4) | copy-start | bytes 663556
  9.1 1.6 %copy-start.1 = (f32[32,4,32,128]{3,2,1,0:T(8,128)S(1)}, f32[32,4,32,128]{3,2,1,0:T(8,128)}, u32[]{:S(2)}) copy-start(f32[32,4,32,128]{3,2,1,0:T(8,128)} %refs_1_) | copy-start | bytes 6291460
  16.3 18.1 %collective-permute-start.6 = (f32[32,1,32,128]{3,2,1,0:T(8,128)S(1)}, f32[32,1,32,128]{3,2,1,0:T(8,128)S(1)}, u32[]{:S(2)}, u32[]{:S(2)}) collective-permute-start(f32[32,1,32,128]{3,2,1,0:T(8,128)S(1)} %get-tuple-element.78), channel_id=1, source_target_pairs={{0,2},{2,0},{4,6},{6,4},{8,10},{10,8},{12,14},{14,12},{16,18},{18,... | collective-permute-start | bytes 1572872 | tf_op jit(solution)/shard_map/ppermute | solution.py:475
  21.8 12.7 %collective-permute-start.7 = (f32[32,1,32,128]{3,2,1,0:T(8,128)S(1)}, f32[32,1,32,128]{3,2,1,0:T(8,128)S(1)}, u32[]{:S(2)}, u32[]{:S(2)}) collective-permute-start(f32[32,1,32,128]{3,2,1,0:T(8,128)S(1)} %get-tuple-element.79), channel_id=1, source_target_pairs={{2,4},{6,8},{10,12},{14,16},{18,20},{22,24},{26,28},{4,2},{8,6},{1... | collective-permute-start | bytes 1572872 | tf_op jit(solution)/shard_map/ppermute | solution.py:471
  22.4 58.4 %collective-permute-start.4 = (f32[32,2,32,128]{3,2,1,0:T(8,128)S(1)}, f32[32,2,32,128]{3,2,1,0:T(8,128)S(1)}, u32[]{:S(2)}, u32[]{:S(2)}) collective-permute-start(f32[32,2,32,128]{3,2,1,0:T(8,128)S(1)} %get-tuple-element.73), channel_id=1, source_target_pairs={{0,1},{1,0},{2,3},{3,2},{4,5},{5,4},{6,7},{7,6},{8,9},{9,8},{10,11... | collective-permute-start | bytes 3145736 | tf_op jit(solution)/shard_map/ppermute | solution.py:526
  51.7 22.2 %collective-permute-start.10 = (f32[32,1,32,128]{3,2,1,0:T(8,128)S(1)}, f32[32,1,32,128]{3,2,1,0:T(8,128)S(1)}, u32[]{:S(2)}, u32[]{:S(2)}) collective-permute-start(f32[32,1,32,128]{3,2,1,0:T(8,128)S(1)} %get-tuple-element.90), channel_id=1, source_target_pairs={{0,2},{2,0},{4,6},{6,4},{8,10},{10,8},{12,14},{14,12},{16,18},{18,... | collective-permute-start | bytes 1572872 | tf_op jit(solution)/shard_map/ppermute | solution.py:475
  51.8 22.1 %collective-permute-start.11 = (f32[32,1,32,128]{3,2,1,0:T(8,128)S(1)}, f32[32,1,32,128]{3,2,1,0:T(8,128)S(1)}, u32[]{:S(2)}, u32[]{:S(2)}) collective-permute-start(f32[32,1,32,128]{3,2,1,0:T(8,128)S(1)} %get-tuple-element.91), channel_id=1, source_target_pairs={{2,4},{6,8},{10,12},{14,16},{18,20},{22,24},{26,28},{4,2},{8,6},{1... | collective-permute-start | bytes 1572872 | tf_op jit(solution)/shard_map/ppermute | solution.py:471
  52.6 40.3 %collective-permute-start.3 = (f32[24,2,32,128]{3,2,1,0:T(8,128)S(1)}, f32[24,2,32,128]{3,2,1,0:T(8,128)S(1)}, u32[]{:S(2)}, u32[]{:S(2)}) collective-permute-start(f32[24,2,32,128]{3,2,1,0:T(8,128)S(1)} %get-tuple-element.72), channel_id=1, source_target_pairs={{0,1},{1,0},{2,3},{3,2},{4,5},{5,4},{6,7},{7,6},{8,9},{9,8},{10,11... | collective-permute-start | bytes 2359304 | tf_op jit(solution)/shard_map/ppermute | solution.py:526
  62.0 3.6 %collective-permute-start.8 = (f32[2,144,128]{2,1,0:T(8,128)S(1)}, f32[2,144,128]{2,1,0:T(8,128)S(1)}, u32[]{:S(2)}, u32[]{:S(2)}) collective-permute-start(f32[2,144,128]{2,1,0:T(8,128)S(1)} %get-tuple-element.84), channel_id=1, source_target_pairs={{0,2},{2,0},{4,6},{6,4},{8,10},{10,8},{12,14},{14,12},{16,18},{18,... | collective-permute-start | bytes 442376 | tf_op jit(solution)/shard_map/ppermute | solution.py:475
  65.7 8.2 %collective-permute-start.9 = (f32[2,144,128]{2,1,0:T(8,128)S(1)}, f32[2,144,128]{2,1,0:T(8,128)S(1)}, u32[]{:S(2)}, u32[]{:S(2)}) collective-permute-start(f32[2,144,128]{2,1,0:T(8,128)S(1)} %add.24), channel_id=1, source_target_pairs={{0,4},{2,6},{4,0},{6,2},{8,12},{10,14},{12,8},{14,10},{16,20},{18,... | collective-permute-start | bytes 442376 | tf_op jit(solution)/shard_map/ppermute | solution.py:475
  73.9 7.0 %collective-permute-start.12 = (f32[2,144,128]{2,1,0:T(8,128)S(1)}, f32[2,144,128]{2,1,0:T(8,128)S(1)}, u32[]{:S(2)}, u32[]{:S(2)}) collective-permute-start(f32[2,144,128]{2,1,0:T(8,128)S(1)} %add.25), channel_id=1, source_target_pairs={{0,8},{2,10},{4,12},{6,14},{8,0},{10,2},{12,4},{14,6},{16,24},{18,... | collective-permute-start | bytes 442376 | tf_op jit(solution)/shard_map/ppermute | solution.py:475
  80.9 9.6 %collective-permute-start.13 = (f32[2,144,128]{2,1,0:T(8,128)S(1)}, f32[2,144,128]{2,1,0:T(8,128)S(1)}, u32[]{:S(2)}, u32[]{:S(2)}) collective-permute-start(f32[2,144,128]{2,1,0:T(8,128)S(1)} %add.26), channel_id=1, source_target_pairs={{0,16},{2,18},{4,20},{6,22},{8,24},{10,26},{12,28},{14,30},{16,0},... | collective-permute-start | bytes 442376 | tf_op jit(solution)/shard_map/ppermute | solution.py:475
  83.1 11.3 %collective-permute-start.2 = (f32[8,2,32,128]{3,2,1,0:T(8,128)S(1)}, f32[8,2,32,128]{3,2,1,0:T(8,128)S(1)}, u32[]{:S(2)}, u32[]{:S(2)}) collective-permute-start(f32[8,2,32,128]{3,2,1,0:T(8,128)S(1)} %get-tuple-element.71), channel_id=1, source_target_pairs={{0,1},{1,0},{2,3},{3,2},{4,5},{5,4},{6,7},{7,6},{8,9},{9,8},{10,11... | collective-permute-start | bytes 786440 | tf_op jit(solution)/shard_map/ppermute | solution.py:526
  90.5 1.4 %collective-permute-start.14 = (f32[2,144,128]{2,1,0:T(8,128)S(1)}, f32[2,144,128]{2,1,0:T(8,128)S(1)}, u32[]{:S(2)}, u32[]{:S(2)}) collective-permute-start(f32[2,144,128]{2,1,0:T(8,128)S(1)} %add.27.mine_ref), channel_id=1, source_target_pairs={{0,2},{2,0},{4,6},{6,4},{8,10},{10,8},{12,14},{14,12},{16,18},{18,... | collective-permute-start | bytes 442376 | tf_op jit(solution)/shard_map/ppermute | solution.py:475
